TPU v7x, 32 devices: a whole 2x2x4 slice. The times are simulated.
32 devices in a mesh: dp: 16 (over z, x, core), mp: 2 (over y).
Axes of the slice: x: 2, y: 2, z: 4, core: 2. Of those that a mesh axis runs over, the one named last changes fastest.
Arguments:
- inputs: bfloat16 [16384, 2048], P('dp'), may hold values from -6 to 6
- prefix_len: int32 [16], P('dp'), may hold values from 102 to 512, as said below
- norm1_gain: float32 [2048], replicated, may hold values from 0.1 to 1.9
- norm1_bias: float32 [2048], replicated, may hold values from -4 to 4
- query_weight: bfloat16 [2048, 2048], P(None, 'mp'), may hold values from -0.25 to 0.25
- query_bias: float32 [16, 128], P('mp'), may hold values from -6 to 6
- key_weight: bfloat16 [2048, 2048], P(None, 'mp'), may hold values from -0.125 to 0.125
- value_weight: bfloat16 [2048, 2048], P(None, 'mp'), may hold values from -0.125 to 0.125
- value_bias: float32 [16, 128], P('mp'), may hold values from -6 to 6
- out_weight: bfloat16 [2048, 2048], P('mp'), may hold values from -0.5 to 0.5
- out_bias: float32 [2048], replicated, may hold values from -4 to 4
- norm2_gain: float32 [2048], replicated, may hold values from 0.1 to 1.9
- norm2_bias: float32 [2048], replicated, may hold values from -4 to 4
- up_weight: bfloat16 [2048, 8192], P(None, 'mp'), may hold values from -0.125 to 0.125
- up_bias: float32 [64, 128], P('mp'), may hold values from -6 to 6
- down_weight: bfloat16 [8192, 2048], P('mp'), may hold values from -0.0625 to 0.0625
- down_bias: float32 [2048], replicated, may hold values from -4 to 4
- out_grad: bfloat16 [16384, 2048], P('dp'), may hold values from -6 to 6
Outputs:
- outputs: bfloat16 [16384, 2048], P('dp')
- in_grad: bfloat16 [16384, 2048], P('dp')
- norm1_gain_grad: float32 [2048], P('dp')
- norm1_bias_grad: float32 [2048], P('dp')
- query_weight_grad: float32 [2048, 2048], P('dp', 'mp')
- query_bias_grad: float32 [16, 128], P('mp', 'dp')
- key_weight_grad: float32 [2048, 2048], P('dp', 'mp')
- value_weight_grad: float32 [2048, 2048], P('dp', 'mp')
- value_bias_grad: float32 [16, 128], P('mp', 'dp')
- out_weight_grad: float32 [2048, 2048], P('mp', 'dp')
- out_bias_grad: float32 [2048], P('dp')
- norm2_gain_grad: float32 [2048], P('dp')
- norm2_bias_grad: float32 [2048], P('dp')
- up_weight_grad: float32 [2048, 8192], P('dp', 'mp')
- up_bias_grad: float32 [64, 128], P('mp', 'dp')
- down_weight_grad: float32 [8192, 2048], P('mp', 'dp')
- down_bias_grad: float32 [2048], P('dp')
Inputs may be any that keep to these rules, and one draw needn't show every extreme that they name: `prefix_len`: each sequence's prefix length; some sequence has exactly 512 and some exactly 102 in every draw.
All inputs are finite; a program needn't handle non-finite values.
Results may differ from a plain program's by a relative error of at most 0.014.
The roundings to bfloat16 on the way count: a program that leaves them out, or rounds other values in their place, can miss the bound.
Values sent between devices are 32-bit elements; how exact they have to be, the bound alone decides.
No kernel may reach another device: no remote copies, remote signals or barrier semaphores. Data moves between devices by JAX's collectives and lax.ppermute only.
A program may use at most 384 MiB of HBM per device.

v0:
```python
import math

import jax
import jax.numpy as jnp
from jax import lax
from jax.sharding import PartitionSpec as P


def layer_norm(field, norm_gain, norm_bias):
    average = jnp.mean(field, -1, keepdims=True)
    centred = field - average
    variance = jnp.mean(centred * centred, -1, keepdims=True)
    return centred * lax.rsqrt(variance + 1e-05) * norm_gain + norm_bias


def exact_gelu(field):
    return jax.nn.gelu(field, approximate=False)


def body(
    inputs,
    prefix_len,
    norm1_gain,
    norm1_bias,
    query_weight,
    query_bias,
    key_weight,
    value_weight,
    value_bias,
    out_weight,
    out_bias,
    norm2_gain,
    norm2_bias,
    up_weight,
    up_bias,
    down_weight,
    down_bias,
    out_grad,
):
    length = inputs.shape[0]
    heads_local, head_dim = query_bias.shape
    block_rows = min(512, length)
    block_count = length // block_rows
    score_scale = 1.0 / math.sqrt(head_dim)
    positions = jnp.arange(length, dtype=jnp.int32)
    boundary = prefix_len[0]
    features = inputs.astype(jnp.float32)
    normed_float, norm1_pull = jax.vjp(layer_norm, features, norm1_gain, norm1_bias)
    normed = normed_float.astype(jnp.bfloat16)
    queries = (
        (jnp.dot(normed, query_weight, preferred_element_type=jnp.float32) + query_bias.reshape(-1))
        .astype(jnp.bfloat16)
        .reshape(length, heads_local, head_dim)
    )
    keys = (
        jnp.dot(normed, key_weight, preferred_element_type=jnp.float32)
        .astype(jnp.bfloat16)
        .reshape(length, heads_local, head_dim)
    )
    values = (
        (jnp.dot(normed, value_weight, preferred_element_type=jnp.float32) + value_bias.reshape(-1))
        .astype(jnp.bfloat16)
        .reshape(length, heads_local, head_dim)
    )

    def block_scores(row_begin):
        query_block = queries[row_begin : row_begin + block_rows]
        scores = (
            jnp.einsum("qhd,khd->hqk", query_block, keys, preferred_element_type=jnp.float32)
            * score_scale
        )
        rows = row_begin + jnp.arange(block_rows, dtype=jnp.int32)
        visible = (positions[None, :] <= rows[:, None]) | (positions[None, :] < boundary)
        return (query_block, jnp.where(visible[None], scores, -1e30))

    mixed_blocks = []
    totals_log = []
    for block_index in range(block_count):
        row_begin = block_index * block_rows
        query_block, scores = block_scores(row_begin)
        peak = jnp.max(scores, -1, keepdims=True)
        exps = jnp.exp(scores - peak)
        sums = jnp.sum(exps, -1, keepdims=True)
        probs = exps / sums
        totals_log.append(peak + jnp.log(sums))
        mixed_blocks.append(
            jnp.einsum(
                "hqk,khd->qhd",
                probs.astype(jnp.bfloat16),
                values,
                preferred_element_type=jnp.float32,
            )
        )
    mixed = (
        jnp.concatenate(mixed_blocks, 0)
        .astype(jnp.bfloat16)
        .reshape(length, heads_local * head_dim)
    )
    attn = lax.psum(jnp.dot(mixed, out_weight, preferred_element_type=jnp.float32), "mp") + out_bias
    resid = features + attn
    normed2_float, norm2_pull = jax.vjp(layer_norm, resid, norm2_gain, norm2_bias)
    normed2 = normed2_float.astype(jnp.bfloat16)
    hidden = jnp.dot(normed2, up_weight, preferred_element_type=jnp.float32) + up_bias.reshape(-1)
    acts_float, gelu_pull = jax.vjp(exact_gelu, hidden)
    acts = acts_float.astype(jnp.bfloat16)
    branch = (
        lax.psum(jnp.dot(acts, down_weight, preferred_element_type=jnp.float32), "mp") + down_bias
    )
    outputs = (resid + branch).astype(jnp.bfloat16)
    grad_float = out_grad.astype(jnp.float32)
    down_bias_grad = jnp.sum(grad_float, 0)
    down_weight_grad = jnp.einsum("tf,td->fd", acts, out_grad, preferred_element_type=jnp.float32)
    acts_grad = jnp.einsum("td,fd->tf", out_grad, down_weight, preferred_element_type=jnp.float32)
    (hidden_float,) = gelu_pull(acts_grad)
    hidden_grad = hidden_float.astype(jnp.bfloat16)
    up_bias_grad = jnp.sum(hidden_grad.astype(jnp.float32), 0).reshape(up_bias.shape)
    up_weight_grad = jnp.einsum(
        "td,tf->df", normed2, hidden_grad, preferred_element_type=jnp.float32
    )
    norm2_in = lax.psum(
        jnp.einsum("tf,df->td", hidden_grad, up_weight, preferred_element_type=jnp.float32), "mp"
    )
    resid_part, norm2_gain_grad, norm2_bias_grad = norm2_pull(norm2_in)
    resid_grad = grad_float + resid_part
    attn_grad = resid_grad.astype(jnp.bfloat16)
    out_bias_grad = jnp.sum(attn_grad.astype(jnp.float32), 0)
    out_weight_grad = jnp.einsum("te,td->ed", mixed, attn_grad, preferred_element_type=jnp.float32)
    mixed_grad = (
        jnp.einsum("td,ed->te", attn_grad, out_weight, preferred_element_type=jnp.float32)
        .astype(jnp.bfloat16)
        .reshape(length, heads_local, head_dim)
    )
    query_blocks = []
    key_accum = jnp.zeros((length, heads_local, head_dim), jnp.float32)
    value_accum = jnp.zeros((length, heads_local, head_dim), jnp.float32)
    for block_index in range(block_count):
        row_begin = block_index * block_rows
        query_block, scores = block_scores(row_begin)
        probs = jnp.exp(scores - totals_log[block_index])
        mixed_block = mixed_grad[row_begin : row_begin + block_rows]
        prob_grad = jnp.einsum(
            "qhd,khd->hqk", mixed_block, values, preferred_element_type=jnp.float32
        )
        row_dot = jnp.sum(probs * prob_grad, -1, keepdims=True)
        score_grad = (probs * (prob_grad - row_dot) * score_scale).astype(jnp.bfloat16)
        query_blocks.append(
            jnp.einsum("hqk,khd->qhd", score_grad, keys, preferred_element_type=jnp.float32)
        )
        key_accum = key_accum + jnp.einsum(
            "hqk,qhd->khd", score_grad, query_block, preferred_element_type=jnp.float32
        )
        value_accum = value_accum + jnp.einsum(
            "hqk,qhd->khd",
            probs.astype(jnp.bfloat16),
            mixed_block,
            preferred_element_type=jnp.float32,
        )
    query_grad = (
        jnp.concatenate(query_blocks, 0)
        .astype(jnp.bfloat16)
        .reshape(length, heads_local * head_dim)
    )
    key_grad = key_accum.astype(jnp.bfloat16).reshape(length, heads_local * head_dim)
    value_grad = value_accum.astype(jnp.bfloat16).reshape(length, heads_local * head_dim)
    query_bias_grad = jnp.sum(query_grad.astype(jnp.float32), 0).reshape(heads_local, head_dim)
    value_bias_grad = jnp.sum(value_grad.astype(jnp.float32), 0).reshape(heads_local, head_dim)
    query_weight_grad = jnp.einsum(
        "td,te->de", normed, query_grad, preferred_element_type=jnp.float32
    )
    key_weight_grad = jnp.einsum("td,te->de", normed, key_grad, preferred_element_type=jnp.float32)
    value_weight_grad = jnp.einsum(
        "td,te->de", normed, value_grad, preferred_element_type=jnp.float32
    )
    norm1_part = jnp.einsum(
        "te,de->td", query_grad, query_weight, preferred_element_type=jnp.float32
    )
    norm1_part = norm1_part + jnp.einsum(
        "te,de->td", key_grad, key_weight, preferred_element_type=jnp.float32
    )
    norm1_part = norm1_part + jnp.einsum(
        "te,de->td", value_grad, value_weight, preferred_element_type=jnp.float32
    )
    norm1_in = lax.psum(norm1_part, "mp")
    input_part, norm1_gain_grad, norm1_bias_grad = norm1_pull(norm1_in)
    in_grad = (resid_grad + input_part).astype(jnp.bfloat16)
    summed = (
        lax.psum_scatter(norm1_gain_grad, "dp", scatter_dimension=0, tiled=True),
        lax.psum_scatter(norm1_bias_grad, "dp", scatter_dimension=0, tiled=True),
        lax.psum_scatter(query_weight_grad, "dp", scatter_dimension=0, tiled=True),
        lax.psum_scatter(query_bias_grad, "dp", scatter_dimension=1, tiled=True),
        lax.psum_scatter(key_weight_grad, "dp", scatter_dimension=0, tiled=True),
        lax.psum_scatter(value_weight_grad, "dp", scatter_dimension=0, tiled=True),
        lax.psum_scatter(value_bias_grad, "dp", scatter_dimension=1, tiled=True),
        lax.psum_scatter(out_weight_grad, "dp", scatter_dimension=1, tiled=True),
        lax.psum_scatter(out_bias_grad, "dp", scatter_dimension=0, tiled=True),
        lax.psum_scatter(norm2_gain_grad, "dp", scatter_dimension=0, tiled=True),
        lax.psum_scatter(norm2_bias_grad, "dp", scatter_dimension=0, tiled=True),
        lax.psum_scatter(up_weight_grad, "dp", scatter_dimension=0, tiled=True),
        lax.psum_scatter(up_bias_grad, "dp", scatter_dimension=1, tiled=True),
        lax.psum_scatter(down_weight_grad, "dp", scatter_dimension=1, tiled=True),
        lax.psum_scatter(down_bias_grad, "dp", scatter_dimension=0, tiled=True),
    )
    return (
        outputs,
        in_grad,
        summed[0],
        summed[1],
        summed[2],
        summed[3],
        summed[4],
        summed[5],
        summed[6],
        summed[7],
        summed[8],
        summed[9],
        summed[10],
        summed[11],
        summed[12],
        summed[13],
        summed[14],
    )


def solution(mesh):
    in_specs = (
        P("dp", None),
        P("dp"),
        P(),
        P(),
        P(None, "mp"),
        P("mp", None),
        P(None, "mp"),
        P(None, "mp"),
        P("mp", None),
        P("mp", None),
        P(),
        P(),
        P(),
        P(None, "mp"),
        P("mp", None),
        P("mp", None),
        P(),
        P("dp", None),
    )
    out_specs = (
        P("dp", None),
        P("dp", None),
        P("dp"),
        P("dp"),
        P("dp", "mp"),
        P("mp", "dp"),
        P("dp", "mp"),
        P("dp", "mp"),
        P("mp", "dp"),
        P("mp", "dp"),
        P("dp"),
        P("dp"),
        P("dp"),
        P("dp", "mp"),
        P("mp", "dp"),
        P("mp", "dp"),
        P("dp"),
    )
    return jax.shard_map(body, mesh=mesh, in_specs=in_specs, out_specs=out_specs, check_vma=False)
```

profile of v0, /device:TPU:0, one launch (start us, length us, event | category | flops | bytes accessed | tf_op | source)
XLA Modules:
  0.0 2404.6 jit_solution(17381376005318204398)
XLA Ops:
  8.1 3.2 convert_reduce_fusion.1
  11.4 3.4 fusion.27
  16.0 1.9 fusion.25
  17.9 4.9 convolution_convert_fusion.1
  22.8 4.9 add_convert_fusion.6
  30.1 4.9 add_convert_fusion.7
  35.0 5.6 fusion.98
  40.6 3.8 fusion.15
  44.4 1.9 copy-done.4
  46.7 5.5 fusion.62
  52.2 3.6 fusion.99
  55.9 3.8 fusion.14
  59.6 1.9 copy-done.3
  62.0 4.6 fusion.63
  66.6 9.4 fusion.71
  76.1 200.9 %all-reduce.16.cloned.1.call-done = f32[1024,2048]{1,0:T(8,128)} async-done(((f32[1024,2048]{1,0:T(8,128)}), f32[1024,2048]{1,0:T(8,128)}) %all-reduce.16.cloned.1.call-update) | async-done | bytes 8388624 | tf_op jit(solution)/shard_map/psum | solution.py:99
  277.0 5.7 fusion.95
  283.8 25.0 %fusion.90 = f32[1024,4096]{1,0:T(8,128)} fusion(bf16[2048,4096]{1,0:T(8,128)(2,1)} %param.31, f32[1024,2048]{1,0:T(8,128)S(1)} %get-tuple-element.77, f32[2048]{0:T(1024)S(1)} %copy-done.64, f32[2048]{0:T(1024)S(1)} %copy-done.50, f32[1024]{0:T(1024)S(1)} %fusion.75, f32[1024]{0:T(1024)S(1)} %broadcast_multiply_fusion), kind=kOutput, calls=%fused_computation.134 | convolution fusion | flops 17190354944 | bytes 41967616 | tf_op jit(solution)/shard_map/dot_general | solution.py:103
  308.9 60.8 %convert_reduce_fusion = (f32[4096]{0:T(1024)}, bf16[1024,4096]{1,0:T(8,128)(2,1)}, f32[1024,4096]{1,0:T(8,128)}) fusion(f32[1024,4096]{1,0:T(8,128)} %fusion.90, f32[4096]{0:T(1024)S(1)} %bitcast.113, bf16[1024,2048]{1,0:T(8,128)(2,1)S(1)} %copy-done.10, bf16[4096,2048]{1,0:T(8,128)(2,1)} %param.33), kind=kOutput, calls=%fused_computation.4 | convolution fusion | flops 17494437888 | bytes 62947328 | tf_op jit(solution)/shard_map/td,fd->tf/dot_general | solution.py:113
  369.7 21.9 fusion.101
  392.4 13.0 multiply_convert_fusion.2
  405.5 3.2 copy-done.13
  408.7 21.8 fusion.100
  430.5 159.8 %all-reduce.18.cloned.1.call-done = f32[1024,2048]{1,0:T(8,128)} async-done(((f32[1024,2048]{1,0:T(8,128)}), f32[1024,2048]{1,0:T(8,128)}) %all-reduce.18.cloned.1.call-update) | async-done | bytes 8388624 | tf_op jit(solution)/shard_map/psum | solution.py:120
  590.3 8.1 multiply_reduce_fusion.2
  598.5 5.1 fusion.94
  603.6 3.2 convert_reduce_fusion.3
  608.9 5.2 convolution_convert_fusion
  614.3 10.7 fusion.103
  625.6 4.6 fusion.29
  630.2 30.4 %fusion.67 = bf16[8,128,512]{2,1,0:T(8,128)(2,1)} fusion(bf16[1024,8,128]{0,2,1:T(8,128)(2,1)} %bitcast.99, f32[8,512,1024]{2,1,0:T(8,128)} %fusion.103, f32[8,512,1024]{2,1,0:T(8,128)} %copy-done.4, f32[8,512]{1,0:T(8,128)S(1)} %log_add_fusion), kind=kOutput, calls=%fused_computation.98 | convolution fusion | flops 1103631360 | bytes 36716544 | tf_op jit(solution)/shard_map/hqk,khd->qhd/dot_general | solution.py:147
  660.6 31.4 %fusion.36 = f32[8,128,1024]{2,1,0:T(8,128)} fusion(bf16[512,8,128]{0,2,1:T(8,128)(2,1)} %bitcast.104, f32[8,512,1024]{2,1,0:T(8,128)} %fusion.103, f32[8,512,1024]{2,1,0:T(8,128)} %copy-done.4, f32[8,512]{1,0:T(8,128)S(1)} %log_add_fusion), kind=kOutput, calls=%fused_computation.64 | convolution fusion | flops 1103107072 | bytes 38813696 | tf_op jit(solution)/shard_map/hqk,qhd->khd/dot_general | solution.py:149
  692.1 8.1 fusion.102
  700.2 9.4 convert_reduce_fusion.4
  709.6 37.1 %fusion.64 = bf16[8,128,512]{2,1,0:T(8,128)(2,1)} fusion(bf16[1024,8,128]{0,2,1:T(8,128)(2,1)S(1)} %bitcast.100, f32[8,512,1024]{2,1,0:T(8,128)} %fusion.102, f32[8,512,1024]{2,1,0:T(8,128)} %copy-done.3, f32[8,512]{1,0:T(8,128)S(1)} %log_add_fusion.1), kind=kOutput, calls=%fused_computation.97 | convolution fusion | flops 1103631360 | bytes 36716544 | tf_op jit(solution)/shard_map/hqk,khd->qhd/dot_general | solution.py:147
  746.6 31.7 %add_convert_fusion.5 = bf16[8,128,1024]{2,1,0:T(8,128)(2,1)} fusion(f32[8,128,1024]{2,1,0:T(8,128)} %fusion.36, bf16[512,8,128]{0,2,1:T(8,128)(2,1)S(1)} %bitcast.102, f32[8,512,1024]{2,1,0:T(8,128)} %fusion.102, f32[8,512,1024]{2,1,0:T(8,128)} %copy-done.3, f32[8,512]{1,0:T(8,128)S(1)} %log_add_fusion.1), kind=kOutput, calls=%fused_computation.84 | convolution fusion | flops 1105204224 | bytes 40910848 | tf_op jit(solution)/shard_map/hqk,qhd->khd/dot_general | solution.py:149
  778.4 10.8 fusion.104
  789.2 7.1 fusion.73
  796.4 10.4 add_add_fusion.2
  807.8 377.5 %all-reduce.22.cloned.1.call-done = (f32[1024,2048]{1,0:T(8,128)}, f32[1024,2048]{1,0:T(8,128)}) async-done(((f32[1024,2048]{1,0:T(8,128)}, f32[1024,2048]{1,0:T(8,128)}), (f32[1024,2048]{1,0:T(8,128)}, f32[1024,2048]{1,0:T(8,128)})) %all-reduce.22.cloned.1.call-update) | async-done | bytes 16777232 | tf_op jit(solution)/shard_map/psum | solution.py:107
  1185.4 6.9 fusion.91
  1192.3 1.4 copy-done.6
  1193.7 4.5 fusion.26
  1198.2 8.0 convert_reduce_fusion.2
  1206.7 10.7 fusion.70
  1217.4 1.5 copy-done.21
  1218.9 9.1 fusion.106
  1228.1 1.5 copy-done.68
  1229.6 9.1 fusion.105
  1240.2 9.1 fusion.72
  1250.0 26.3 %fusion.89 = f32[2048,4096]{1,0:T(8,128)} fusion(bf16[1024,4096]{1,0:T(8,128)(2,1)} %get-tuple-element.70, f32[1024,2048]{1,0:T(8,128)} %copy-done, f32[2048]{0:T(1024)S(1)} %copy-done.65, f32[2048]{0:T(1024)S(1)} %copy-done.52, f32[1024]{0:T(1024)S(1)} %copy-done.47, f32[1024]{0:T(1024)S(1)} %copy-done.36), kind=kOutput, calls=%fused_computation.133 | convolution fusion | flops 17190354944 | bytes 50356224 | tf_op jit(solution)/shard_map/td,tf->df/dot_general | solution.py:117
  1276.4 25.6 %fusion.107 = f32[4096,2048]{1,0:T(8,128)} fusion(bf16[1024,4096]{1,0:T(8,128)(2,1)} %copy-done.13, bf16[1024,2048]{1,0:T(8,128)(2,1)} %param.35), kind=kOutput, calls=%fused_computation.149 | convolution fusion | flops 17179869184 | bytes 46137344 | tf_op jit(solution)/shard_map/tf,td->fd/dot_general | solution.py:112
  1304.5 11.0 add_convert_fusion.2
  1315.5 1.3 dynamic-slice.1
  1316.8 1.3 dynamic-slice.3
  1318.0 1.3 dynamic-slice.9
  1321.8 1.3 dynamic-slice.17
  1324.5 1.4 constant_dynamic-slice_fusion.1
  1325.9 79.4 %reduce-scatter.16.cloned.1.call-done = f32[1024,128]{1,0:T(8,128)} async-done(((f32[1024,2048]{1,0:T(8,128)}), f32[1024,128]{1,0:T(8,128)}) %reduce-scatter.16.cloned.1.call-update) | async-done | bytes 524304 | tf_op jit(solution)/shard_map/reduce_scatter | solution.py:194
  1405.3 107.6 %reduce-scatter.14.cloned.1.call-done = f32[128,1024]{1,0:T(8,128)} async-done(((f32[2048,1024]{1,0:T(8,128)}), f32[128,1024]{1,0:T(8,128)}) %reduce-scatter.14.cloned.1.call-update) | async-done | bytes 524304 | tf_op jit(solution)/shard_map/reduce_scatter | solution.py:192
  1513.0 107.8 %reduce-scatter.12.cloned.1.call-done = f32[128,1024]{1,0:T(8,128)} async-done(((f32[2048,1024]{1,0:T(8,128)}), f32[128,1024]{1,0:T(8,128)}) %reduce-scatter.12.cloned.1.call-update) | async-done | bytes 524304 | tf_op jit(solution)/shard_map/reduce_scatter | solution.py:191
  1620.7 107.8 %reduce-scatter.10.cloned.1.call-done = f32[128,1024]{1,0:T(8,128)} async-done(((f32[2048,1024]{1,0:T(8,128)}), f32[128,1024]{1,0:T(8,128)}) %reduce-scatter.10.cloned.1.call-update) | async-done | bytes 524304 | tf_op jit(solution)/shard_map/reduce_scatter | solution.py:189
  1728.5 334.9 %reduce-scatter.18.cloned.1.call-done = f32[128,4096]{1,0:T(8,128)} async-done(((f32[2048,4096]{1,0:T(8,128)}), f32[128,4096]{1,0:T(8,128)}) %reduce-scatter.18.cloned.1.call-update) | async-done | bytes 2097168 | tf_op jit(solution)/shard_map/reduce_scatter | solution.py:198
  2063.4 334.1 %reduce-scatter.20.cloned.1.call-done = f32[4096,128]{1,0:T(8,128)} async-done(((f32[4096,2048]{1,0:T(8,128)}), f32[4096,128]{1,0:T(8,128)}) %reduce-scatter.20.cloned.1.call-update) | async-done | bytes 2097168 | tf_op jit(solution)/shard_map/reduce_scatter | solution.py:200
  (195 shorter events, 18.5 us)
Async XLA Ops:
  7.2 8.8 copy-start.32
  7.2 8.8 copy-start.54
  7.2 269.8 %all-reduce.16.cloned.1.call-start = ((), (), s32[]{:S(2)}) async-start(), calls=%async_computation.6 | async-start | bytes 16777216 | tf_op jit(solution)/shard_map/psum | solution.py:99
  7.3 8.7 copy-start.1
  8.1 9.7 copy-start.59
  17.8 12.2 copy-start.16
  17.8 4.9 copy-start.60
  17.9 4.9 copy-start.66
  22.8 29.4 %copy-start.14 = (bf16[1024,1024]{0,1:T(8,128)(2,1)}, bf16[1024,1024]{0,1:T(8,128)(2,1)S(1)}, u32[]{:S(2)}) copy-start(bf16[1024,1024]{0,1:T(8,128)(2,1)S(1)} %convolution_convert_fusion.1) | copy-start | bytes 6291460
  22.8 7.3 copy-start.62
  22.8 7.3 copy-start.67
  28.9 23.3 copy-start.17
  35.0 24.6 %copy-start.8 = (bf16[1024,1024]{0,1:T(8,128)(2,1)}, bf16[1024,1024]{0,1:T(8,128)(2,1)S(1)}, u32[]{:S(2)}) copy-start(bf16[1024,1024]{0,1:T(8,128)(2,1)S(1)} %add_convert_fusion.7) | copy-start | bytes 6291460
  40.6 5.7 copy-start.4
  40.6 6.1 copy-start.28
  44.4 7.8 copy-start.39
  55.8 5.7 copy-start.3
  55.8 6.1 copy-start.30
  66.6 9.5 copy-start.70
  66.6 210.4 %copy-start.55 = (f32[2048]{0:T(1024)S(1)}, f32[2048]{0:T(1024)}, u32[]{:S(2)}) copy-start(f32[2048]{0:T(1024)} %param.28) | copy-start | bytes 24580
  76.0 514.2 %all-reduce.18.cloned.1.call-start = ((), (), s32[]{:S(2)}) async-start(), calls=%async_computation.7 | async-start | bytes 16777216 | tf_op jit(solution)/shard_map/psum | solution.py:120
  282.7 26.1 %copy-start = (f32[1024,2048]{1,0:T(8,128)}, f32[1024,2048]{1,0:T(8,128)S(1)}, u32[]{:S(2)}) copy-start(f32[1024,2048]{1,0:T(8,128)S(1)} %get-tuple-element.77) | copy-start | bytes 25165828
  282.8 26.1 %copy-start.34 = (f32[1024]{0:T(1024)}, f32[1024]{0:T(1024)S(1)}, u32[]{:S(2)}) copy-start(f32[1024]{0:T(1024)S(1)} %broadcast_multiply_fusion) | copy-start | bytes 12292
  283.7 25.1 %copy-start.43 = (f32[1024]{0:T(1024)}, f32[1024]{0:T(1024)S(1)}, u32[]{:S(2)}) copy-start(f32[1024]{0:T(1024)S(1)} %multiply_reduce_fusion.4) | copy-start | bytes 12292
  283.8 25.1 %copy-start.45 = (f32[1024]{0:T(1024)}, f32[1024]{0:T(1024)S(1)}, u32[]{:S(2)}) copy-start(f32[1024]{0:T(1024)S(1)} %fusion.75) | copy-start | bytes 12292
  283.8 25.1 %copy-start.10 = (bf16[1024,2048]{1,0:T(8,128)(2,1)S(1)}, bf16[1024,2048]{1,0:T(8,128)(2,1)}, u32[]{:S(2)}) copy-start(bf16[1024,2048]{1,0:T(8,128)(2,1)} %param.35) | copy-start | bytes 12582916
  283.8 25.0 %copy-start.53 = (f32[32,128]{1,0:T(8,128)S(1)}, f32[32,128]{1,0:T(8,128)}, u32[]{:S(2)}) copy-start(f32[32,128]{1,0:T(8,128)} %param.32) | copy-start | bytes 49156
  308.9 60.9 %copy-start.57 = (bf16[2048,4096]{1,0:T(8,128)(2,1)S(1)}, bf16[2048,4096]{1,0:T(8,128)(2,1)}, u32[]{:S(2)}) copy-start(bf16[2048,4096]{1,0:T(8,128)(2,1)} %param.31) | copy-start | bytes 50331652
  391.7 793.7 %all-reduce.22.cloned.1.call-start = ((), (), s32[]{:S(2)}) async-start(), calls=%async_computation.15 | async-start | bytes 33554432 | tf_op jit(solution)/shard_map/psum | solution.py:107
  408.7 181.5 %copy-start.35 = (f32[1024]{0:T(1024)S(1)}, f32[1024]{0:T(1024)}, u32[]{:S(2)}) copy-start(f32[1024]{0:T(1024)} %copy-done.34) | copy-start | bytes 12292
  408.7 181.5 %copy-start.46 = (f32[1024]{0:T(1024)S(1)}, f32[1024]{0:T(1024)}, u32[]{:S(2)}) copy-start(f32[1024]{0:T(1024)} %copy-done.45) | copy-start | bytes 12292
  408.7 181.5 %copy-start.51 = (f32[2048]{0:T(1024)S(1)}, f32[2048]{0:T(1024)}, u32[]{:S(2)}) copy-start(f32[2048]{0:T(1024)} %param.29) | copy-start | bytes 24580
  430.5 167.9 %copy-start.44 = (f32[1024]{0:T(1024)S(1)}, f32[1024]{0:T(1024)}, u32[]{:S(2)}) copy-start(f32[1024]{0:T(1024)} %copy-done.43) | copy-start | bytes 12292
  590.3 8.2 copy-start.7
  598.5 5.1 copy-start.11
  603.6 5.3 copy-start.58
  607.8 6.3 copy-start.19
  608.9 5.4 copy-start.9
  614.1 10.9 slice-start
  614.3 10.7 slice-start.1
  614.3 10.7 slice-start.2
  614.3 11.3 slice-start.3
  692.1 8.1 copy-start.12
  700.2 9.4 copy-start.15
  709.6 37.1 %copy-start.18 = (bf16[512,1024]{0,1:T(8,128)(2,1)S(1)}, bf16[512,1024]{0,1:T(8,128)(2,1)}, u32[]{:S(2)}) copy-start(bf16[512,1024]{0,1:T(8,128)(2,1)} %copy-done.17) | copy-start | bytes 3145732
  778.4 10.8 copy-start.22
  778.4 10.8 copy-start.24
  778.4 10.8 copy-start.61
  789.2 7.2 copy-start.20
  789.2 7.1 copy-start.63
  806.8 378.6 %copy-start.27 = (f32[1024]{0:T(1024)S(1)}, f32[1024]{0:T(1024)}, u32[]{:S(2)}) copy-start(f32[1024]{0:T(1024)} %copy-done.26) | copy-start | bytes 12292
  806.8 378.6 %copy-start.33 = (f32[2048]{0:T(1024)S(1)}, f32[2048]{0:T(1024)}, u32[]{:S(2)}) copy-start(f32[2048]{0:T(1024)} %param.20) | copy-start | bytes 24580
  806.8 385.5 %copy-start.49 = (f32[1024]{0:T(1024)S(1)}, f32[1024]{0:T(1024)}, u32[]{:S(2)}) copy-start(f32[1024]{0:T(1024)} %copy-done.48) | copy-start | bytes 12292
  806.8 385.5 %copy-start.38 = (f32[1024]{0:T(1024)S(1)}, f32[1024]{0:T(1024)}, u32[]{:S(2)}) copy-start(f32[1024]{0:T(1024)} %copy-done.37) | copy-start | bytes 12292
  806.9 508.7 %all-reduce.20.cloned.1.call-start = ((), (), s32[]{:S(2)}) async-start(), calls=%async_computation.14 | async-start | bytes 147456
  1185.4 7.0 copy-start.2
  1185.4 8.3 copy-start.6
  1185.4 12.8 slice-start.4
  1206.2 199.1 %reduce-scatter.16.cloned.1.call-start = ((), (), s32[]{:S(2)}) async-start(), calls=%async_computation.11 | async-start | bytes 8912896 | tf_op jit(solution)/shard_map/reduce_scatter | solution.py:194
  1217.4 295.6 %reduce-scatter.14.cloned.1.call-start = ((), (), s32[]{:S(2)}) async-start(), calls=%async_computation.10 | async-start | bytes 8912896 | tf_op jit(solution)/shard_map/reduce_scatter | solution.py:192
  1228.0 392.7 %reduce-scatter.12.cloned.1.call-start = ((), (), s32[]{:S(2)}) async-start(), calls=%async_computation.9 | async-start | bytes 8912896 | tf_op jit(solution)/shard_map/reduce_scatter | solution.py:191
  1238.7 489.8 %reduce-scatter.10.cloned.1.call-start = ((), (), s32[]{:S(2)}) async-start(), calls=%async_computation.8 | async-start | bytes 8912896 | tf_op jit(solution)/shard_map/reduce_scatter | solution.py:189
  1249.3 814.1 %reduce-scatter.18.cloned.1.call-start = ((), (), s32[]{:S(2)}) async-start(), calls=%async_computation.12 | async-start | bytes 35651584 | tf_op jit(solution)/shard_map/reduce_scatter | solution.py:198
  1276.3 1121.2 %reduce-scatter.20.cloned.1.call-start = ((), (), s32[]{:S(2)}) async-start(), calls=%async_computation.13 | async-start | bytes 35651584 | tf_op jit(solution)/shard_map/reduce_scatter | solution.py:200
  (24 other events, 42.9 us)
Sparse Core Ops, SparseCore 0:
  76.2 200.7 all-reduce.15
  391.8 198.3 all-reduce.17
  807.0 378.3 all-reduce.21
  1206.4 89.5 all-reduce.19
  1300.5 104.8 reduce-scatter.15
  1409.8 103.0 reduce-scatter.13
  1517.6 103.0 reduce-scatter.11
  1625.4 103.0 reduce-scatter.9
  1733.3 330.0 reduce-scatter.17
  2068.1 329.4 reduce-scatter.19
where the time goes:
time: 2420 us; the launch traced here: 2400 us
  waiting for transfers between devices  1810 us (75%)
  matrix products  460 us (19%)
  other arithmetic  84.7 us (4%)
  local copies, waits for them, and re-layouts  32.1 us (1%)
    psum x1, waiting for transfers between devices, body(): lax.psum(jnp.dot(acts, down_weight, preferred_element_type=jnp.float32),...  378 us
    reduce_scatter x1, waiting for transfers between devices, body(): lax.psum_scatter(up_weight_grad, 'dp', scatter_dimension=0, tiled=True)  335 us
    reduce_scatter x1, waiting for transfers between devices, body(): lax.psum_scatter(down_weight_grad, 'dp', scatter_dimension=1, tiled=True)  334 us
    psum x1, waiting for transfers between devices, body(): lax.psum(jnp.dot(mixed, out_weight, preferred_element_type=jnp.float32),...  201 us
    psum x1, waiting for transfers between devices, body(): lax.psum(jnp.einsum('tf,df->td', hidden_grad, up_weight, preferred_elemen...  160 us
    reduce_scatter x1, waiting for transfers between devices, body(): lax.psum_scatter(key_weight_grad, 'dp', scatter_dimension=0, tiled=True)  108 us
    reduce_scatter x1, waiting for transfers between devices, body(): lax.psum_scatter(query_weight_grad, 'dp', scatter_dimension=0, tiled=True)  108 us
    reduce_scatter x1, waiting for transfers between devices, body(): lax.psum_scatter(value_weight_grad, 'dp', scatter_dimension=0, tiled=True)  108 us
  transfers between devices with their start and end apart: 10, of which 9 were waited for; matrix products, arithmetic and copies ran while one was open for 6% of the time, Pallas kernels for 0%

commit v1 on v0

v1 whole, which is shorter than its diff:
```python
import math

import jax
import jax.numpy as jnp
from jax import lax
from jax.sharding import Mesh
from jax.sharding import PartitionSpec as P

F32 = jnp.float32
BF16 = jnp.bfloat16
CHUNKS = 4


def swap(value, axis):
    return lax.ppermute(value, axis, [(0, 1), (1, 0)])


def mm(left, right, contract):
    return lax.dot_general(left, right, (contract, ((), ())), preferred_element_type=F32)


def norm_parts(field):
    average = jnp.mean(field, -1, keepdims=True)
    centred = field - average
    variance = jnp.mean(centred * centred, -1, keepdims=True)
    scale = lax.rsqrt(variance + 1e-05)
    return centred * scale, scale


def norm_pull(grad, unit, scale, gain):
    scaled = grad * gain
    first = jnp.mean(scaled, -1, keepdims=True)
    second = jnp.mean(scaled * unit, -1, keepdims=True)
    return scale * (scaled - first - unit * second)


def exact_gelu(field):
    return jax.nn.gelu(field, approximate=False)


def body(
    inputs,
    prefix_len,
    norm1_gain,
    norm1_bias,
    query_weight,
    query_bias,
    key_weight,
    value_weight,
    value_bias,
    out_weight,
    out_bias,
    norm2_gain,
    norm2_bias,
    up_weight,
    up_bias,
    down_weight,
    down_bias,
    out_grad,
):
    length, width = inputs.shape
    heads_local, head_dim = query_bias.shape
    zs, xs, cs = lax.axis_size("z"), lax.axis_size("x"), lax.axis_size("c")
    dps = zs * xs * cs
    at_x, at_c = lax.axis_index("x"), lax.axis_index("c")
    here, over_x = at_x * 2 + at_c, (1 - at_x) * 2 + at_c
    over_c, over_xc = at_x * 2 + 1 - at_c, (1 - at_x) * 2 + 1 - at_c
    block_rows = min(512, length)
    block_count = length // block_rows
    chunk = length // CHUNKS
    score_scale = 1.0 / math.sqrt(head_dim)
    boundary = prefix_len[0]

    def pieces(field):
        parts = field.reshape(length, zs, xs * cs, width // dps)
        return jnp.transpose(parts, (2, 0, 1, 3)).reshape(xs * cs, length, width // (xs * cs))

    def reduce_weight(parts, other, by_rows):
        def part(index):
            piece = lax.dynamic_index_in_dim(parts, index, 0, keepdims=False)
            if by_rows:
                return mm(piece, other, ((0,), (0,)))
            return mm(other, piece, ((0,), (0,)))

        far = swap(part(over_xc), "c")
        near = swap(part(over_c), "c")
        across = swap(part(over_x) + far, "x")
        total = part(here) + near + across
        return lax.psum_scatter(total, "z", scatter_dimension=0 if by_rows else 1, tiled=True)

    features = inputs.astype(F32)
    unit1, scale1 = norm_parts(features)
    normed = (unit1 * norm1_gain + norm1_bias).astype(BF16)
    queries = (mm(normed, query_weight, ((1,), (0,))) + query_bias.reshape(-1)).astype(BF16)
    keys = mm(normed, key_weight, ((1,), (0,))).astype(BF16)
    values = (mm(normed, value_weight, ((1,), (0,))) + value_bias.reshape(-1)).astype(BF16)
    queries = queries.reshape(length, heads_local, head_dim)
    keys = keys.reshape(length, heads_local, head_dim)
    values = values.reshape(length, heads_local, head_dim)

    def block_scores(row_begin, seen):
        query_block = queries[row_begin : row_begin + block_rows]
        scores = (
            jnp.einsum("qhd,khd->hqk", query_block, keys[:seen], preferred_element_type=F32)
            * score_scale
        )
        rows = row_begin + jnp.arange(block_rows, dtype=jnp.int32)
        positions = jnp.arange(seen, dtype=jnp.int32)
        visible = (positions[None, :] <= rows[:, None]) | (positions[None, :] < boundary)
        return (query_block, jnp.where(visible[None], scores, -1e30))

    mixed_blocks = []
    totals_log = []
    attn_parts = []
    for block_index in range(block_count):
        row_begin = block_index * block_rows
        seen = max(row_begin + block_rows, length // 2)
        query_block, scores = block_scores(row_begin, seen)
        peak = jnp.max(scores, -1, keepdims=True)
        exps = jnp.exp(scores - peak)
        sums = jnp.sum(exps, -1, keepdims=True)
        probs = exps / sums
        totals_log.append(peak + jnp.log(sums))
        mixed_block = (
            jnp.einsum(
                "hqk,khd->qhd", probs.astype(BF16), values[:seen], preferred_element_type=F32
            )
            .astype(BF16)
            .reshape(block_rows, heads_local * head_dim)
        )
        mixed_blocks.append(mixed_block)
        for begin in range(0, block_rows, chunk):
            attn_parts.append(mm(mixed_block[begin : begin + chunk], out_weight, ((1,), (0,))))
    mixed = jnp.concatenate(mixed_blocks, 0)
    attn_others = [swap(part, "mp") for part in attn_parts]

    resids, units2, scales2, normeds2, acts, hidden_grads = [], [], [], [], [], []
    norm2_parts, branch_parts, up_bias_grad = [], [], 0.0
    for index in range(CHUNKS):
        rows = slice(index * chunk, (index + 1) * chunk)
        resid = features[rows] + ((attn_parts[index] + attn_others[index]) + out_bias)
        unit2, scale2 = norm_parts(resid)
        normed2 = (unit2 * norm2_gain + norm2_bias).astype(BF16)
        hidden = mm(normed2, up_weight, ((1,), (0,))) + up_bias.reshape(-1)
        acts_float, gelu_pull = jax.vjp(exact_gelu, hidden)
        act = acts_float.astype(BF16)
        acts_grad = mm(out_grad[rows], down_weight, ((1,), (1,)))
        hidden_grad = gelu_pull(acts_grad)[0].astype(BF16)
        up_bias_grad = up_bias_grad + jnp.sum(hidden_grad.astype(F32), 0)
        norm2_parts.append(mm(hidden_grad, up_weight, ((1,), (1,))))
        branch_parts.append(mm(act, down_weight, ((1,), (0,))))
        resids.append(resid)
        units2.append(unit2)
        scales2.append(scale2)
        normeds2.append(normed2)
        acts.append(act)
        hidden_grads.append(hidden_grad)
    norm2_others = [swap(part, "mp") for part in norm2_parts]
    branch_others = [swap(part, "mp") for part in branch_parts]

    acts = jnp.concatenate(acts, 0)
    hidden_grads = jnp.concatenate(hidden_grads, 0)
    normed2 = jnp.concatenate(normeds2, 0)
    down_weight_grad = reduce_weight(pieces(out_grad), acts, False)
    up_weight_grad = reduce_weight(pieces(normed2), hidden_grads, True)

    grad_float = out_grad.astype(F32)
    down_bias_grad = jnp.sum(grad_float, 0)

    resid_grads, attn_grads, mixed_grads = [], [], []
    norm2_gain_grad, norm2_bias_grad, out_bias_grad = 0.0, 0.0, 0.0
    for index in range(CHUNKS):
        rows = slice(index * chunk, (index + 1) * chunk)
        norm2_in = norm2_parts[index] + norm2_others[index]
        norm2_bias_grad = norm2_bias_grad + jnp.sum(norm2_in, 0)
        norm2_gain_grad = norm2_gain_grad + jnp.sum(norm2_in * units2[index], 0)
        resid_grad = grad_float[rows] + norm_pull(norm2_in, units2[index], scales2[index], norm2_gain)
        attn_grad = resid_grad.astype(BF16)
        out_bias_grad = out_bias_grad + jnp.sum(attn_grad.astype(F32), 0)
        mixed_grads.append(mm(attn_grad, out_weight, ((1,), (1,))).astype(BF16))
        resid_grads.append(resid_grad)
        attn_grads.append(attn_grad)
    mixed_grad = jnp.concatenate(mixed_grads, 0).reshape(length, heads_local, head_dim)
    attn_grad = jnp.concatenate(attn_grads, 0)
    out_weight_grad = reduce_weight(pieces(attn_grad), mixed, False)

    query_blocks = []
    key_accum = jnp.zeros((length, heads_local, head_dim), F32)
    value_accum = jnp.zeros((length, heads_local, head_dim), F32)
    for block_index in range(block_count):
        row_begin = block_index * block_rows
        seen = max(row_begin + block_rows, length // 2)
        query_block, scores = block_scores(row_begin, seen)
        probs = jnp.exp(scores - totals_log[block_index])
        mixed_block = mixed_grad[row_begin : row_begin + block_rows]
        prob_grad = jnp.einsum(
            "qhd,khd->hqk", mixed_block, values[:seen], preferred_element_type=F32
        )
        row_dot = jnp.sum(probs * prob_grad, -1, keepdims=True)
        score_grad = (probs * (prob_grad - row_dot) * score_scale).astype(BF16)
        query_blocks.append(
            jnp.einsum("hqk,khd->qhd", score_grad, keys[:seen], preferred_element_type=F32)
        )
        key_accum = key_accum.at[:seen].add(
            jnp.einsum("hqk,qhd->khd", score_grad, query_block, preferred_element_type=F32)
        )
        value_accum = value_accum.at[:seen].add(
            jnp.einsum("hqk,qhd->khd", probs.astype(BF16), mixed_block, preferred_element_type=F32)
        )
    flat = (length, heads_local * head_dim)
    query_grad = jnp.concatenate(query_blocks, 0).astype(BF16).reshape(flat)
    key_grad = key_accum.astype(BF16).reshape(flat)
    value_grad = value_accum.astype(BF16).reshape(flat)
    query_bias_grad = jnp.sum(query_grad.astype(F32), 0)
    value_bias_grad = jnp.sum(value_grad.astype(F32), 0)

    norm1_parts = []
    norm1_gain_grad, norm1_bias_grad = 0.0, 0.0
    for index in range(CHUNKS):
        rows = slice(index * chunk, (index + 1) * chunk)
        part = mm(query_grad[rows], query_weight, ((1,), (1,)))
        part = part + mm(key_grad[rows], key_weight, ((1,), (1,)))
        part = part + mm(value_grad[rows], value_weight, ((1,), (1,)))
        norm1_parts.append(part)
        norm1_bias_grad = norm1_bias_grad + jnp.sum(part, 0)
        norm1_gain_grad = norm1_gain_grad + jnp.sum(part * unit1[rows], 0)
    norm1_others = [swap(part, "mp") for part in norm1_parts]

    normed_pieces = pieces(normed)
    query_weight_grad = reduce_weight(normed_pieces, query_grad, True)
    key_weight_grad = reduce_weight(normed_pieces, key_grad, True)
    value_weight_grad = reduce_weight(normed_pieces, value_grad, True)

    def blocks(vector, lead):
        return jnp.transpose(vector.reshape(lead, dps, -1), (1, 0, 2)).reshape(dps, -1)

    shared = jnp.concatenate([blocks(norm1_gain_grad, 1), blocks(norm1_bias_grad, 1)], 1)
    shared = shared + swap(shared, "mp")
    small = jnp.concatenate(
        [
            shared,
            blocks(query_bias_grad, heads_local),
            blocks(value_bias_grad, heads_local),
            blocks(out_bias_grad, 1),
            blocks(norm2_gain_grad, 1),
            blocks(norm2_bias_grad, 1),
            blocks(up_bias_grad, up_bias.shape[0]),
            blocks(down_bias_grad, 1),
        ],
        1,
    )
    small = small.reshape(zs, xs * cs, -1)

    def take(field, index, axis):
        return lax.dynamic_index_in_dim(field, index, axis, keepdims=False)

    far = swap(jnp.stack([take(small, over_xc, 1), take(small, over_c, 1)]), "c")
    across = swap(take(small, over_x, 1) + far[0], "x")
    small = take(small, here, 1) + far[1] + across
    at_z, span = lax.axis_index("z"), zs
    while span > 1:
        span //= 2
        halves = small.reshape(2, span, -1)
        side = (at_z // span) % 2
        pairs = [(i, i ^ span) for i in range(zs)]
        other = lax.ppermute(take(halves, 1 - side, 0), "z", pairs)
        small = take(halves, side, 0) + other
    small = small.reshape(-1)

    in_grads, outputs = [], []
    for index in range(CHUNKS):
        rows = slice(index * chunk, (index + 1) * chunk)
        outputs.append(
            (resids[index] + ((branch_parts[index] + branch_others[index]) + down_bias)).astype(BF16)
        )
        norm1_in = norm1_parts[index] + norm1_others[index]
        pulled = norm_pull(norm1_in, unit1[rows], scale1[rows], norm1_gain)
        in_grads.append((resid_grads[index] + pulled).astype(BF16))
    outputs = jnp.concatenate(outputs, 0)
    in_grad = jnp.concatenate(in_grads, 0)

    wide = width // dps
    thin = head_dim // dps
    sizes = [wide, wide, heads_local * thin, heads_local * thin, wide, wide, wide]
    sizes += [up_bias.shape[0] * thin, wide]
    split, begin = [], 0
    for size in sizes:
        split.append(small[begin : begin + size])
        begin += size
    gain1, bias1, query_b, value_b, out_b, gain2, bias2, up_b, down_b = split
    return (
        outputs,
        in_grad,
        gain1,
        bias1,
        query_weight_grad,
        query_b.reshape(heads_local, thin),
        key_weight_grad,
        value_weight_grad,
        value_b.reshape(heads_local, thin),
        out_weight_grad,
        out_b,
        gain2,
        bias2,
        up_weight_grad,
        up_b.reshape(-1, thin),
        down_weight_grad,
        down_b,
    )


def solution(mesh):
    dps = mesh.shape["dp"]
    fine = Mesh(mesh.devices.reshape(dps // 4, 2, 2, mesh.shape["mp"]), ("z", "x", "c", "mp"))
    dp = ("z", "x", "c")
    in_specs = (
        P(dp, None),
        P(dp),
        P(),
        P(),
        P(None, "mp"),
        P("mp", None),
        P(None, "mp"),
        P(None, "mp"),
        P("mp", None),
        P("mp", None),
        P(),
        P(),
        P(),
        P(None, "mp"),
        P("mp", None),
        P("mp", None),
        P(),
        P(dp, None),
    )
    out_specs = (
        P(dp, None),
        P(dp, None),
        P(dp),
        P(dp),
        P(dp, "mp"),
        P("mp", dp),
        P(dp, "mp"),
        P(dp, "mp"),
        P("mp", dp),
        P("mp", dp),
        P(dp),
        P(dp),
        P(dp),
        P(dp, "mp"),
        P("mp", dp),
        P("mp", dp),
        P(dp),
    )
    return jax.shard_map(body, mesh=fine, in_specs=in_specs, out_specs=out_specs, check_vma=False)
```

time: 2420 us -> 1690 us (0.70)
  waiting for transfers between devices: 1810 us -> 844 us
  matrix products: 460 us -> 555 us
  other arithmetic: 84.7 us -> 143 us
  local copies, waits for them, and re-layouts: 32.1 us -> 83.3 us
  starting transfers between devices: 0.99 us -> 30.6 us
    reduce_scatter x6, waiting for transfers between devices: 1070 us -> 0.08 us  [reduce_weight(): lax.psum_scatter(total, 'z', scatter_dimension=0 if by_rows else 1, tiled...]
    ppermute x0 -> x39, waiting for transfers between devices: none -> 844 us  [the longest x37 844 us: swap(): return lax.ppermute(value, axis, [(0, 1), (1, 0)])]
    psum x3 -> x0, waiting for transfers between devices: 738 us -> none  [the longest x1 378 us: body(): lax.psum(jnp.dot(acts, down_weight, preferred_element_type=jnp.float32),...]
    dot_general x28 -> x73, matrix products: 396 us -> 508 us  [the longest x63 415 us: mm(): lax.dot_general(left, right, (contract, ((), ())), preferred_element_type...]
    reshape x0 -> x12, local copies, waits for them, and re-layouts: none -> 47.3 us  [the longest x6 45.7 us: pieces(): parts = field.reshape(length, zs, xs * cs, width // dps)]
    add x0 -> x17, other arithmetic: none -> 37.1 us  [the longest x6 37 us: reduce_weight(): total = part(here) + near + across]
    ppermute x0 -> x39, starting transfers between devices: none -> 30.3 us  [the longest x37 26.5 us: swap(): return lax.ppermute(value, axis, [(0, 1), (1, 0)])]
    reduce_sum x10 -> x11, other arithmetic: 42 us -> 53.6 us  [the longest x2 15 us: body(): norm2_gain_grad = norm2_gain_grad + jnp.sum(norm2_in * units2[index], 0)]
  transfers between devices with their start and end apart: 10 -> 45, of which waited for: 9 -> 16; matrix products, arithmetic and copies ran while one was open for 6% -> 36% of each run, Pallas kernels for 0% -> 0%
where the time goes in v1:
time: 1690 us; the launch traced here: 1670 us
  waiting for transfers between devices  844 us (50%)
  matrix products  555 us (33%)
  other arithmetic  143 us (8%)
  local copies, waits for them, and re-layouts  83.3 us (5%)
  starting transfers between devices  30.6 us (2%)
  between operations  17.3 us (1%)
    ppermute x37, waiting for transfers between devices, swap(): return lax.ppermute(value, axis, [(0, 1), (1, 0)])  844 us
    dot_general x63, matrix products, mm(): lax.dot_general(left, right, (contract, ((), ())), preferred_element_type...  415 us
    dot_general x2, matrix products, body(): jnp.einsum('hqk,khd->qhd', score_grad, keys[:seen], preferred_element_typ...  52.3 us
    dot_general x2, matrix products, body(): jnp.einsum('hqk,qhd->khd', score_grad, query_block, preferred_element_typ...  47.3 us
    reshape x6, local copies, waits for them, and re-layouts, pieces(): parts = field.reshape(length, zs, xs * cs, width // dps)  45.7 us
    add x6, other arithmetic, reduce_weight(): total = part(here) + near + across  37 us
  transfers between devices with their start and end apart: 45, of which 16 were waited for; matrix products, arithmetic and copies ran while one was open for 36% of the time, Pallas kernels for 0%

profile of v1, /device:TPU:0, one launch (start us, length us, event | category | flops | bytes accessed | tf_op | source)
XLA Modules:
  0.0 1674.0 jit_solution(8439415277387278322)
XLA Ops:
  60.3 5.3 fusion.95
  79.8 7.7 reshape.596
  87.5 6.6 convert_element_type.194
  94.0 7.4 copy.87
  102.7 36.9 %collective-permute-done.2 = f32[256,2048]{1,0:T(8,128)} collective-permute-done((f32[256,2048]{1,0:T(8,128)}, f32[256,2048]{1,0:T(8,128)}, u32[]{:S(2)}, u32[]{:S(2)}) %collective-permute-start.2) | collective-permute-done | bytes 2097184 | tf_op jit(solution)/shard_map/ppermute | solution.py:15
  139.7 44.9 %collective-permute-done.4 = f32[256,2048]{1,0:T(8,128)} collective-permute-done((f32[256,2048]{1,0:T(8,128)S(1)}, f32[256,2048]{1,0:T(8,128)}, u32[]{:S(2)}, u32[]{:S(2)}) %collective-permute-start.4) | collective-permute-done | bytes 2097184 | tf_op jit(solution)/shard_map/ppermute | solution.py:15
  184.6 44.1 %collective-permute-done.6 = f32[256,2048]{1,0:T(8,128)} collective-permute-done((f32[256,2048]{1,0:T(8,128)}, f32[256,2048]{1,0:T(8,128)}, u32[]{:S(2)}, u32[]{:S(2)}) %collective-permute-start.6) | collective-permute-done | bytes 2097184 | tf_op jit(solution)/shard_map/ppermute | solution.py:15
  228.7 8.3 fusion.230
  243.2 18.6 %multiply_convert_fusion.5 = (bf16[256,4096]{1,0:T(8,128)(2,1)}, f32[256,4096]{1,0:T(8,128)S(1)}) fusion(f32[4096]{0:T(1024)S(1)} %bitcast.382, bf16[256,2048]{1,0:T(8,128)(2,1)S(1)} %get-tuple-element.226, bf16[2048,4096]{1,0:T(8,128)(2,1)} %param.43), kind=kOutput, calls=%fused_computation.114 | convolution fusion | flops 4364173312 | bytes 24133632 | tf_op jit(solution)/shard_map/dot_general | solution.py:19
  261.8 18.4 %convert_reduce_fusion.4 = (f32[4096]{0:T(1024)}, bf16[256,4096]{1,0:T(8,128)(2,1)S(1)}) fusion(f32[256,4096]{1,0:T(8,128)S(1)} %get-tuple-element.250, bf16[4096,2048]{1,0:T(8,128)(2,1)} %param.45, bf16[1024,2048]{1,0:T(8,128)(2,1)} %param.47), kind=kOutput, calls=%fused_computation.65 | convolution fusion | flops 4372557824 | bytes 24133632 | tf_op jit(solution)/shard_map/dot_general | solution.py:19
  280.2 10.2 fusion.251
  292.1 12.4 fusion.244
  304.8 16.3 multiply_convert_fusion.3
  321.2 6.0 fusion.248
  329.0 18.4 %convert_reduce_fusion.2 = (f32[4096]{0:T(1024)}, bf16[256,4096]{1,0:T(8,128)(2,1)S(1)}) fusion(f32[256,4096]{1,0:T(8,128)S(1)} %get-tuple-element.252, bf16[4096,2048]{1,0:T(8,128)(2,1)} %param.45, bf16[1024,2048]{1,0:T(8,128)(2,1)} %param.47), kind=kOutput, calls=%fused_computation.63 | convolution fusion | flops 4372557824 | bytes 24133632 | tf_op jit(solution)/shard_map/dot_general | solution.py:19
  347.4 10.3 fusion.255
  357.9 18.3 %multiply_convert_fusion.4 = (bf16[256,4096]{1,0:T(8,128)(2,1)}, f32[256,4096]{1,0:T(8,128)S(1)}) fusion(f32[4096]{0:T(1024)S(1)} %bitcast.384, bf16[256,2048]{1,0:T(8,128)(2,1)S(1)} %copy-done.51, bf16[2048,4096]{1,0:T(8,128)(2,1)} %param.43), kind=kOutput, calls=%fused_computation.101 | convolution fusion | flops 4364173312 | bytes 24133632 | tf_op jit(solution)/shard_map/dot_general | solution.py:19
  376.2 18.4 %convert_reduce_fusion.3 = (f32[4096]{0:T(1024)}, bf16[256,4096]{1,0:T(8,128)(2,1)S(1)}) fusion(f32[256,4096]{1,0:T(8,128)S(1)} %get-tuple-element.256, bf16[4096,2048]{1,0:T(8,128)(2,1)} %param.45, bf16[1024,2048]{1,0:T(8,128)(2,1)} %param.47), kind=kOutput, calls=%fused_computation.64 | convolution fusion | flops 4372557824 | bytes 24133632 | tf_op jit(solution)/shard_map/dot_general | solution.py:19
  394.6 10.5 fusion.252
  406.9 18.0 %multiply_convert_fusion.2 = (bf16[256,4096]{1,0:T(8,128)(2,1)}, f32[256,4096]{1,0:T(8,128)S(1)}) fusion(f32[4096]{0:T(1024)S(1)} %bitcast.385, bf16[256,2048]{1,0:T(8,128)(2,1)S(1)} %copy-done.54, bf16[2048,4096]{1,0:T(8,128)(2,1)} %param.43), kind=kOutput, calls=%fused_computation.75 | convolution fusion | flops 4364173312 | bytes 24133632 | tf_op jit(solution)/shard_map/dot_general | solution.py:19
  424.9 18.6 %convert_reduce_fusion.1 = (f32[4096]{0:T(1024)}, bf16[256,4096]{1,0:T(8,128)(2,1)S(1)}) fusion(f32[256,4096]{1,0:T(8,128)S(1)} %get-tuple-element.254, bf16[4096,2048]{1,0:T(8,128)(2,1)} %param.45, bf16[1024,2048]{1,0:T(8,128)(2,1)} %param.47), kind=kOutput, calls=%fused_computation.62 | convolution fusion | flops 4372557824 | bytes 24133632 | tf_op jit(solution)/shard_map/dot_general | solution.py:19
  443.5 10.2 fusion.256
  453.7 12.4 fusion.250
  466.4 8.8 fusion.246
  477.5 9.4 multiply_reduce_fusion.6
  486.9 32.1 %collective-permute-done.9 = f32[256,2048]{1,0:T(8,128)} collective-permute-done((f32[256,2048]{1,0:T(8,128)}, f32[256,2048]{1,0:T(8,128)}, u32[]{:S(2)}, u32[]{:S(2)}) %collective-permute-start.9) | collective-permute-done | bytes 2097184 | tf_op jit(solution)/shard_map/ppermute | solution.py:15
  519.0 44.8 %collective-permute-done.11 = f32[256,2048]{1,0:T(8,128)S(1)} collective-permute-done((f32[256,2048]{1,0:T(8,128)}, f32[256,2048]{1,0:T(8,128)S(1)}, u32[]{:S(2)}, u32[]{:S(2)}) %collective-permute-start.11) | collective-permute-done | bytes 2097184 | tf_op jit(solution)/shard_map/ppermute | solution.py:15
  563.9 5.6 multiply_reduce_fusion.5
  569.4 82.6 %collective-permute-done.3 = f32[256,2048]{1,0:T(8,128)S(1)} collective-permute-done((f32[256,2048]{1,0:T(8,128)S(1)}, f32[256,2048]{1,0:T(8,128)S(1)}, u32[]{:S(2)}, u32[]{:S(2)}) %collective-permute-start.3) | collective-permute-done | bytes 2097184 | tf_op jit(solution)/shard_map/ppermute | solution.py:15
  662.6 6.0 fusion.253
  668.6 6.9 convert_reduce_fusion.8
  680.7 8.2 fusion.257
  688.9 14.9 fusion.92
  703.8 37.5 %fusion.96 = bf16[8,128,512]{2,1,0:T(8,128)(2,1)} fusion(bf16[1024,8,128]{0,2,1:T(8,128)(2,1)S(1)} %bitcast.294, f32[8,512,1024]{2,1,0:T(8,128)} %fusion.257, f32[8,512,1024]{2,1,0:T(8,128)} %copy-done, f32[8,512]{1,0:T(8,128)S(1)} %copy-done.77), kind=kOutput, calls=%fused_computation.225 | convolution fusion | flops 1103631360 | bytes 36716544 | tf_op jit(solution)/shard_map/hqk,khd->qhd/dot_general | solution.py:202
  745.8 7.0 pad_maximum_fusion.5
  752.9 7.7 reshape.606
  760.6 7.7 copy.89
  779.0 7.8 fusion.107
  786.8 15.2 fusion.89
  802.0 32.1 %fusion.39 = bf16[1024,8,128]{0,2,1:T(8,128)(2,1)} fusion(f32[512,8,128]{0,2,1:T(8,128)} %fusion.89, bf16[512,8,128]{0,2,1:T(8,128)(2,1)} %bitcast.336, f32[8,512,1024]{2,1,0:T(8,128)} %fusion.257, f32[8,512,1024]{2,1,0:T(8,128)} %copy-done, f32[8,512]{1,0:T(8,128)S(1)} %copy-done.77), kind=kOutput, calls=%fused_computation.61 | convolution fusion | flops 1105204224 | bytes 38813696 | tf_op jit(solution)/shard_map/hqk,qhd->khd/dot_general | solution.py:205
  855.6 7.3 fusion.86
  862.9 6.3 convert_reduce_fusion.5
  876.5 26.8 %collective-permute-done.26 = f32[512,1024]{1,0:T(8,128)} collective-permute-done((f32[512,1024]{1,0:T(8,128)}, f32[512,1024]{1,0:T(8,128)}, u32[]{:S(2)}, u32[]{:S(2)}) %collective-permute-start.26) | collective-permute-done | bytes 2097184 | tf_op jit(solution)/shard_map/ppermute | solution.py:15
  907.7 9.6 fusion.110
  927.8 7.7 reshape.604
  935.5 7.5 copy.88
  950.7 9.6 convolution_add_fusion
  961.9 12.0 collective-permute-done.29
  988.1 6.6 copy.90
  994.7 4.9 copy.91
  1002.2 195.2 %collective-permute-done.32 = f32[1024,512]{1,0:T(8,128)} collective-permute-done((f32[1024,512]{1,0:T(8,128)}, f32[1024,512]{1,0:T(8,128)}, u32[]{:S(2)}, u32[]{:S(2)}) %collective-permute-start.32) | collective-permute-done | bytes 2097184 | tf_op jit(solution)/shard_map/ppermute | solution.py:15
  1201.9 9.5 fusion.100
  1211.4 5.8 fusion.112
  1217.2 10.1 add_add_fusion.1
  1227.4 9.8 fusion.103
  1237.5 10.6 convolution_add_fusion.1
  1248.9 9.3 fusion.105
  1261.0 170.0 %collective-permute-done.38 = f32[4096,512]{1,0:T(8,128)} collective-permute-done((f32[4096,512]{1,0:T(8,128)}, f32[4096,512]{1,0:T(8,128)}, u32[]{:S(2)}, u32[]{:S(2)}) %collective-permute-start.38) | collective-permute-done | bytes 8388640 | tf_op jit(solution)/shard_map/ppermute | solution.py:15
  1431.1 9.5 add_add_fusion
  1481.6 17.1 %collective-permute-done.12 = f32[256,2048]{1,0:T(8,128)} collective-permute-done((f32[256,2048]{1,0:T(8,128)S(1)}, f32[256,2048]{1,0:T(8,128)}, u32[]{:S(2)}, u32[]{:S(2)}) %collective-permute-start.12) | collective-permute-done | bytes 2097184 | tf_op jit(solution)/shard_map/ppermute | solution.py:15
  1498.7 44.9 %collective-permute-done.13 = f32[256,2048]{1,0:T(8,128)} collective-permute-done((f32[256,2048]{1,0:T(8,128)}, f32[256,2048]{1,0:T(8,128)}, u32[]{:S(2)}, u32[]{:S(2)}) %collective-permute-start.13) | collective-permute-done | bytes 2097184 | tf_op jit(solution)/shard_map/ppermute | solution.py:15
  1543.6 44.9 %collective-permute-done.14 = f32[256,2048]{1,0:T(8,128)} collective-permute-done((f32[256,2048]{1,0:T(8,128)}, f32[256,2048]{1,0:T(8,128)}, u32[]{:S(2)}, u32[]{:S(2)}) %collective-permute-start.14) | collective-permute-done | bytes 2097184 | tf_op jit(solution)/shard_map/ppermute | solution.py:15
  1588.6 42.7 %collective-permute-done.15 = f32[256,2048]{1,0:T(8,128)} collective-permute-done((f32[256,2048]{1,0:T(8,128)}, f32[256,2048]{1,0:T(8,128)}, u32[]{:S(2)}, u32[]{:S(2)}) %collective-permute-start.15) | collective-permute-done | bytes 2097184 | tf_op jit(solution)/shard_map/ppermute | solution.py:15
  1631.3 12.1 multiply_reduce_fusion.9
  (549 shorter events, 254.1 us)
Async XLA Ops:
  7.2 1659.6 %reduce-scatter.7.cloned.1.call-start = ((), (), s32[]{:S(2)}) async-start(), calls=%async_computation.6 | async-start | bytes 2621440 | tf_op jit(solution)/shard_map/reduce_scatter | solution.py:89
  21.3 16.5 copy-start.28
  29.3 21.7 %copy-start.36 = (bf16[512,1024]{0,1:T(8,128)(2,1)}, bf16[512,1024]{0,1:T(8,128)(2,1)S(1)}, u32[]{:S(2)}) copy-start(bf16[512,1024]{0,1:T(8,128)(2,1)S(1)} %get-tuple-element.207) | copy-start | bytes 3145732
  34.1 16.8 %copy-start.26 = (bf16[1024,1024]{0,1:T(8,128)(2,1)}, bf16[1024,1024]{0,1:T(8,128)(2,1)S(1)}, u32[]{:S(2)}) copy-start(bf16[1024,1024]{0,1:T(8,128)(2,1)S(1)} %convolution_convert_fusion) | copy-start | bytes 6291460
  44.9 57.8 %collective-permute-start = (f32[256,2048]{1,0:T(8,128)}, f32[256,2048]{1,0:T(8,128)}, u32[]{:S(2)}, u32[]{:S(2)}) collective-permute-start(f32[256,2048]{1,0:T(8,128)} %fusion.243), channel_id=1, source_target_pairs={{0,1},{1,0},{2,3},{3,2},{4,5},{5,4},{6,7},{7,6},{8,9},{9,8},{10,11... | collective-permute-start | bytes 6291464 | tf_op jit(solution)/shard_map/ppermute | solution.py:15
  50.5 89.1 %collective-permute-start.2 = (f32[256,2048]{1,0:T(8,128)}, f32[256,2048]{1,0:T(8,128)}, u32[]{:S(2)}, u32[]{:S(2)}) collective-permute-start(f32[256,2048]{1,0:T(8,128)} %fusion.245), channel_id=1, source_target_pairs={{0,1},{1,0},{2,3},{3,2},{4,5},{5,4},{6,7},{7,6},{8,9},{9,8},{10,11... | collective-permute-start | bytes 6291464 | tf_op jit(solution)/shard_map/ppermute | solution.py:15
  70.7 113.9 %collective-permute-start.4 = (f32[256,2048]{1,0:T(8,128)S(1)}, f32[256,2048]{1,0:T(8,128)}, u32[]{:S(2)}, u32[]{:S(2)}) collective-permute-start(f32[256,2048]{1,0:T(8,128)S(1)} %fusion.247), channel_id=1, source_target_pairs={{0,1},{1,0},{2,3},{3,2},{4,5},{5,4},{6,7},{7,6},{8,9},{9,8},{10,11... | collective-permute-start | bytes 6291464 | tf_op jit(solution)/shard_map/ppermute | solution.py:15
  75.4 153.2 %collective-permute-start.6 = (f32[256,2048]{1,0:T(8,128)}, f32[256,2048]{1,0:T(8,128)}, u32[]{:S(2)}, u32[]{:S(2)}) collective-permute-start(f32[256,2048]{1,0:T(8,128)} %fusion.249), channel_id=1, source_target_pairs={{0,1},{1,0},{2,3},{3,2},{4,5},{5,4},{6,7},{7,6},{8,9},{9,8},{10,11... | collective-permute-start | bytes 6291464 | tf_op jit(solution)/shard_map/ppermute | solution.py:15
  94.0 134.6 %copy-start.118 = (f32[2048]{0:T(1024)S(1)}, f32[2048]{0:T(1024)}, u32[]{:S(2)}) copy-start(f32[2048]{0:T(1024)} %param.40) | copy-start | bytes 24580
  243.1 18.6 %copy-start.49 = (bf16[256,2048]{1,0:T(8,128)(2,1)}, bf16[256,2048]{1,0:T(8,128)(2,1)S(1)}, u32[]{:S(2)}) copy-start(bf16[256,2048]{1,0:T(8,128)(2,1)S(1)} %get-tuple-element.226) | copy-start | bytes 3145732
  243.2 61.7 %copy-start.53 = (bf16[256,2048]{1,0:T(8,128)(2,1)}, bf16[256,2048]{1,0:T(8,128)(2,1)S(1)}, u32[]{:S(2)}) copy-start(bf16[256,2048]{1,0:T(8,128)(2,1)S(1)} %get-tuple-element.228) | copy-start | bytes 3145732
  290.4 175.7 %collective-permute-start.8 = (f32[256,2048]{1,0:T(8,128)}, f32[256,2048]{1,0:T(8,128)}, u32[]{:S(2)}, u32[]{:S(2)}) collective-permute-start(f32[256,2048]{1,0:T(8,128)} %fusion.251), channel_id=1, source_target_pairs={{0,1},{1,0},{2,3},{3,2},{4,5},{5,4},{6,7},{7,6},{8,9},{9,8},{10,11... | collective-permute-start | bytes 6291464 | tf_op jit(solution)/shard_map/ppermute | solution.py:15
  292.1 29.0 %slice-start.8 = ((s8[16777216]{0:T(1024)(128)(4,1)}), s8[4194304]{0:T(1024)(128)(4,1)S(1)}, s32[]{:S(2)}) async-start(s8[16777216]{0:T(1024)(128)(4,1)} %bitcast.380), calls=%async_computation.20 | async-start | bytes 8388608
  304.5 170.8 %collective-permute-start.1 = (f32[256,2048]{1,0:T(8,128)}, f32[256,2048]{1,0:T(8,128)}, u32[]{:S(2)}, u32[]{:S(2)}) collective-permute-start(f32[256,2048]{1,0:T(8,128)} %fusion.244), channel_id=1, source_target_pairs={{0,1},{1,0},{2,3},{3,2},{4,5},{5,4},{6,7},{7,6},{8,9},{9,8},{10,11... | collective-permute-start | bytes 6291464 | tf_op jit(solution)/shard_map/ppermute | solution.py:15
  304.8 16.3 slice-start.11
  327.2 149.9 %collective-permute-start.5 = (f32[256,2048]{1,0:T(8,128)}, f32[256,2048]{1,0:T(8,128)}, u32[]{:S(2)}, u32[]{:S(2)}) collective-permute-start(f32[256,2048]{1,0:T(8,128)} %fusion.248), channel_id=1, source_target_pairs={{0,1},{1,0},{2,3},{3,2},{4,5},{5,4},{6,7},{7,6},{8,9},{9,8},{10,11... | collective-permute-start | bytes 6291464 | tf_op jit(solution)/shard_map/ppermute | solution.py:15
  357.7 119.7 %collective-permute-start.10 = (f32[256,2048]{1,0:T(8,128)}, f32[256,2048]{1,0:T(8,128)}, u32[]{:S(2)}, u32[]{:S(2)}) collective-permute-start(f32[256,2048]{1,0:T(8,128)} %fusion.255), channel_id=1, source_target_pairs={{0,1},{1,0},{2,3},{3,2},{4,5},{5,4},{6,7},{7,6},{8,9},{9,8},{10,11... | collective-permute-start | bytes 6291464 | tf_op jit(solution)/shard_map/ppermute | solution.py:15
  405.2 113.8 %collective-permute-start.9 = (f32[256,2048]{1,0:T(8,128)}, f32[256,2048]{1,0:T(8,128)}, u32[]{:S(2)}, u32[]{:S(2)}) collective-permute-start(f32[256,2048]{1,0:T(8,128)} %fusion.252), channel_id=1, source_target_pairs={{0,1},{1,0},{2,3},{3,2},{4,5},{5,4},{6,7},{7,6},{8,9},{9,8},{10,11... | collective-permute-start | bytes 6291464 | tf_op jit(solution)/shard_map/ppermute | solution.py:15
  466.1 97.7 %collective-permute-start.11 = (f32[256,2048]{1,0:T(8,128)}, f32[256,2048]{1,0:T(8,128)S(1)}, u32[]{:S(2)}, u32[]{:S(2)}) collective-permute-start(f32[256,2048]{1,0:T(8,128)} %fusion.256), channel_id=1, source_target_pairs={{0,1},{1,0},{2,3},{3,2},{4,5},{5,4},{6,7},{7,6},{8,9},{9,8},{10,11... | collective-permute-start | bytes 6291464 | tf_op jit(solution)/shard_map/ppermute | solution.py:15
  475.2 88.6 %copy-start.7 = (f32[256,2048]{1,0:T(8,128)S(1)}, f32[256,2048]{1,0:T(8,128)}, u32[]{:S(2)}) copy-start(f32[256,2048]{1,0:T(8,128)} %copy-done.6) | copy-start | bytes 6291460
  475.3 88.6 %copy-start.9 = (f32[256,2048]{1,0:T(8,128)S(1)}, f32[256,2048]{1,0:T(8,128)}, u32[]{:S(2)}) copy-start(f32[256,2048]{1,0:T(8,128)} %copy-done.8) | copy-start | bytes 6291460
  475.3 88.6 %copy-start.95 = (f32[256]{0:T(256)S(1)}, f32[256]{0:T(256)}, u32[]{:S(2)}) copy-start(f32[256]{0:T(256)} %copy-done.94) | copy-start | bytes 3076
  475.3 88.6 %copy-start.99 = (f32[256]{0:T(256)S(1)}, f32[256]{0:T(256)}, u32[]{:S(2)}) copy-start(f32[256]{0:T(256)} %copy-done.98) | copy-start | bytes 3076
  475.3 88.6 %copy-start.111 = (f32[256]{0:T(256)S(1)}, f32[256]{0:T(256)}, u32[]{:S(2)}) copy-start(f32[256]{0:T(256)} %copy-done.110) | copy-start | bytes 3076
  475.3 88.6 %copy-start.115 = (f32[256]{0:T(256)S(1)}, f32[256]{0:T(256)}, u32[]{:S(2)}) copy-start(f32[256]{0:T(256)} %copy-done.114) | copy-start | bytes 3076
  475.3 193.3 %collective-permute-start.7 = (f32[256,2048]{1,0:T(8,128)}, f32[256,2048]{1,0:T(8,128)}, u32[]{:S(2)}, u32[]{:S(2)}) collective-permute-start(f32[256,2048]{1,0:T(8,128)} %fusion.250), channel_id=1, source_target_pairs={{0,1},{1,0},{2,3},{3,2},{4,5},{5,4},{6,7},{7,6},{8,9},{9,8},{10,11... | collective-permute-start | bytes 6291464 | tf_op jit(solution)/shard_map/ppermute | solution.py:15
  477.1 174.8 %collective-permute-start.3 = (f32[256,2048]{1,0:T(8,128)S(1)}, f32[256,2048]{1,0:T(8,128)S(1)}, u32[]{:S(2)}, u32[]{:S(2)}) collective-permute-start(f32[256,2048]{1,0:T(8,128)S(1)} %fusion.246), channel_id=1, source_target_pairs={{0,1},{1,0},{2,3},{3,2},{4,5},{5,4},{6,7},{7,6},{8,9},{9,8},{10,11... | collective-permute-start | bytes 6291464 | tf_op jit(solution)/shard_map/ppermute | solution.py:15
  486.9 165.1 %slice-start.6 = ((s8[8388608]{0:T(1024)(128)(4,1)}), s8[4194304]{0:T(1024)(128)(4,1)S(1)}, s32[]{:S(2)}) async-start(s8[8388608]{0:T(1024)(128)(4,1)} %bitcast.282), calls=%async_computation.18 | async-start | bytes 8388608
  486.9 165.1 %slice-start.7 = ((s8[8388608]{0:T(1024)(128)(4,1)}), s8[4194304]{0:T(1024)(128)(4,1)S(1)}, s32[]{:S(2)}) async-start(s8[8388608]{0:T(1024)(128)(4,1)} %bitcast.282), calls=%async_computation.19 | async-start | bytes 8388608
  745.8 26.9 %collective-permute-start.22 = (f32[512,1024]{1,0:T(8,128)}, f32[512,1024]{1,0:T(8,128)}, u32[]{:S(2)}, u32[]{:S(2)}) collective-permute-start(f32[512,1024]{1,0:T(8,128)} %fusion.125), channel_id=1, source_target_pairs={{0,2},{2,0},{1,3},{3,1},{4,6},{6,4},{5,7},{7,5},{8,10},{10,8},{9,1... | collective-permute-start | bytes 6291464 | tf_op jit(solution)/shard_map/ppermute | solution.py:15
  772.3 69.4 %collective-permute-start.21 = (f32[512,1024]{1,0:T(8,128)}, f32[512,1024]{1,0:T(8,128)}, u32[]{:S(2)}, u32[]{:S(2)}) collective-permute-start(f32[512,1024]{1,0:T(8,128)} %fusion.134), channel_id=1, source_target_pairs={{0,2},{2,0},{1,3},{3,1},{4,6},{6,4},{5,7},{7,5},{8,10},{10,8},{9,1... | collective-permute-start | bytes 6291464 | tf_op jit(solution)/shard_map/ppermute | solution.py:15
  777.5 64.1 %collective-permute-start.23 = (f32[512,1024]{1,0:T(8,128)}, f32[512,1024]{1,0:T(8,128)}, u32[]{:S(2)}, u32[]{:S(2)}) collective-permute-start(f32[512,1024]{1,0:T(8,128)} %convolution_add_fusion.17), channel_id=1, source_target_pairs={{0,4},{4,0},{1,5},{5,1},{2,6},{6,2},{3,7},{7,3},{8,12},{12,8},{9,1... | collective-permute-start | bytes 6291464 | tf_op jit(solution)/shard_map/ppermute | solution.py:15
  786.8 163.4 %collective-permute-start.34 = (f32[512,4096]{1,0:T(8,128)}, f32[512,4096]{1,0:T(8,128)}, u32[]{:S(2)}, u32[]{:S(2)}) collective-permute-start(f32[512,4096]{1,0:T(8,128)} %fusion.107), channel_id=1, source_target_pairs={{0,2},{2,0},{1,3},{3,1},{4,6},{6,4},{5,7},{7,5},{8,10},{10,8},{9,1... | collective-permute-start | bytes 25165832 | tf_op jit(solution)/shard_map/ppermute | solution.py:15
  838.6 11.6 collective-permute-start.25
  846.1 820.7 %reduce-scatter.9.cloned.1.call-start = ((), (), s32[]{:S(2)}) async-start(), calls=%async_computation.7 | async-start | bytes 2621440 | tf_op jit(solution)/shard_map/reduce_scatter | solution.py:89
  846.1 16.7 slice-start
  846.2 16.7 slice-start.1
  850.2 26.3 %collective-permute-start.24 = (f32[512,1024]{1,0:T(8,128)}, f32[512,1024]{1,0:T(8,128)}, u32[]{:S(2)}, u32[]{:S(2)}) collective-permute-start(f32[512,1024]{1,0:T(8,128)} %fusion.132), channel_id=1, source_target_pairs={{0,2},{2,0},{1,3},{3,1},{4,6},{6,4},{5,7},{7,5},{8,10},{10,8},{9,1... | collective-permute-start | bytes 6291464 | tf_op jit(solution)/shard_map/ppermute | solution.py:15
  855.0 48.4 %collective-permute-start.26 = (f32[512,1024]{1,0:T(8,128)}, f32[512,1024]{1,0:T(8,128)}, u32[]{:S(2)}, u32[]{:S(2)}) collective-permute-start(f32[512,1024]{1,0:T(8,128)} %convolution_add_fusion.16), channel_id=1, source_target_pairs={{0,4},{4,0},{1,5},{5,1},{2,6},{6,2},{3,7},{7,3},{8,12},{12,8},{9,1... | collective-permute-start | bytes 6291464 | tf_op jit(solution)/shard_map/ppermute | solution.py:15
  873.9 46.6 %collective-permute-start.28 = (f32[512,1024]{1,0:T(8,128)}, f32[512,1024]{1,0:T(8,128)}, u32[]{:S(2)}, u32[]{:S(2)}) collective-permute-start(f32[512,1024]{1,0:T(8,128)} %fusion.121), channel_id=1, source_target_pairs={{0,2},{2,0},{1,3},{3,1},{4,6},{6,4},{5,7},{7,5},{8,10},{10,8},{9,1... | collective-permute-start | bytes 6291464 | tf_op jit(solution)/shard_map/ppermute | solution.py:15
  907.6 759.2 %reduce-scatter.11.cloned.1.call-start = ((), (), s32[]{:S(2)}) async-start(), calls=%async_computation.8 | async-start | bytes 2621440 | tf_op jit(solution)/shard_map/reduce_scatter | solution.py:89
  917.3 299.9 %collective-permute-start.33 = (f32[512,4096]{1,0:T(8,128)}, f32[512,4096]{1,0:T(8,128)}, u32[]{:S(2)}, u32[]{:S(2)}) collective-permute-start(f32[512,4096]{1,0:T(8,128)} %fusion.110), channel_id=1, source_target_pairs={{0,2},{2,0},{1,3},{3,1},{4,6},{6,4},{5,7},{7,5},{8,10},{10,8},{9,1... | collective-permute-start | bytes 25165832 | tf_op jit(solution)/shard_map/ppermute | solution.py:15
  920.0 41.9 %collective-permute-start.27 = (f32[512,1024]{1,0:T(8,128)}, f32[512,1024]{1,0:T(8,128)}, u32[]{:S(2)}, u32[]{:S(2)}) collective-permute-start(f32[512,1024]{1,0:T(8,128)} %fusion.130), channel_id=1, source_target_pairs={{0,2},{2,0},{1,3},{3,1},{4,6},{6,4},{5,7},{7,5},{8,10},{10,8},{9,1... | collective-permute-start | bytes 6291464 | tf_op jit(solution)/shard_map/ppermute | solution.py:15
  925.1 48.8 %collective-permute-start.29 = (f32[512,1024]{1,0:T(8,128)}, f32[512,1024]{1,0:T(8,128)}, u32[]{:S(2)}, u32[]{:S(2)}) collective-permute-start(f32[512,1024]{1,0:T(8,128)} %convolution_add_fusion.15), channel_id=1, source_target_pairs={{0,4},{4,0},{1,5},{5,1},{2,6},{6,2},{3,7},{7,3},{8,12},{12,8},{9,1... | collective-permute-start | bytes 6291464 | tf_op jit(solution)/shard_map/ppermute | solution.py:15
  947.5 35.6 %collective-permute-start.31 = (f32[1024,512]{1,0:T(8,128)}, f32[1024,512]{1,0:T(8,128)}, u32[]{:S(2)}, u32[]{:S(2)}) collective-permute-start(f32[1024,512]{1,0:T(8,128)} %fusion.114), channel_id=1, source_target_pairs={{0,2},{2,0},{1,3},{3,1},{4,6},{6,4},{5,7},{7,5},{8,10},{10,8},{9,1... | collective-permute-start | bytes 6291464 | tf_op jit(solution)/shard_map/ppermute | solution.py:15
  960.4 256.9 %collective-permute-start.35 = (f32[512,4096]{1,0:T(8,128)}, f32[512,4096]{1,0:T(8,128)}, u32[]{:S(2)}, u32[]{:S(2)}) collective-permute-start(f32[512,4096]{1,0:T(8,128)} %convolution_add_fusion), channel_id=1, source_target_pairs={{0,4},{4,0},{1,5},{5,1},{2,6},{6,2},{3,7},{7,3},{8,12},{12,8},{9,1... | collective-permute-start | bytes 25165832 | tf_op jit(solution)/shard_map/ppermute | solution.py:15
  978.4 688.5 %reduce-scatter.13.cloned.1.call-start = ((), (), s32[]{:S(2)}) async-start(), calls=%async_computation.9 | async-start | bytes 2621440 | tf_op jit(solution)/shard_map/reduce_scatter | solution.py:89
  983.1 19.2 %collective-permute-start.30 = (f32[1024,512]{1,0:T(8,128)}, f32[1024,512]{1,0:T(8,128)}, u32[]{:S(2)}, u32[]{:S(2)}) collective-permute-start(f32[1024,512]{1,0:T(8,128)} %fusion.117), channel_id=1, source_target_pairs={{0,2},{2,0},{1,3},{3,1},{4,6},{6,4},{5,7},{7,5},{8,10},{10,8},{9,1... | collective-permute-start | bytes 6291464 | tf_op jit(solution)/shard_map/ppermute | solution.py:15
  987.8 209.7 %collective-permute-start.32 = (f32[1024,512]{1,0:T(8,128)}, f32[1024,512]{1,0:T(8,128)}, u32[]{:S(2)}, u32[]{:S(2)}) collective-permute-start(f32[1024,512]{1,0:T(8,128)} %convolution_add_fusion.14), channel_id=1, source_target_pairs={{0,4},{4,0},{1,5},{5,1},{2,6},{6,2},{3,7},{7,3},{8,12},{12,8},{9,1... | collective-permute-start | bytes 6291464 | tf_op jit(solution)/shard_map/ppermute | solution.py:15
  1201.8 465.1 %reduce-scatter.15.cloned.1.call-start = ((), (), s32[]{:S(2)}) async-start(), calls=%async_computation.10 | async-start | bytes 10485760 | tf_op jit(solution)/shard_map/reduce_scatter | solution.py:89
  1211.4 26.1 %collective-permute-start.37 = (f32[4096,512]{1,0:T(8,128)}, f32[4096,512]{1,0:T(8,128)}, u32[]{:S(2)}, u32[]{:S(2)}) collective-permute-start(f32[4096,512]{1,0:T(8,128)} %fusion.100), channel_id=1, source_target_pairs={{0,2},{2,0},{1,3},{3,1},{4,6},{6,4},{5,7},{7,5},{8,10},{10,8},{9,1... | collective-permute-start | bytes 25165832 | tf_op jit(solution)/shard_map/ppermute | solution.py:15
  1227.3 439.6 %reduce-scatter.17.cloned.1.call-start = ((), (), s32[]{:S(2)}) async-start(), calls=%async_computation.11 | async-start | bytes 10485760 | tf_op jit(solution)/shard_map/reduce_scatter | solution.py:89
  1237.2 23.8 %collective-permute-start.36 = (f32[4096,512]{1,0:T(8,128)}, f32[4096,512]{1,0:T(8,128)S(1)}, u32[]{:S(2)}, u32[]{:S(2)}) collective-permute-start(f32[4096,512]{1,0:T(8,128)} %fusion.103), channel_id=1, source_target_pairs={{0,2},{2,0},{1,3},{3,1},{4,6},{6,4},{5,7},{7,5},{8,10},{10,8},{9,1... | collective-permute-start | bytes 25165832 | tf_op jit(solution)/shard_map/ppermute | solution.py:15
  1248.1 182.9 %collective-permute-start.38 = (f32[4096,512]{1,0:T(8,128)}, f32[4096,512]{1,0:T(8,128)}, u32[]{:S(2)}, u32[]{:S(2)}) collective-permute-start(f32[4096,512]{1,0:T(8,128)} %convolution_add_fusion.1), channel_id=1, source_target_pairs={{0,4},{4,0},{1,5},{5,1},{2,6},{6,2},{3,7},{7,3},{8,12},{12,8},{9,1... | collective-permute-start | bytes 25165832 | tf_op jit(solution)/shard_map/ppermute | solution.py:15
  1450.0 48.7 %collective-permute-start.12 = (f32[256,2048]{1,0:T(8,128)S(1)}, f32[256,2048]{1,0:T(8,128)}, u32[]{:S(2)}, u32[]{:S(2)}) collective-permute-start(f32[256,2048]{1,0:T(8,128)S(1)} %convolution_add_fusion.12), channel_id=1, source_target_pairs={{0,1},{1,0},{2,3},{3,2},{4,5},{5,4},{6,7},{7,6},{8,9},{9,8},{10,11... | collective-permute-start | bytes 6291464 | tf_op jit(solution)/shard_map/ppermute | solution.py:15
  1456.7 86.9 %collective-permute-start.13 = (f32[256,2048]{1,0:T(8,128)}, f32[256,2048]{1,0:T(8,128)}, u32[]{:S(2)}, u32[]{:S(2)}) collective-permute-start(f32[256,2048]{1,0:T(8,128)} %convolution_add_fusion.10), channel_id=1, source_target_pairs={{0,1},{1,0},{2,3},{3,2},{4,5},{5,4},{6,7},{7,6},{8,9},{9,8},{10,11... | collective-permute-start | bytes 6291464 | tf_op jit(solution)/shard_map/ppermute | solution.py:15
  1462.9 125.7 %collective-permute-start.14 = (f32[256,2048]{1,0:T(8,128)}, f32[256,2048]{1,0:T(8,128)}, u32[]{:S(2)}, u32[]{:S(2)}) collective-permute-start(f32[256,2048]{1,0:T(8,128)} %convolution_add_fusion.8), channel_id=1, source_target_pairs={{0,1},{1,0},{2,3},{3,2},{4,5},{5,4},{6,7},{7,6},{8,9},{9,8},{10,11... | collective-permute-start | bytes 6291464 | tf_op jit(solution)/shard_map/ppermute | solution.py:15
  1469.8 161.4 %collective-permute-start.15 = (f32[256,2048]{1,0:T(8,128)}, f32[256,2048]{1,0:T(8,128)}, u32[]{:S(2)}, u32[]{:S(2)}) collective-permute-start(f32[256,2048]{1,0:T(8,128)} %convolution_add_fusion.6), channel_id=1, source_target_pairs={{0,1},{1,0},{2,3},{3,2},{4,5},{5,4},{6,7},{7,6},{8,9},{9,8},{10,11... | collective-permute-start | bytes 6291464 | tf_op jit(solution)/shard_map/ppermute | solution.py:15
  1477.8 153.5 %copy-start.93 = (f32[2048]{0:T(1024)S(1)}, f32[2048]{0:T(1024)}, u32[]{:S(2)}) copy-start(f32[2048]{0:T(1024)} %param.32) | copy-start | bytes 24580
  1643.4 6.3 collective-permute-start.16
  1650.0 1.3 collective-permute-start.17
  1651.3 3.8 collective-permute-start.18
  1655.2 4.9 collective-permute-start.19
  1660.1 3.9 collective-permute-start.20
  (139 other events, 914.7 us)
Sparse Core Ops, SparseCore 0:
  846.2 43.9 reduce-scatter.6
  907.7 43.9 reduce-scatter.8
  978.5 43.9 reduce-scatter.10
  1201.9 44.0 reduce-scatter.12
  1248.8 143.8 reduce-scatter.14
  1440.8 144.7 reduce-scatter.16

commit v2 on v1

--- a/solution.py
+++ b/solution.py
@@ -32,6 +32,10 @@
     first = jnp.mean(scaled, -1, keepdims=True)
     second = jnp.mean(scaled * unit, -1, keepdims=True)
     return scale * (scaled - first - unit * second)
+
+
+def after(value, *others):
+    return lax.optimization_barrier((value,) + others)[0]
 
 
 def exact_gelu(field):
@@ -63,8 +67,8 @@
     zs, xs, cs = lax.axis_size("z"), lax.axis_size("x"), lax.axis_size("c")
     dps = zs * xs * cs
     at_x, at_c = lax.axis_index("x"), lax.axis_index("c")
-    here, over_x = at_x * 2 + at_c, (1 - at_x) * 2 + at_c
-    over_c, over_xc = at_x * 2 + 1 - at_c, (1 - at_x) * 2 + 1 - at_c
+    wide = width // dps
+    part = zs * wide
     block_rows = min(512, length)
     block_count = length // block_rows
     chunk = length // CHUNKS
@@ -72,21 +76,40 @@
     boundary = prefix_len[0]
 
     def pieces(field):
-        parts = field.reshape(length, zs, xs * cs, width // dps)
-        return jnp.transpose(parts, (2, 0, 1, 3)).reshape(xs * cs, length, width // (xs * cs))
-
-    def reduce_weight(parts, other, by_rows):
-        def part(index):
-            piece = lax.dynamic_index_in_dim(parts, index, 0, keepdims=False)
-            if by_rows:
+        order = [(z * xs + x) * cs + c for c in range(cs) for x in range(xs) for z in range(zs)]
+        return jnp.concatenate([field[:, at * wide : (at + 1) * wide] for at in order], 1)
+
+    class Sum:
+        def __init__(self, parts, other, by_rows):
+            self.parts, self.other, self.by_rows = parts, other, by_rows
+            self.dim = 0 if by_rows else 1
+
+        def product(self, begin, size, gate):
+            piece = lax.dynamic_slice_in_dim(self.parts, begin, size, 1)
+            other = after(self.other, *gate)
+            if self.by_rows:
                 return mm(piece, other, ((0,), (0,)))
             return mm(other, piece, ((0,), (0,)))
 
-        far = swap(part(over_xc), "c")
-        near = swap(part(over_c), "c")
-        across = swap(part(over_x) + far, "x")
-        total = part(here) + near + across
-        return lax.psum_scatter(total, "z", scatter_dimension=0 if by_rows else 1, tiled=True)
+        def arrived(self, x):
+            return lax.dynamic_slice_in_dim(self.near, x * part, part, self.dim)
+
+        def over_cores(self, *gate):
+            own = self.product((1 - at_c) * xs * part, xs * part, gate)
+            self.near = swap(own, "c")
+            return own
+
+        def over_x(self, *gate):
+            far = 1 - at_x
+            own = self.product((at_c * xs + far) * part, part, gate) + self.arrived(far)
+            self.across = swap(own, "x")
+            return own
+
+        def over_z(self, *gate):
+            own = self.product((at_c * xs + at_x) * part, part, gate) + self.arrived(at_x)
+            total = own + self.across
+            self.result = lax.psum_scatter(total, "z", scatter_dimension=self.dim, tiled=True)
+            return total
 
     features = inputs.astype(F32)
     unit1, scale1 = norm_parts(features)
@@ -135,10 +158,13 @@
     attn_others = [swap(part, "mp") for part in attn_parts]
 
     resids, units2, scales2, normeds2, acts, hidden_grads = [], [], [], [], [], []
-    norm2_parts, branch_parts, up_bias_grad = [], [], 0.0
+    norm2_parts, up_bias_grad = [], 0.0
     for index in range(CHUNKS):
         rows = slice(index * chunk, (index + 1) * chunk)
-        resid = features[rows] + ((attn_parts[index] + attn_others[index]) + out_bias)
+        attn_other = attn_others[index]
+        if index > 0:
+            attn_other = after(attn_other, norm2_parts[index - 1], hidden_grads[index - 1])
+        resid = features[rows] + ((attn_parts[index] + attn_other) + out_bias)
         unit2, scale2 = norm_parts(resid)
         normed2 = (unit2 * norm2_gain + norm2_bias).astype(BF16)
         hidden = mm(normed2, up_weight, ((1,), (0,))) + up_bias.reshape(-1)
@@ -148,30 +174,33 @@
         hidden_grad = gelu_pull(acts_grad)[0].astype(BF16)
         up_bias_grad = up_bias_grad + jnp.sum(hidden_grad.astype(F32), 0)
         norm2_parts.append(mm(hidden_grad, up_weight, ((1,), (1,))))
-        branch_parts.append(mm(act, down_weight, ((1,), (0,))))
         resids.append(resid)
         units2.append(unit2)
         scales2.append(scale2)
         normeds2.append(normed2)
         acts.append(act)
         hidden_grads.append(hidden_grad)
-    norm2_others = [swap(part, "mp") for part in norm2_parts]
-    branch_others = [swap(part, "mp") for part in branch_parts]
-
-    acts = jnp.concatenate(acts, 0)
-    hidden_grads = jnp.concatenate(hidden_grads, 0)
-    normed2 = jnp.concatenate(normeds2, 0)
-    down_weight_grad = reduce_weight(pieces(out_grad), acts, False)
-    up_weight_grad = reduce_weight(pieces(normed2), hidden_grads, True)
+    norm2_others = [swap(piece, "mp") for piece in norm2_parts]
 
     grad_float = out_grad.astype(F32)
     down_bias_grad = jnp.sum(grad_float, 0)
+    half = up_weight.shape[1] // 2
+    halves = [slice(0, half), slice(half, 2 * half)]
+    grad_pieces = pieces(out_grad)
+    normed2_pieces = pieces(jnp.concatenate(normeds2, 0))
+    downs = [Sum(grad_pieces, jnp.concatenate([act[:, cut] for act in acts], 0), False) for cut in halves]
+    ups = [
+        Sum(normed2_pieces, jnp.concatenate([pull[:, cut] for pull in hidden_grads], 0), True)
+        for cut in halves
+    ]
 
     resid_grads, attn_grads, mixed_grads = [], [], []
     norm2_gain_grad, norm2_bias_grad, out_bias_grad = 0.0, 0.0, 0.0
-    for index in range(CHUNKS):
+
+    def norm2_pull(index, *gate):
+        nonlocal norm2_gain_grad, norm2_bias_grad, out_bias_grad
         rows = slice(index * chunk, (index + 1) * chunk)
-        norm2_in = norm2_parts[index] + norm2_others[index]
+        norm2_in = norm2_parts[index] + after(norm2_others[index], *gate)
         norm2_bias_grad = norm2_bias_grad + jnp.sum(norm2_in, 0)
         norm2_gain_grad = norm2_gain_grad + jnp.sum(norm2_in * units2[index], 0)
         resid_grad = grad_float[rows] + norm_pull(norm2_in, units2[index], scales2[index], norm2_gain)
@@ -180,9 +209,28 @@
         mixed_grads.append(mm(attn_grad, out_weight, ((1,), (1,))).astype(BF16))
         resid_grads.append(resid_grad)
         attn_grads.append(attn_grad)
+        return mixed_grads[-1]
+
+    def branch_part(index, *gate):
+        return mm(after(acts[index], *gate), down_weight, ((1,), (0,)))
+
+    gate = downs[0].over_cores(norm2_parts[-1], hidden_grads[-1], norm2_others[0])
+    gate = norm2_pull(0, gate)
+    gate = downs[0].over_x(gate)
+    gate = downs[1].over_cores(gate, downs[0].near)
+    gate = norm2_pull(1, gate)
+    gate = downs[1].over_x(gate)
+    gate = ups[0].over_cores(gate, downs[1].near)
+    branch_parts = [branch_part(0, gate)]
+    gate = norm2_pull(2, branch_parts[0], ups[0].near)
+    branch_parts += [branch_part(index, gate) for index in range(1, CHUNKS)]
+    gate = norm2_pull(3, *branch_parts)
+    gate = downs[0].over_z(gate)
+    branch = jnp.concatenate(branch_parts, 0)
+    branch_other = swap(after(branch, norm2_others[-1]), "mp")
+    gate = ups[0].over_x(gate)
     mixed_grad = jnp.concatenate(mixed_grads, 0).reshape(length, heads_local, head_dim)
     attn_grad = jnp.concatenate(attn_grads, 0)
-    out_weight_grad = reduce_weight(pieces(attn_grad), mixed, False)
 
     query_blocks = []
     key_accum = jnp.zeros((length, heads_local, head_dim), F32)
@@ -192,7 +240,7 @@
         seen = max(row_begin + block_rows, length // 2)
         query_block, scores = block_scores(row_begin, seen)
         probs = jnp.exp(scores - totals_log[block_index])
-        mixed_block = mixed_grad[row_begin : row_begin + block_rows]
+        mixed_block = after(mixed_grad[row_begin : row_begin + block_rows], gate)
         prob_grad = jnp.einsum(
             "qhd,khd->hqk", mixed_block, values[:seen], preferred_element_type=F32
         )
@@ -207,6 +255,10 @@
         value_accum = value_accum.at[:seen].add(
             jnp.einsum("hqk,qhd->khd", probs.astype(BF16), mixed_block, preferred_element_type=F32)
         )
+        if block_index == 0:
+            gate = ups[1].over_cores(query_blocks[0], key_accum, value_accum)
+            gate = downs[1].over_z(gate, ups[1].near)
+            gate = ups[1].over_x(gate)
     flat = (length, heads_local * head_dim)
     query_grad = jnp.concatenate(query_blocks, 0).astype(BF16).reshape(flat)
     key_grad = key_accum.astype(BF16).reshape(flat)
@@ -214,31 +266,60 @@
     query_bias_grad = jnp.sum(query_grad.astype(F32), 0)
     value_bias_grad = jnp.sum(value_grad.astype(F32), 0)
 
+    half_rows = length // 2
     norm1_parts = []
+    for begin in range(0, length, half_rows):
+        rows = slice(begin, begin + half_rows)
+        piece = mm(query_grad[rows], query_weight, ((1,), (1,)))
+        piece = piece + mm(key_grad[rows], key_weight, ((1,), (1,)))
+        piece = piece + mm(value_grad[rows], value_weight, ((1,), (1,)))
+        norm1_parts.append(piece)
+    norm1_others = [swap(piece, "mp") for piece in norm1_parts]
+
+    normed_pieces = pieces(normed)
+    out_sum = Sum(pieces(attn_grad), mixed, False)
+    query_sum, key_sum, value_sum = [
+        Sum(normed_pieces, pull, True) for pull in (query_grad, key_grad, value_grad)
+    ]
+    gate = out_sum.over_cores(*norm1_parts)
+    gate = ups[0].over_z(gate, branch_other)
+    gate = out_sum.over_x(gate)
+    outputs = (jnp.concatenate(resids, 0) + ((branch + after(branch_other, gate)) + down_bias)).astype(BF16)
+    gate = query_sum.over_cores(outputs)
+    gate = ups[1].over_z(gate, query_sum.near)
+    gate = query_sum.over_x(gate)
+    gate = key_sum.over_cores(gate)
+
     norm1_gain_grad, norm1_bias_grad = 0.0, 0.0
-    for index in range(CHUNKS):
-        rows = slice(index * chunk, (index + 1) * chunk)
-        part = mm(query_grad[rows], query_weight, ((1,), (1,)))
-        part = part + mm(key_grad[rows], key_weight, ((1,), (1,)))
-        part = part + mm(value_grad[rows], value_weight, ((1,), (1,)))
-        norm1_parts.append(part)
-        norm1_bias_grad = norm1_bias_grad + jnp.sum(part, 0)
-        norm1_gain_grad = norm1_gain_grad + jnp.sum(part * unit1[rows], 0)
-    norm1_others = [swap(part, "mp") for part in norm1_parts]
-
-    normed_pieces = pieces(normed)
-    query_weight_grad = reduce_weight(normed_pieces, query_grad, True)
-    key_weight_grad = reduce_weight(normed_pieces, key_grad, True)
-    value_weight_grad = reduce_weight(normed_pieces, value_grad, True)
+    in_grads = []
+
+    def norm1_pull(index, gate):
+        nonlocal norm1_gain_grad, norm1_bias_grad
+        rows = slice(index * half_rows, (index + 1) * half_rows)
+        norm1_in = norm1_parts[index] + after(norm1_others[index], gate)
+        norm1_bias_grad = norm1_bias_grad + jnp.sum(norm1_in, 0)
+        norm1_gain_grad = norm1_gain_grad + jnp.sum(norm1_in * unit1[rows], 0)
+        pulled = norm_pull(norm1_in, unit1[rows], scale1[rows], norm1_gain)
+        resid_grad = jnp.concatenate(resid_grads[index * 2 : index * 2 + 2], 0)
+        in_grads.append((resid_grad + pulled).astype(BF16))
+        return in_grads[-1]
+
+    gate = norm1_pull(0, gate)
+    gate = out_sum.over_z(gate, key_sum.near)
+    gate = key_sum.over_x(gate)
+    gate = value_sum.over_cores(gate)
+    gate = query_sum.over_z(gate, value_sum.near)
+    gate = value_sum.over_x(gate)
+    gate = norm1_pull(1, gate)
+    in_grad = jnp.concatenate(in_grads, 0)
 
     def blocks(vector, lead):
         return jnp.transpose(vector.reshape(lead, dps, -1), (1, 0, 2)).reshape(dps, -1)
 
-    shared = jnp.concatenate([blocks(norm1_gain_grad, 1), blocks(norm1_bias_grad, 1)], 1)
-    shared = shared + swap(shared, "mp")
     small = jnp.concatenate(
         [
-            shared,
+            blocks(norm1_gain_grad, 1),
+            blocks(norm1_bias_grad, 1),
             blocks(query_bias_grad, heads_local),
             blocks(value_bias_grad, heads_local),
             blocks(out_bias_grad, 1),
@@ -249,37 +330,32 @@
         ],
         1,
     )
-    small = small.reshape(zs, xs * cs, -1)
-
-    def take(field, index, axis):
-        return lax.dynamic_index_in_dim(field, index, axis, keepdims=False)
-
-    far = swap(jnp.stack([take(small, over_xc, 1), take(small, over_c, 1)]), "c")
-    across = swap(take(small, over_x, 1) + far[0], "x")
-    small = take(small, here, 1) + far[1] + across
+    small = small.reshape(zs, xs, cs, -1)
+
+    def fold(field, axis, at, dim):
+        def take(index):
+            return lax.dynamic_index_in_dim(field, index, dim, keepdims=False)
+
+        return take(at) + swap(take(1 - at), axis)
+
+    small = fold(small, "c", at_c, 2)
+    small = fold(small, "x", at_x, 1)
     at_z, span = lax.axis_index("z"), zs
     while span > 1:
         span //= 2
-        halves = small.reshape(2, span, -1)
+        halved = small.reshape(2, span, -1)
         side = (at_z // span) % 2
         pairs = [(i, i ^ span) for i in range(zs)]
-        other = lax.ppermute(take(halves, 1 - side, 0), "z", pairs)
-        small = take(halves, side, 0) + other
+        mine = lax.dynamic_index_in_dim(halved, side, 0, keepdims=False)
+        other = lax.dynamic_index_in_dim(halved, 1 - side, 0, keepdims=False)
+        small = mine + lax.ppermute(other, "z", pairs)
     small = small.reshape(-1)
 
-    in_grads, outputs = [], []
-    for index in range(CHUNKS):
-        rows = slice(index * chunk, (index + 1) * chunk)
-        outputs.append(
-            (resids[index] + ((branch_parts[index] + branch_others[index]) + down_bias)).astype(BF16)
-        )
-        norm1_in = norm1_parts[index] + norm1_others[index]
-        pulled = norm_pull(norm1_in, unit1[rows], scale1[rows], norm1_gain)
-        in_grads.append((resid_grads[index] + pulled).astype(BF16))
-    outputs = jnp.concatenate(outputs, 0)
-    in_grad = jnp.concatenate(in_grads, 0)
-
-    wide = width // dps
+    gate = key_sum.over_z(gate)
+    gate = value_sum.over_z(gate)
+    down_weight_grad = jnp.concatenate([item.result for item in downs], 0)
+    up_weight_grad = jnp.concatenate([item.result for item in ups], 1)
+
     thin = head_dim // dps
     sizes = [wide, wide, heads_local * thin, heads_local * thin, wide, wide, wide]
     sizes += [up_bias.shape[0] * thin, wide]
@@ -293,12 +369,12 @@
         in_grad,
         gain1,
         bias1,
-        query_weight_grad,
+        query_sum.result,
         query_b.reshape(heads_local, thin),
-        key_weight_grad,
-        value_weight_grad,
+        key_sum.result,
+        value_sum.result,
         value_b.reshape(heads_local, thin),
-        out_weight_grad,
+        out_sum.result,
         out_b,
         gain2,
         bias2,

time: 1690 us -> 1290 us (0.76)
  waiting for transfers between devices: 844 us -> 388 us
  other arithmetic: 143 us -> 165 us
  matrix products: 555 us -> 574 us
  local copies, waits for them, and re-layouts: 83.3 us -> 101 us
    ppermute x37 -> x29, waiting for transfers between devices: 844 us -> 361 us  [swap(): return lax.ppermute(value, axis, [(0, 1), (1, 0)])]
    unnamed x320 -> x421, local copies, waits for them, and re-layouts: 20.6 us -> 78.9 us
    reshape x7 -> x1, local copies, waits for them, and re-layouts: 45.7 us -> 0.02 us  [body(): halved = small.reshape(2, span, -1)]
    reduce_scatter x6 -> x8, waiting for transfers between devices: 0.08 us -> 26.5 us  [over_z(): lax.psum_scatter(total, 'z', scatter_dimension=self.dim, tiled=True)]
    dot_general x63 -> x57, matrix products: 415 us -> 432 us  [mm(): lax.dot_general(left, right, (contract, ((), ())), preferred_element_type...]
    reduce_sum x5 -> x10, other arithmetic: 38.4 us -> 30.6 us  [the longest x4 12.1 us: norm2_pull(): norm2_gain_grad = norm2_gain_grad + jnp.sum(norm2_in * units2[index], 0)]
    add x16 -> x17, other arithmetic: 37.1 us -> 38.8 us  [the longest x8 38 us: over_z(): total = own + self.across]
  transfers between devices with their start and end apart: 45 -> 39, of which waited for: 16 -> 13; matrix products, arithmetic and copies ran while one was open for 36% -> 56% of each run, Pallas kernels for 0% -> 0%
where the time goes in v2:
time: 1290 us; the launch traced here: 1280 us
  matrix products  574 us (44%)
  waiting for transfers between devices  388 us (30%)
  other arithmetic  165 us (13%)
  local copies, waits for them, and re-layouts  101 us (8%)
  starting transfers between devices  31 us (2%)
  between operations  17.7 us (1%)
    dot_general x57, matrix products, mm(): lax.dot_general(left, right, (contract, ((), ())), preferred_element_type...  432 us
    ppermute x29, waiting for transfers between devices, swap(): return lax.ppermute(value, axis, [(0, 1), (1, 0)])  361 us
    unnamed x421, local copies, waits for them, and re-layouts  78.9 us
    dot_general x2, matrix products, body(): jnp.einsum('hqk,khd->qhd', score_grad, keys[:seen], preferred_element_typ...  51.3 us
    dot_general x2, matrix products, body(): jnp.einsum('hqk,qhd->khd', score_grad, query_block, preferred_element_typ...  47.1 us
    add x8, other arithmetic, over_z(): total = own + self.across  38 us
    reduce_scatter x8, waiting for transfers between devices, over_z(): lax.psum_scatter(total, 'z', scatter_dimension=self.dim, tiled=True)  26.5 us
    ppermute x29, starting transfers between devices, swap(): return lax.ppermute(value, axis, [(0, 1), (1, 0)])  26.4 us
  transfers between devices with their start and end apart: 39, of which 13 were waited for; matrix products, arithmetic and copies ran while one was open for 56% of the time, Pallas kernels for 0%

profile of v2, /device:TPU:0, one launch (start us, length us, event | category | flops | bytes accessed | tf_op | source)
XLA Modules:
  0.0 1277.0 jit_solution(7097783544731719909)
XLA Ops:
  17.1 4.9 convolution_convert_fusion
  22.2 8.0 add_convert_fusion.6
  30.4 4.9 add_convert_fusion.5
  61.9 5.7 fusion.114
  67.8 5.2 fusion.231
  114.4 18.3 %multiply_convert_fusion.5 = (bf16[256,4096]{1,0:T(8,128)(2,1)}, f32[256,4096]{1,0:T(8,128)S(1)}) fusion(f32[4096]{0:T(1024)S(1)} %bitcast.246, bf16[256,2048]{1,0:T(8,128)(2,1)S(1)} %add_convert_fusion.10, bf16[2048,4096]{1,0:T(8,128)(2,1)} %param.43), kind=kOutput, calls=%fused_computation.105 | convolution fusion | flops 4364173312 | bytes 24133632 | tf_op jit(solution)/shard_map/dot_general | solution.py:19
  132.7 18.6 %convert_reduce_fusion.4 = (f32[4096]{0:T(1024)}, bf16[256,4096]{1,0:T(8,128)(2,1)S(1)}) fusion(f32[256,4096]{1,0:T(8,128)S(1)} %get-tuple-element.279, bf16[4096,2048]{1,0:T(8,128)(2,1)} %param.45, bf16[1024,2048]{1,0:T(8,128)(2,1)} %param.47), kind=kOutput, calls=%fused_computation.69 | convolution fusion | flops 4372557824 | bytes 24133632 | tf_op jit(solution)/shard_map/dot_general | solution.py:19
  151.3 10.2 fusion.230
  168.6 18.3 %multiply_convert_fusion.4 = (bf16[256,4096]{1,0:T(8,128)(2,1)}, f32[256,4096]{1,0:T(8,128)S(1)}) fusion(f32[4096]{0:T(1024)S(1)} %bitcast.247, bf16[256,2048]{1,0:T(8,128)(2,1)S(1)} %add_convert_fusion.9, bf16[2048,4096]{1,0:T(8,128)(2,1)} %param.43), kind=kOutput, calls=%fused_computation.91 | convolution fusion | flops 4364173312 | bytes 24133632 | tf_op jit(solution)/shard_map/dot_general | solution.py:19
  186.9 18.4 %convert_reduce_fusion.3 = (f32[4096]{0:T(1024)}, bf16[256,4096]{1,0:T(8,128)(2,1)S(1)}) fusion(f32[256,4096]{1,0:T(8,128)S(1)} %get-tuple-element.283, bf16[4096,2048]{1,0:T(8,128)(2,1)} %param.45, bf16[1024,2048]{1,0:T(8,128)(2,1)} %param.47), kind=kOutput, calls=%fused_computation.68 | convolution fusion | flops 4372557824 | bytes 24133632 | tf_op jit(solution)/shard_map/dot_general | solution.py:19
  205.3 10.2 fusion.232
  220.6 18.3 %multiply_convert_fusion.3 = (bf16[256,4096]{1,0:T(8,128)(2,1)}, f32[256,4096]{1,0:T(8,128)S(1)}) fusion(f32[4096]{0:T(1024)S(1)} %bitcast.248, bf16[256,2048]{1,0:T(8,128)(2,1)S(1)} %add_convert_fusion.8, bf16[2048,4096]{1,0:T(8,128)(2,1)} %param.43), kind=kOutput, calls=%fused_computation.90 | convolution fusion | flops 4364173312 | bytes 24133632 | tf_op jit(solution)/shard_map/dot_general | solution.py:19
  238.9 18.6 %convert_reduce_fusion.2 = (f32[4096]{0:T(1024)}, bf16[256,4096]{1,0:T(8,128)(2,1)S(1)}) fusion(f32[256,4096]{1,0:T(8,128)S(1)} %get-tuple-element.281, bf16[4096,2048]{1,0:T(8,128)(2,1)} %param.45, bf16[1024,2048]{1,0:T(8,128)(2,1)} %param.47), kind=kOutput, calls=%fused_computation.67 | convolution fusion | flops 4372557824 | bytes 24133632 | tf_op jit(solution)/shard_map/dot_general | solution.py:19
  257.4 10.3 fusion.234
  272.7 18.4 %multiply_convert_fusion.2 = (bf16[256,4096]{1,0:T(8,128)(2,1)S(1)}, f32[256,4096]{1,0:T(8,128)}) fusion(f32[4096]{0:T(1024)S(1)} %bitcast.249, bf16[256,2048]{1,0:T(8,128)(2,1)S(1)} %add_convert_fusion.7, bf16[2048,4096]{1,0:T(8,128)(2,1)} %param.43), kind=kOutput, calls=%fused_computation.89 | convolution fusion | flops 4364173312 | bytes 24133632 | tf_op jit(solution)/shard_map/dot_general | solution.py:19
  291.1 20.9 %convert_reduce_fusion.1 = (f32[4096]{0:T(1024)}, bf16[256,4096]{1,0:T(8,128)(2,1)}) fusion(f32[256,4096]{1,0:T(8,128)} %get-tuple-element.277, bf16[4096,2048]{1,0:T(8,128)(2,1)} %param.45, bf16[1024,2048]{1,0:T(8,128)(2,1)} %param.47), kind=kOutput, calls=%fused_computation.66 | convolution fusion | flops 4372557824 | bytes 24133632 | tf_op jit(solution)/shard_map/dot_general | solution.py:19
  318.3 12.3 fusion.235
  330.6 10.7 fusion.93
  341.3 6.5 convert_element_type.179
  347.8 5.7 pad_maximum_fusion.3
  353.5 5.5 multiply_reduce_fusion.12
  365.3 7.0 dynamic-slice_add_fusion.3
  372.3 8.6 fusion.91
  390.1 6.1 collective-permute-done.4
  407.1 6.8 dynamic-slice_add_fusion.2
  413.9 7.0 fusion.97
  429.3 9.1 fusion.236
  438.5 31.2 %collective-permute-done.8 = f32[256,2048]{1,0:T(8,128)S(1)} collective-permute-done((f32[256,2048]{1,0:T(8,128)}, f32[256,2048]{1,0:T(8,128)S(1)}, u32[]{:S(2)}, u32[]{:S(2)}) %collective-permute-start.8) | collective-permute-done | bytes 2097184 | tf_op jit(solution)/shard_map/ppermute | solution.py:15
  477.3 9.7 fusion.239
  487.0 9.6 fusion.238
  496.7 9.7 fusion.237
  506.4 7.7 collective-permute-done.10
  525.2 5.9 add_add_fusion.5
  531.1 8.2 dynamic-slice_add_fusion.1
  541.8 5.9 fusion.240
  547.7 13.8 %fusion.102 = bf16[512,8,128]{0,2,1:T(8,128)(2,1)S(1)} fusion(bf16[512,8,128]{0,2,1:T(8,128)(2,1)} %bitcast.219, f32[8,512,512]{1,2,0:T(8,128)} %fusion.240, f32[8,512,512]{1,2,0:T(8,128)} %copy-done.11, f32[8,512]{1,0:T(8,128)S(1)} %log_add_fusion.1, pred[512,512]{0,1:T(8,128)(4,1)S(1)} %copy-done.70), kind=kOutput, calls=%fused_computation.226 | convolution fusion | flops 559944192 | bytes 19152896 | tf_op jit(solution)/shard_map/hqk,khd->qhd/dot_general | solution.py:250
  561.6 11.2 fusion.95
  586.2 5.2 pad_maximum_fusion
  605.7 15.2 %fusion.105 = f32[512,8,128]{0,2,1:T(8,128)} fusion(bf16[512,8,128]{0,2,1:T(8,128)(2,1)S(1)} %bitcast.221, f32[8,512,512]{1,2,0:T(8,128)} %fusion.240, f32[8,512,512]{1,2,0:T(8,128)} %copy-done.11, f32[8,512]{1,0:T(8,128)S(1)} %log_add_fusion.1, pred[512,512]{0,1:T(8,128)(4,1)S(1)} %copy-done.70), kind=kOutput, calls=%fused_computation.227 | convolution fusion | flops 559944192 | bytes 20201472 | tf_op jit(solution)/shard_map/hqk,qhd->khd/dot_general | solution.py:253
  620.9 6.7 fusion.241
  627.6 7.2 fusion.99
  638.7 36.6 %collective-permute-done.14 = f32[2048,512]{1,0:T(8,128)} collective-permute-done((f32[2048,512]{1,0:T(8,128)}, f32[2048,512]{1,0:T(8,128)}, u32[]{:S(2)}, u32[]{:S(2)}) %collective-permute-start.14) | collective-permute-done | bytes 4194336 | tf_op jit(solution)/shard_map/ppermute | solution.py:15
  675.3 5.9 add_add_fusion.4
  681.3 8.2 dynamic-slice_add_fusion
  691.4 8.2 fusion.242
  699.6 31.9 %fusion.42 = bf16[1024,8,128]{0,2,1:T(8,128)(2,1)} fusion(bf16[512,8,128]{0,2,1:T(8,128)(2,1)} %bitcast.205, f32[8,512,1024]{2,1,0:T(8,128)} %fusion.242, f32[8,512,1024]{2,1,0:T(8,128)} %copy-done, f32[8,512]{1,0:T(8,128)S(1)} %log_add_fusion, f32[512,8,128]{0,2,1:T(8,128)} %fusion.105), kind=kOutput, calls=%fused_computation.65 | convolution fusion | flops 1105204224 | bytes 38813696 | tf_op jit(solution)/shard_map/hqk,qhd->khd/dot_general | solution.py:253
  731.5 8.2 convert_reduce_fusion.5
  744.2 37.5 %fusion.115 = bf16[8,128,512]{2,1,0:T(8,128)(2,1)S(1)} fusion(bf16[1024,8,128]{0,2,1:T(8,128)(2,1)S(1)} %bitcast.201, f32[8,512,1024]{2,1,0:T(8,128)} %fusion.242, f32[8,512,1024]{2,1,0:T(8,128)} %copy-done, f32[8,512]{1,0:T(8,128)S(1)} %log_add_fusion), kind=kOutput, calls=%fused_computation.235 | convolution fusion | flops 1103631360 | bytes 36716544 | tf_op jit(solution)/shard_map/hqk,khd->qhd/dot_general | solution.py:250
  781.7 5.3 fusion.243
  797.6 4.9 add_add_fusion.2
  802.5 6.2 fusion.88
  819.8 6.9 add_add_fusion.1
  838.4 11.5 fusion.9
  856.8 5.2 collective-permute-done.18
  866.5 81.3 %collective-permute-done.19 = f32[512,2048]{1,0:T(8,128)S(1)} collective-permute-done((f32[512,2048]{1,0:T(8,128)S(1)}, f32[512,2048]{1,0:T(8,128)S(1)}, u32[]{:S(2)}, u32[]{:S(2)}) %collective-permute-start.19) | collective-permute-done | bytes 4194336 | tf_op jit(solution)/shard_map/ppermute | solution.py:15
  947.8 5.6 add_add_fusion
  954.5 5.6 dynamic-slice_add_fusion.6
  964.4 81.1 %collective-permute-done.17 = f32[512,2048]{1,0:T(8,128)S(1)} collective-permute-done((f32[512,2048]{1,0:T(8,128)}, f32[512,2048]{1,0:T(8,128)S(1)}, u32[]{:S(2)}, u32[]{:S(2)}) %collective-permute-start.17) | collective-permute-done | bytes 4194336 | tf_op jit(solution)/shard_map/ppermute | solution.py:15
  1056.0 5.3 dynamic-slice_add_fusion.5
  1076.4 38.4 %collective-permute-done.24 = f32[512,1024]{1,0:T(8,128)S(1)} collective-permute-done((f32[512,1024]{1,0:T(8,128)}, f32[512,1024]{1,0:T(8,128)S(1)}, u32[]{:S(2)}, u32[]{:S(2)}) %collective-permute-start.24) | collective-permute-done | bytes 2097184 | tf_op jit(solution)/shard_map/ppermute | solution.py:15
  1118.6 5.3 dynamic-slice_add_fusion.4
  1123.9 35.2 %collective-permute-done.20 = f32[512,2048]{1,0:T(8,128)} collective-permute-done((f32[512,2048]{1,0:T(8,128)}, f32[512,2048]{1,0:T(8,128)}, u32[]{:S(2)}, u32[]{:S(2)}) %collective-permute-start.20) | collective-permute-done | bytes 4194336 | tf_op jit(solution)/shard_map/ppermute | solution.py:15
  1186.9 33.9 %collective-permute-done.30 = f32[512,1024]{1,0:T(8,128)} collective-permute-done((f32[512,1024]{1,0:T(8,128)}, f32[512,1024]{1,0:T(8,128)}, u32[]{:S(2)}, u32[]{:S(2)}) %collective-permute-start.30) | collective-permute-done | bytes 2097184 | tf_op jit(solution)/shard_map/ppermute | solution.py:15
  1243.2 26.5 %reduce-scatter.13.cloned.1.call-done = f32[128,1024]{1,0:T(8,128)} async-done(((f32[512,1024]{1,0:T(8,128)}), f32[128,1024]{1,0:T(8,128)}) %reduce-scatter.13.cloned.1.call-update) | async-done | bytes 524304 | tf_op jit(solution)/shard_map/reduce_scatter | solution.py:111
  (652 shorter events, 322.8 us)
Async XLA Ops:
  7.2 1219.7 %reduce-scatter.21.cloned.1.call-start = ((), (), s32[]{:S(2)}) async-start(), calls=%async_computation.14 | async-start | bytes 5242880 | tf_op jit(solution)/shard_map/reduce_scatter | solution.py:111
  12.8 26.3 %copy-start.69 = (pred[512,512]{0,1:T(8,128)(4,1)}, pred[512,512]{0,1:T(8,128)(4,1)S(1)}, u32[]{:S(2)}) copy-start(pred[512,512]{0,1:T(8,128)(4,1)S(1)} %fusion.138) | copy-start | bytes 786436
  46.2 63.1 %collective-permute-start = (f32[256,2048]{1,0:T(8,128)}, f32[256,2048]{1,0:T(8,128)}, u32[]{:S(2)}, u32[]{:S(2)}) collective-permute-start(f32[256,2048]{1,0:T(8,128)} %fusion.228), channel_id=1, source_target_pairs={{0,1},{1,0},{2,3},{3,2},{4,5},{5,4},{6,7},{7,6},{8,9},{9,8},{10,11... | collective-permute-start | bytes 6291464 | tf_op jit(solution)/shard_map/ppermute | solution.py:15
  51.9 111.5 %collective-permute-start.1 = (f32[256,2048]{1,0:T(8,128)}, f32[256,2048]{1,0:T(8,128)}, u32[]{:S(2)}, u32[]{:S(2)}) collective-permute-start(f32[256,2048]{1,0:T(8,128)} %fusion.229), channel_id=1, source_target_pairs={{0,1},{1,0},{2,3},{3,2},{4,5},{5,4},{6,7},{7,6},{8,9},{9,8},{10,11... | collective-permute-start | bytes 6291464 | tf_op jit(solution)/shard_map/ppermute | solution.py:15
  73.0 142.5 %collective-permute-start.2 = (f32[256,2048]{1,0:T(8,128)}, f32[256,2048]{1,0:T(8,128)}, u32[]{:S(2)}, u32[]{:S(2)}) collective-permute-start(f32[256,2048]{1,0:T(8,128)} %fusion.231), channel_id=1, source_target_pairs={{0,1},{1,0},{2,3},{3,2},{4,5},{5,4},{6,7},{7,6},{8,9},{9,8},{10,11... | collective-permute-start | bytes 6291464 | tf_op jit(solution)/shard_map/ppermute | solution.py:15
  77.6 190.1 %collective-permute-start.3 = (f32[256,2048]{1,0:T(8,128)}, f32[256,2048]{1,0:T(8,128)}, u32[]{:S(2)}, u32[]{:S(2)}) collective-permute-start(f32[256,2048]{1,0:T(8,128)} %fusion.233), channel_id=1, source_target_pairs={{0,1},{1,0},{2,3},{3,2},{4,5},{5,4},{6,7},{7,6},{8,9},{9,8},{10,11... | collective-permute-start | bytes 6291464 | tf_op jit(solution)/shard_map/ppermute | solution.py:15
  82.0 27.4 %copy-start.113 = (f32[2048]{0:T(1024)S(1)}, f32[2048]{0:T(1024)}, u32[]{:S(2)}) copy-start(f32[2048]{0:T(1024)} %param.40) | copy-start | bytes 24580
  161.4 169.1 %collective-permute-start.5 = (f32[256,2048]{1,0:T(8,128)}, f32[256,2048]{1,0:T(8,128)}, u32[]{:S(2)}, u32[]{:S(2)}) collective-permute-start(f32[256,2048]{1,0:T(8,128)} %fusion.230), channel_id=1, source_target_pairs={{0,1},{1,0},{2,3},{3,2},{4,5},{5,4},{6,7},{7,6},{8,9},{9,8},{10,11... | collective-permute-start | bytes 6291464 | tf_op jit(solution)/shard_map/ppermute | solution.py:15
  341.3 23.4 %collective-permute-start.6 = (f32[2048,1024]{1,0:T(8,128)}, f32[2048,1024]{1,0:T(8,128)}, u32[]{:S(2)}, u32[]{:S(2)}) collective-permute-start(f32[2048,1024]{1,0:T(8,128)} %fusion.93), channel_id=1, source_target_pairs={{0,2},{2,0},{1,3},{3,1},{4,6},{6,4},{5,7},{7,5},{8,10},{10,8},{9,1... | collective-permute-start | bytes 25165832 | tf_op jit(solution)/shard_map/ppermute | solution.py:15
  347.8 48.4 %collective-permute-start.4 = (f32[256,2048]{1,0:T(8,128)}, f32[256,2048]{1,0:T(8,128)}, u32[]{:S(2)}, u32[]{:S(2)}) collective-permute-start(f32[256,2048]{1,0:T(8,128)} %fusion.232), channel_id=1, source_target_pairs={{0,1},{1,0},{2,3},{3,2},{4,5},{5,4},{6,7},{7,6},{8,9},{9,8},{10,11... | collective-permute-start | bytes 6291464 | tf_op jit(solution)/shard_map/ppermute | solution.py:15
  353.5 53.6 %copy-start.38 = (bf16[1024,2048]{1,0:T(8,128)(2,1)}, bf16[1024,2048]{1,0:T(8,128)(2,1)S(1)}, u32[]{:S(2)}) copy-start(bf16[1024,2048]{1,0:T(8,128)(2,1)S(1)} %pad_maximum_fusion.3) | copy-start | bytes 12582916
  380.9 26.2 %collective-permute-start.7 = (f32[2048,1024]{1,0:T(8,128)}, f32[2048,1024]{1,0:T(8,128)S(1)}, u32[]{:S(2)}, u32[]{:S(2)}) collective-permute-start(f32[2048,1024]{1,0:T(8,128)} %fusion.91), channel_id=1, source_target_pairs={{0,2},{2,0},{1,3},{3,1},{4,6},{6,4},{5,7},{7,5},{8,10},{10,8},{9,1... | collective-permute-start | bytes 25165832 | tf_op jit(solution)/shard_map/ppermute | solution.py:15
  390.1 23.8 %copy-start.15 = (bf16[1024,2048]{1,0:T(8,128)(2,1)}, bf16[1024,2048]{1,0:T(8,128)(2,1)S(1)}, u32[]{:S(2)}) copy-start(bf16[1024,2048]{1,0:T(8,128)(2,1)S(1)} %pad_maximum_fusion.2) | copy-start | bytes 12582916
  420.9 48.7 %collective-permute-start.9 = (f32[1024,2048]{1,0:T(8,128)}, f32[1024,2048]{1,0:T(8,128)}, u32[]{:S(2)}, u32[]{:S(2)}) collective-permute-start(f32[1024,2048]{1,0:T(8,128)} %fusion.97), channel_id=1, source_target_pairs={{0,2},{2,0},{1,3},{3,1},{4,6},{6,4},{5,7},{7,5},{8,10},{10,8},{9,1... | collective-permute-start | bytes 25165832 | tf_op jit(solution)/shard_map/ppermute | solution.py:15
  420.9 48.7 %collective-permute-start.8 = (f32[256,2048]{1,0:T(8,128)}, f32[256,2048]{1,0:T(8,128)S(1)}, u32[]{:S(2)}, u32[]{:S(2)}) collective-permute-start(f32[256,2048]{1,0:T(8,128)} %fusion.234), channel_id=1, source_target_pairs={{0,1},{1,0},{2,3},{3,2},{4,5},{5,4},{6,7},{7,6},{8,9},{9,8},{10,11... | collective-permute-start | bytes 6291464 | tf_op jit(solution)/shard_map/ppermute | solution.py:15
  421.2 92.9 %collective-permute-start.10 = (f32[256,2048]{1,0:T(8,128)}, f32[256,2048]{1,0:T(8,128)S(1)}, u32[]{:S(2)}, u32[]{:S(2)}) collective-permute-start(f32[256,2048]{1,0:T(8,128)} %fusion.235), channel_id=1, source_target_pairs={{0,1},{1,0},{2,3},{3,2},{4,5},{5,4},{6,7},{7,6},{8,9},{9,8},{10,11... | collective-permute-start | bytes 6291464 | tf_op jit(solution)/shard_map/ppermute | solution.py:15
  426.4 98.8 %collective-permute-start.12 = (f32[2048,512]{1,0:T(8,128)}, f32[2048,512]{1,0:T(8,128)S(1)}, u32[]{:S(2)}, u32[]{:S(2)}) collective-permute-start(f32[2048,512]{1,0:T(8,128)} %dynamic-slice_add_fusion.3), channel_id=1, source_target_pairs={{0,4},{4,0},{1,5},{5,1},{2,6},{6,2},{3,7},{7,3},{8,12},{12,8},{9,1... | collective-permute-start | bytes 12582920 | tf_op jit(solution)/shard_map/ppermute | solution.py:15
  428.0 43.3 %slice-start.4 = ((s8[8388608]{0:T(1024)(128)(4,1)}), s8[4194304]{0:T(1024)(128)(4,1)S(1)}, s32[]{:S(2)}) async-start(s8[8388608]{0:T(1024)(128)(4,1)} %bitcast.193), calls=%async_computation.20 | async-start | bytes 8388608
  429.3 40.4 %copy-start.7 = (f32[256,2048]{1,0:T(8,128)S(1)}, f32[256,2048]{1,0:T(8,128)}, u32[]{:S(2)}) copy-start(f32[256,2048]{1,0:T(8,128)} %copy-done.6) | copy-start | bytes 6291460
  429.3 40.4 %copy-start.72 = (f32[256,2048]{1,0:T(8,128)S(1)}, f32[256,2048]{1,0:T(8,128)}, u32[]{:S(2)}) copy-start(f32[256,2048]{1,0:T(8,128)} %fusion.234) | copy-start | bytes 6291460
  429.3 40.4 %copy-start.135 = (f32[256]{0:T(256)S(1)}, f32[256]{0:T(256)}, u32[]{:S(2)}) copy-start(f32[256]{0:T(256)} %copy-done.134) | copy-start | bytes 3076
  429.3 40.4 %copy-start.143 = (f32[256]{0:T(256)S(1)}, f32[256]{0:T(256)}, u32[]{:S(2)}) copy-start(f32[256]{0:T(256)} %copy-done.142) | copy-start | bytes 3076
  429.3 42.0 %slice-start.5 = ((s8[8388608]{0:T(1024)(128)(4,1)}), s8[4194304]{0:T(1024)(128)(4,1)S(1)}, s32[]{:S(2)}) async-start(s8[8388608]{0:T(1024)(128)(4,1)} %bitcast.193), calls=%async_computation.21 | async-start | bytes 8388608
  438.5 147.7 %copy-start.27 = (f32[256,2048]{1,0:T(8,128)}, f32[256,2048]{1,0:T(8,128)S(1)}, u32[]{:S(2)}) copy-start(f32[256,2048]{1,0:T(8,128)S(1)} %fusion.236) | copy-start | bytes 6291460
  561.6 59.4 %copy-start.44 = (bf16[512,8,128]{0,2,1:T(8,128)(2,1)}, bf16[512,8,128]{0,2,1:T(8,128)(2,1)S(1)}, u32[]{:S(2)}) copy-start(bf16[512,8,128]{0,2,1:T(8,128)(2,1)S(1)} %fusion.102) | copy-start | bytes 3145732
  572.8 62.1 %collective-permute-start.13 = (f32[1024,2048]{1,0:T(8,128)}, f32[1024,2048]{1,0:T(8,128)}, u32[]{:S(2)}, u32[]{:S(2)}) collective-permute-start(f32[1024,2048]{1,0:T(8,128)} %fusion.95), channel_id=1, source_target_pairs={{0,2},{2,0},{1,3},{3,1},{4,6},{6,4},{5,7},{7,5},{8,10},{10,8},{9,1... | collective-permute-start | bytes 25165832 | tf_op jit(solution)/shard_map/ppermute | solution.py:15
  576.2 650.7 %reduce-scatter.23.cloned.1.call-start = ((), (), s32[]{:S(2)}) async-start(), calls=%async_computation.15 | async-start | bytes 5242880 | tf_op jit(solution)/shard_map/reduce_scatter | solution.py:111
  581.5 93.8 %collective-permute-start.14 = (f32[2048,512]{1,0:T(8,128)}, f32[2048,512]{1,0:T(8,128)}, u32[]{:S(2)}, u32[]{:S(2)}) collective-permute-start(f32[2048,512]{1,0:T(8,128)} %dynamic-slice_add_fusion.2), channel_id=1, source_target_pairs={{0,4},{4,0},{1,5},{5,1},{2,6},{6,2},{3,7},{7,3},{8,12},{12,8},{9,1... | collective-permute-start | bytes 12582920 | tf_op jit(solution)/shard_map/ppermute | solution.py:15
  583.0 236.7 %collective-permute-start.15 = (f32[512,2048]{1,0:T(8,128)}, f32[512,2048]{1,0:T(8,128)}, u32[]{:S(2)}, u32[]{:S(2)}) collective-permute-start(f32[512,2048]{1,0:T(8,128)} %dynamic-slice_add_fusion.1), channel_id=1, source_target_pairs={{0,4},{4,0},{1,5},{5,1},{2,6},{6,2},{3,7},{7,3},{8,12},{12,8},{9,1... | collective-permute-start | bytes 12582920 | tf_op jit(solution)/shard_map/ppermute | solution.py:15
  591.4 224.7 %collective-permute-start.11 = (f32[1024,2048]{1,0:T(8,128)}, f32[1024,2048]{1,0:T(8,128)}, u32[]{:S(2)}, u32[]{:S(2)}) collective-permute-start(f32[1024,2048]{1,0:T(8,128)} %pad_maximum_fusion), channel_id=1, source_target_pairs={{0,1},{1,0},{2,3},{3,2},{4,5},{5,4},{6,7},{7,6},{8,9},{9,8},{10,11... | collective-permute-start | bytes 25165832 | tf_op jit(solution)/shard_map/ppermute | solution.py:15
  627.6 47.7 %slice-start.6 = ((s8[8388608]{0:T(1024)(128)(4,1)}), s8[4194304]{0:T(1024)(128)(4,1)S(1)}, s32[]{:S(2)}) async-start(s8[8388608]{0:T(1024)(128)(4,1)} %bitcast.222), calls=%async_computation.22 | async-start | bytes 8388608
  634.9 40.4 %slice-start.7 = ((s8[8388608]{0:T(1024)(128)(4,1)}), s8[4194304]{0:T(1024)(128)(4,1)S(1)}, s32[]{:S(2)}) async-start(s8[8388608]{0:T(1024)(128)(4,1)} %bitcast.222), calls=%async_computation.23 | async-start | bytes 8388608
  681.2 551.3 %reduce-scatter.17.cloned.1.call-start = ((), (), s32[]{:S(2)}) async-start(), calls=%async_computation.12 | async-start | bytes 5242880 | tf_op jit(solution)/shard_map/reduce_scatter | solution.py:111
  699.6 31.9 %copy-start.96 = (f32[512,8,128]{0,2,1:T(8,128)S(1)}, f32[512,8,128]{0,2,1:T(8,128)}, u32[]{:S(2)}) copy-start(f32[512,8,128]{0,2,1:T(8,128)} %fusion.99) | copy-start | bytes 6291460
  808.7 25.0 %collective-permute-start.16 = (f32[1024,1024]{1,0:T(8,128)}, f32[1024,1024]{1,0:T(8,128)}, u32[]{:S(2)}, u32[]{:S(2)}) collective-permute-start(f32[1024,1024]{1,0:T(8,128)} %fusion.88), channel_id=1, source_target_pairs={{0,2},{2,0},{1,3},{3,1},{4,6},{6,4},{5,7},{7,5},{8,10},{10,8},{9,1... | collective-permute-start | bytes 12582920 | tf_op jit(solution)/shard_map/ppermute | solution.py:15
  826.6 405.9 %reduce-scatter.19.cloned.1.call-start = ((), (), s32[]{:S(2)}) async-start(), calls=%async_computation.13 | async-start | bytes 5242880 | tf_op jit(solution)/shard_map/reduce_scatter | solution.py:111
  854.7 7.3 collective-permute-start.18
  855.2 92.6 %collective-permute-start.19 = (f32[512,2048]{1,0:T(8,128)S(1)}, f32[512,2048]{1,0:T(8,128)S(1)}, u32[]{:S(2)}, u32[]{:S(2)}) collective-permute-start(f32[512,2048]{1,0:T(8,128)S(1)} %copy-done.42), channel_id=1, source_target_pairs={{0,4},{4,0},{1,5},{5,1},{2,6},{6,2},{3,7},{7,3},{8,12},{12,8},{9,1... | collective-permute-start | bytes 12582920 | tf_op jit(solution)/shard_map/ppermute | solution.py:15
  953.5 289.7 %reduce-scatter.15.cloned.1.call-start = ((), (), s32[]{:S(2)}) async-start(), calls=%async_computation.11 | async-start | bytes 2621440 | tf_op jit(solution)/shard_map/reduce_scatter | solution.py:111
  953.5 92.0 %collective-permute-start.17 = (f32[512,2048]{1,0:T(8,128)}, f32[512,2048]{1,0:T(8,128)S(1)}, u32[]{:S(2)}, u32[]{:S(2)}) collective-permute-start(f32[512,2048]{1,0:T(8,128)} %add_add_fusion.3), channel_id=1, source_target_pairs={{0,1},{1,0},{2,3},{3,2},{4,5},{5,4},{6,7},{7,6},{8,9},{9,8},{10,11... | collective-permute-start | bytes 12582920 | tf_op jit(solution)/shard_map/ppermute | solution.py:15
  954.5 91.0 %slice-start = ((s8[8388608]{0:T(1024)(128)(4,1)}), s8[4194304]{0:T(1024)(128)(4,1)S(1)}, s32[]{:S(2)}) async-start(s8[8388608]{0:T(1024)(128)(4,1)} %bitcast.189), calls=%async_computation.16 | async-start | bytes 8388608
  960.2 85.3 %slice-start.1 = ((s8[8388608]{0:T(1024)(128)(4,1)}), s8[4194304]{0:T(1024)(128)(4,1)S(1)}, s32[]{:S(2)}) async-start(s8[8388608]{0:T(1024)(128)(4,1)} %bitcast.189), calls=%async_computation.17 | async-start | bytes 8388608
  960.2 85.3 %copy-start.34 = (f32[512,2048]{1,0:T(8,128)S(1)}, f32[512,2048]{1,0:T(8,128)}, u32[]{:S(2)}) copy-start(f32[512,2048]{1,0:T(8,128)} %add_add_fusion.3) | copy-start | bytes 12582916
  960.2 85.3 %copy-start.108 = (f32[2048]{0:T(1024)S(1)}, f32[2048]{0:T(1024)}, u32[]{:S(2)}) copy-start(f32[2048]{0:T(1024)} %param.32) | copy-start | bytes 24580
  962.6 87.1 %collective-permute-start.21 = (f32[1024,1024]{1,0:T(8,128)S(1)}, f32[1024,1024]{1,0:T(8,128)}, u32[]{:S(2)}, u32[]{:S(2)}) collective-permute-start(f32[1024,1024]{1,0:T(8,128)S(1)} %fusion.110), channel_id=1, source_target_pairs={{0,2},{2,0},{1,3},{3,1},{4,6},{6,4},{5,7},{7,5},{8,10},{10,8},{9,1... | collective-permute-start | bytes 12582920 | tf_op jit(solution)/shard_map/ppermute | solution.py:15
  962.7 89.5 %collective-permute-start.22 = (f32[1024,512]{1,0:T(8,128)}, f32[1024,512]{1,0:T(8,128)S(1)}, u32[]{:S(2)}, u32[]{:S(2)}) collective-permute-start(f32[1024,512]{1,0:T(8,128)} %dynamic-slice_add_fusion.7), channel_id=1, source_target_pairs={{0,4},{4,0},{1,5},{5,1},{2,6},{6,2},{3,7},{7,3},{8,12},{12,8},{9,1... | collective-permute-start | bytes 6291464 | tf_op jit(solution)/shard_map/ppermute | solution.py:15
  1065.7 7.5 collective-permute-start.23
  1065.7 177.5 %reduce-scatter.9.cloned.1.call-start = ((), (), s32[]{:S(2)}) async-start(), calls=%async_computation.8 | async-start | bytes 2621440 | tf_op jit(solution)/shard_map/reduce_scatter | solution.py:111
  1065.8 49.0 %copy-start.101 = (f32[1024,1024]{1,0:T(8,128)S(1)}, f32[1024,1024]{1,0:T(8,128)}, u32[]{:S(2)}) copy-start(f32[1024,1024]{1,0:T(8,128)} %copy-done.100) | copy-start | bytes 12582916
  1065.8 93.4 %collective-permute-start.20 = (f32[512,2048]{1,0:T(8,128)}, f32[512,2048]{1,0:T(8,128)}, u32[]{:S(2)}, u32[]{:S(2)}) collective-permute-start(f32[512,2048]{1,0:T(8,128)} %add_add_fusion.2), channel_id=1, source_target_pairs={{0,1},{1,0},{2,3},{3,2},{4,5},{5,4},{6,7},{7,6},{8,9},{9,8},{10,11... | collective-permute-start | bytes 12582920 | tf_op jit(solution)/shard_map/ppermute | solution.py:15
  1066.8 48.0 %collective-permute-start.24 = (f32[512,1024]{1,0:T(8,128)}, f32[512,1024]{1,0:T(8,128)S(1)}, u32[]{:S(2)}, u32[]{:S(2)}) collective-permute-start(f32[512,1024]{1,0:T(8,128)} %dynamic-slice_add_fusion.6), channel_id=1, source_target_pairs={{0,4},{4,0},{1,5},{5,1},{2,6},{6,2},{3,7},{7,3},{8,12},{12,8},{9,1... | collective-permute-start | bytes 6291464 | tf_op jit(solution)/shard_map/ppermute | solution.py:15
  1116.8 126.4 %reduce-scatter.11.cloned.1.call-start = ((), (), s32[]{:S(2)}) async-start(), calls=%async_computation.9 | async-start | bytes 2621440 | tf_op jit(solution)/shard_map/reduce_scatter | solution.py:111
  1116.9 42.3 %copy-start.33 = (f32[512,2048]{1,0:T(8,128)S(1)}, f32[512,2048]{1,0:T(8,128)}, u32[]{:S(2)}) copy-start(f32[512,2048]{1,0:T(8,128)} %add_add_fusion.2) | copy-start | bytes 12582916
  1116.9 52.5 %collective-permute-start.29 = (f32[512,1024]{1,0:T(8,128)}, f32[512,1024]{1,0:T(8,128)S(1)}, u32[]{:S(2)}, u32[]{:S(2)}) collective-permute-start(f32[512,1024]{1,0:T(8,128)} %dynamic-slice_add_fusion.5), channel_id=1, source_target_pairs={{0,4},{4,0},{1,5},{5,1},{2,6},{6,2},{3,7},{7,3},{8,12},{12,8},{9,1... | collective-permute-start | bytes 6291464 | tf_op jit(solution)/shard_map/ppermute | solution.py:15
  1118.6 45.2 %slice-start.2 = ((s8[8388608]{0:T(1024)(128)(4,1)}), s8[4194304]{0:T(1024)(128)(4,1)S(1)}, s32[]{:S(2)}) async-start(s8[8388608]{0:T(1024)(128)(4,1)} %bitcast.191), calls=%async_computation.18 | async-start | bytes 8388608
  1123.9 39.9 %slice-start.3 = ((s8[8388608]{0:T(1024)(128)(4,1)}), s8[4194304]{0:T(1024)(128)(4,1)S(1)}, s32[]{:S(2)}) async-start(s8[8388608]{0:T(1024)(128)(4,1)} %bitcast.191), calls=%async_computation.19 | async-start | bytes 8388608
  1123.9 39.9 %copy-start.21 = (f32[256,2048]{1,0:T(8,128)S(1)}, f32[256,2048]{1,0:T(8,128)}, u32[]{:S(2)}) copy-start(f32[256,2048]{1,0:T(8,128)} %get-tuple-element.214) | copy-start | bytes 6291460
  1123.9 40.0 %copy-start.23 = (f32[256,2048]{1,0:T(8,128)S(1)}, f32[256,2048]{1,0:T(8,128)}, u32[]{:S(2)}) copy-start(f32[256,2048]{1,0:T(8,128)} %get-tuple-element.217) | copy-start | bytes 6291460
  1173.2 96.5 %reduce-scatter.13.cloned.1.call-start = ((), (), s32[]{:S(2)}) async-start(), calls=%async_computation.10 | async-start | bytes 2621440 | tf_op jit(solution)/shard_map/reduce_scatter | solution.py:111
  1173.3 47.6 %collective-permute-start.30 = (f32[512,1024]{1,0:T(8,128)}, f32[512,1024]{1,0:T(8,128)}, u32[]{:S(2)}, u32[]{:S(2)}) collective-permute-start(f32[512,1024]{1,0:T(8,128)} %dynamic-slice_add_fusion.4), channel_id=1, source_target_pairs={{0,4},{4,0},{1,5},{5,1},{2,6},{6,2},{3,7},{7,3},{8,12},{12,8},{9,1... | collective-permute-start | bytes 6291464 | tf_op jit(solution)/shard_map/ppermute | solution.py:15
  1183.6 41.5 %collective-permute-start.25 = (f32[4,2,1152]{2,1,0:T(2,128)S(1)}, f32[4,2,1152]{2,1,0:T(2,128)S(1)}, u32[]{:S(2)}, u32[]{:S(2)}) collective-permute-start(f32[4,2,1152]{2,1,0:T(2,128)S(1)} %bitcast.238), channel_id=1, source_target_pairs={{0,2},{2,0},{1,3},{3,1},{4,6},{6,4},{5,7},{7,5},{8,10},{10,8},{9,1... | collective-permute-start | bytes 110600 | tf_op jit(solution)/shard_map/ppermute | solution.py:15
  1225.2 4.7 collective-permute-start.26
  1230.0 5.8 collective-permute-start.27
  1235.7 4.7 collective-permute-start.28
  (153 other events, 1117.5 us)
Sparse Core Ops, SparseCore 0:
  576.3 77.2 reduce-scatter.20
  681.4 77.0 reduce-scatter.22
  826.8 77.2 reduce-scatter.16
  953.6 77.4 reduce-scatter.18
  1065.8 44.4 reduce-scatter.14
  1116.9 44.4 reduce-scatter.8
  1173.3 44.3 reduce-scatter.10
  1225.3 44.3 reduce-scatter.12

commit v3 on v2

v3 whole, which is shorter than its diff:
```python
import math

import jax
import jax.numpy as jnp
from jax import lax
from jax.experimental import pallas as pl
from jax.experimental.pallas import tpu as pltpu
from jax.sharding import Mesh
from jax.sharding import PartitionSpec as P

F32 = jnp.float32
BF16 = jnp.bfloat16
CHUNKS = 4


def swap(value, axis):
    return lax.ppermute(value, axis, [(0, 1), (1, 0)])


def mm(left, right, contract):
    return lax.dot_general(left, right, (contract, ((), ())), preferred_element_type=F32)


def norm_parts(field):
    average = jnp.mean(field, -1, keepdims=True)
    centred = field - average
    variance = jnp.mean(centred * centred, -1, keepdims=True)
    scale = lax.rsqrt(variance + 1e-05)
    return centred * scale, scale


def norm_pull(grad, unit, scale, gain):
    scaled = grad * gain
    first = jnp.mean(scaled, -1, keepdims=True)
    second = jnp.mean(scaled * unit, -1, keepdims=True)
    return scale * (scaled - first - unit * second)


def after(value, *others):
    return lax.optimization_barrier((value,) + others)[0]


def blank(shape):
    return pl.pallas_call(
        lambda out_ref: None,
        out_specs=pl.BlockSpec(memory_space=pl.ANY),
        out_shape=jax.ShapeDtypeStruct(shape, F32),
    )()


def fitting(size, most):
    block = min(size, most)
    while size % block:
        block //= 2
    return block


def paired(left, right, left_at, right_at, shape, near=None, near_at=None, extra=None):
    length = left.shape[0]
    rows, cols = fitting(shape[0], 512), fitting(shape[1], 1024)
    near_at = near_at or (0, 0)
    starts = jnp.stack(
        [
            jnp.int32(left_at // rows),
            jnp.int32(right_at // cols),
            jnp.int32(near_at[0] // rows),
            jnp.int32(near_at[1] // cols),
        ]
    )

    def kernel(starts_ref, left_ref, right_ref, *rest):
        total = mm(left_ref[...], right_ref[...], ((0,), (0,)))
        for ref in rest[:-1]:
            total = total + ref[...]
        rest[-1][...] = total

    out_spec = pl.BlockSpec((rows, cols), lambda i, j, starts: (i, j))
    in_specs = [
        pl.BlockSpec((length, rows), lambda i, j, starts: (0, starts[0] + i)),
        pl.BlockSpec((length, cols), lambda i, j, starts: (0, starts[1] + j)),
    ]
    operands = [left, right]
    if near is not None:
        in_specs.append(pl.BlockSpec((rows, cols), lambda i, j, starts: (starts[2] + i, starts[3] + j)))
        operands.append(near)
    if extra is not None:
        in_specs.append(out_spec)
        operands.append(extra)
    return pl.pallas_call(
        kernel,
        grid_spec=pltpu.PrefetchScalarGridSpec(
            num_scalar_prefetch=1,
            grid=(shape[0] // rows, shape[1] // cols),
            in_specs=in_specs,
            out_specs=out_spec,
        ),
        out_shape=jax.ShapeDtypeStruct(shape, F32),
    )(starts, *operands)


def product_down(left, right):
    rows, inner = left.shape
    cols = right.shape[1]
    deep, wide = fitting(inner, 2048), fitting(cols, 512)

    def kernel(left_ref, right_ref, out_ref):
        share = mm(left_ref[...], right_ref[...], ((1,), (0,)))

        @pl.when(pl.program_id(1) == 0)
        def _():
            out_ref[...] = share

        @pl.when(pl.program_id(1) > 0)
        def _():
            out_ref[...] += share

    return pl.pallas_call(
        kernel,
        grid=(cols // wide, inner // deep),
        in_specs=[
            pl.BlockSpec((rows, deep), lambda j, k: (0, k)),
            pl.BlockSpec((deep, wide), lambda j, k: (k, j)),
        ],
        out_specs=pl.BlockSpec((rows, wide), lambda j, k: (0, j)),
        out_shape=jax.ShapeDtypeStruct((rows, cols), F32),
    )(left, right)


def product_back(pulls, weights, rows, index):
    span = pulls[0].shape[1]
    cols = weights[0].shape[0]
    wide = fitting(cols, 512)
    count = len(pulls)

    def kernel(*refs):
        total = mm(refs[0][...], refs[count][...], ((1,), (1,)))
        for at in range(1, count):
            total = total + mm(refs[at][...], refs[count + at][...], ((1,), (1,)))
        refs[-1][...] = total

    return pl.pallas_call(
        kernel,
        grid=(cols // wide,),
        in_specs=[pl.BlockSpec((rows, span), lambda j: (index, 0))] * count
        + [pl.BlockSpec((wide, span), lambda j: (j, 0))] * count,
        out_specs=pl.BlockSpec((rows, wide), lambda j: (0, j)),
        out_shape=jax.ShapeDtypeStruct((rows, cols), F32),
    )(*pulls, *weights)


def rows_of(count, begin, seen, boundary):
    rows = begin + lax.broadcasted_iota(jnp.int32, (count, seen), 0)
    cols = lax.broadcasted_iota(jnp.int32, (count, seen), 1)
    return (cols <= rows) | (cols < boundary)


def attend(queries, keys, values, boundary, block, block_rows, head_dim):
    length, span = queries.shape
    heads = span // head_dim
    tile = min(256, block_rows)
    scale = 1.0 / math.sqrt(head_dim)

    def kernel(boundary_ref, query_ref, key_ref, value_ref, mixed_ref, log_ref):
        for at in range(0, block_rows, tile):
            begin = block * block_rows + at
            seen = max(begin + tile, length // 2)
            scores = mm(query_ref[at : at + tile, :], key_ref[:seen, :], ((1,), (1,))) * scale
            scores = jnp.where(rows_of(tile, begin, seen, boundary_ref[0]), scores, -1e30)
            peak = jnp.max(scores, -1, keepdims=True)
            exps = jnp.exp(scores - peak)
            sums = jnp.sum(exps, -1, keepdims=True)
            log_ref[0, at : at + tile, :] = peak + jnp.log(sums)
            probs = (exps / sums).astype(BF16)
            mixed = mm(probs, value_ref[:seen, :], ((1,), (0,)))
            mixed_ref[at : at + tile, :] = mixed.astype(BF16)

    whole = pl.BlockSpec((length, head_dim), lambda head: (0, head))
    return pl.pallas_call(
        kernel,
        grid=(heads,),
        in_specs=[
            pl.BlockSpec(memory_space=pltpu.SMEM),
            pl.BlockSpec((block_rows, head_dim), lambda head: (block, head)),
            whole,
            whole,
        ],
        out_specs=[
            pl.BlockSpec((block_rows, head_dim), lambda head: (0, head)),
            pl.BlockSpec((1, block_rows, 1), lambda head: (head, 0, 0)),
        ],
        out_shape=[
            jax.ShapeDtypeStruct((block_rows, span), BF16),
            jax.ShapeDtypeStruct((heads, block_rows, 1), F32),
        ],
    )(boundary, queries, keys, values)


def attend_pull(queries, keys, values, mixed_grad, totals_log, boundary, head_dim):
    length, span = queries.shape
    heads = span // head_dim
    block_rows = totals_log[0].shape[1]
    tile = min(256, block_rows)
    scale = 1.0 / math.sqrt(head_dim)
    blocks = len(totals_log)

    def kernel(boundary_ref, query_ref, key_ref, value_ref, mixed_ref, *rest):
        log_refs, (dq_ref, dk_ref, dv_ref, qb_ref, vb_ref, dk_acc, dv_acc) = rest[:blocks], rest[blocks:]
        dk_acc[...] = jnp.zeros_like(dk_acc)
        dv_acc[...] = jnp.zeros_like(dv_acc)
        query_sum = jnp.zeros((1, head_dim), F32)
        for begin in range(0, length, tile):
            seen = max(begin + tile, length // 2)
            rows = slice(begin, begin + tile)
            query = query_ref[rows, :]
            mixed = mixed_ref[rows, :]
            inner = begin % block_rows
            log_total = log_refs[begin // block_rows][0, inner : inner + tile, :]
            scores = mm(query, key_ref[:seen, :], ((1,), (1,))) * scale
            scores = jnp.where(rows_of(tile, begin, seen, boundary_ref[0]), scores, -1e30)
            probs = jnp.exp(scores - log_total)
            prob_grad = mm(mixed, value_ref[:seen, :], ((1,), (1,)))
            row_dot = jnp.sum(probs * prob_grad, -1, keepdims=True)
            score_grad = (probs * (prob_grad - row_dot) * scale).astype(BF16)
            query_grad = mm(score_grad, key_ref[:seen, :], ((1,), (0,))).astype(BF16)
            dq_ref[rows, :] = query_grad
            query_sum = query_sum + jnp.sum(query_grad.astype(F32), 0, keepdims=True)
            dk_acc[:seen, :] += mm(score_grad, query, ((0,), (0,)))
            dv_acc[:seen, :] += mm(probs.astype(BF16), mixed, ((0,), (0,)))
        dk_ref[...] = dk_acc[...].astype(BF16)
        value_grad = dv_acc[...].astype(BF16)
        dv_ref[...] = value_grad
        qb_ref[0] = query_sum
        vb_ref[0] = jnp.sum(value_grad.astype(F32), 0, keepdims=True)

    whole = pl.BlockSpec((length, head_dim), lambda head: (0, head))
    line = pl.BlockSpec((1, 1, head_dim), lambda head: (head, 0, 0))
    return pl.pallas_call(
        kernel,
        grid=(heads,),
        in_specs=[pl.BlockSpec(memory_space=pltpu.SMEM)]
        + [whole] * 4
        + [pl.BlockSpec((1, block_rows, 1), lambda head: (head, 0, 0))] * blocks,
        out_specs=[whole] * 3 + [line] * 2,
        out_shape=[jax.ShapeDtypeStruct((length, span), BF16)] * 3
        + [jax.ShapeDtypeStruct((heads, 1, head_dim), F32)] * 2,
        scratch_shapes=[pltpu.VMEM((length, head_dim), F32)] * 2,
    )(boundary, queries, keys, values, mixed_grad, *totals_log)


def hidden_step(normed2, dy, up_weight, up_bias, down_weight, index, count, kept):
    chunk, width = normed2.shape
    local = up_weight.shape[1]
    block = min(512, local)
    pair = index % 2

    def kernel(normed_ref, dy_ref, up_ref, bias_ref, down_ref, *rest):
        act_ref, pull_ref, norm_ref, sum_ref = rest[-4:]
        hidden = mm(normed_ref[...], up_ref[...], ((1,), (0,))) + bias_ref[...]
        acts_grad = mm(dy_ref[...], down_ref[...], ((1,), (1,)))
        half = 0.5 * (1.0 + lax.erf(hidden * math.sqrt(0.5)))
        act_ref[...] = (hidden * half).astype(BF16)
        slope = half + hidden * (jnp.exp(-0.5 * hidden * hidden) * (1.0 / math.sqrt(2.0 * math.pi)))
        pull = (acts_grad * slope).astype(BF16)
        pull_ref[...] = pull
        sum_ref[...] = jnp.sum(pull.astype(F32), 0, keepdims=True)
        share = mm(pull, up_ref[...], ((1,), (1,)))

        @pl.when(pl.program_id(0) == 0)
        def _():
            norm_ref[...] = share

        @pl.when(pl.program_id(0) > 0)
        def _():
            norm_ref[...] += share

    same = pl.BlockSpec((chunk, width), lambda at: (0, 0))
    wide = pl.BlockSpec((chunk, block), lambda at: (index, at))
    line = pl.BlockSpec((1, block), lambda at: (0, at))
    held = [] if kept is None else [kept[0], kept[1]] + ([kept[2]] if pair else [])
    return pl.pallas_call(
        kernel,
        grid=(local // block,),
        in_specs=[
            same,
            pl.BlockSpec((chunk, width), lambda at: (index, 0)),
            pl.BlockSpec((width, block), lambda at: (0, at)),
            line,
            pl.BlockSpec((block, width), lambda at: (at, 0)),
        ]
        + [pl.BlockSpec(memory_space=pl.ANY)] * len(held),
        out_specs=[wide, wide, pl.BlockSpec((chunk, width), lambda at: (pair, 0)), line],
        out_shape=[
            jax.ShapeDtypeStruct((chunk * count, local), BF16),
            jax.ShapeDtypeStruct((chunk * count, local), BF16),
            jax.ShapeDtypeStruct((2 * chunk, width), F32),
            jax.ShapeDtypeStruct((1, local), F32),
        ],
        input_output_aliases={5 + at: at for at in range(len(held))},
    )(normed2, dy, up_weight, up_bias, down_weight, *held)


def body(
    inputs,
    prefix_len,
    norm1_gain,
    norm1_bias,
    query_weight,
    query_bias,
    key_weight,
    value_weight,
    value_bias,
    out_weight,
    out_bias,
    norm2_gain,
    norm2_bias,
    up_weight,
    up_bias,
    down_weight,
    down_bias,
    out_grad,
):
    length, width = inputs.shape
    heads_local, head_dim = query_bias.shape
    zs, xs, cs = lax.axis_size("z"), lax.axis_size("x"), lax.axis_size("c")
    dps = zs * xs * cs
    at_x, at_c = lax.axis_index("x"), lax.axis_index("c")
    wide = width // dps
    part = zs * wide
    block_rows = min(512, length)
    block_count = length // block_rows
    chunk = length // CHUNKS

    def pieces(field, by_z=False):
        if wide % 128:
            parts = field.reshape(length, zs, xs, cs, wide)
            return jnp.transpose(parts, (0, 3, 1, 2, 4) if by_z else (0, 3, 2, 1, 4)).reshape(field.shape)

        def source(at):
            c, rest = at // (xs * zs), at % (xs * zs)
            if by_z:
                return (0, rest * cs + c)
            return (0, ((rest % zs) * xs + rest // zs) * cs + c)

        def kernel(field_ref, out_ref):
            out_ref[...] = field_ref[...]

        return pl.pallas_call(
            kernel,
            grid=(dps,),
            in_specs=[pl.BlockSpec((length, wide), source)],
            out_specs=pl.BlockSpec((length, wide), lambda at: (0, at)),
            out_shape=jax.ShapeDtypeStruct(field.shape, field.dtype),
        )(field)

    once = jnp.minimum(prefix_len[0], 1)

    def swap_now(value):
        def step(state):
            return (state[0] + 1, state[1], swap(after(state[1], state[0]), "c"))

        start = (jnp.int32(0), value, blank(value.shape))
        return lax.while_loop(lambda state: state[0] < once, step, start)[2]

    class Sum:
        def __init__(self, parts, other, by_rows, begin=0, size=None):
            self.parts, self.other, self.by_rows = parts, other, by_rows
            self.dim = 0 if by_rows else 1
            self.begin = begin
            self.size = size or other.shape[1]

        def product(self, begin, size, gate, near_at=None, extra=None):
            other = after(self.other, *gate)
            near = None if near_at is None else self.near
            if self.by_rows:
                at = None if near_at is None else (near_at, 0)
                return paired(self.parts, other, begin, self.begin, (size, self.size), near, at, extra)
            at = None if near_at is None else (0, near_at)
            return paired(other, self.parts, self.begin, begin, (self.size, size), near, at, extra)

        def over_cores(self, *gate):
            own = self.product((1 - at_c) * xs * part, xs * part, gate)
            self.own = own
            return own

        def meet(self, *gate):
            self.near = swap_now(after(self.own, *gate))
            return self.near

        def over_x(self, *gate):
            far = 1 - at_x
            own = self.product((at_c * xs + far) * part, part, gate, far * part)
            self.across = swap(own, "x")
            return own

        def over_z(self, *gate):
            across = after(self.across, *gate)
            total = self.product((at_c * xs + at_x) * part, part, gate, at_x * part, across)
            self.result = lax.psum_scatter(total, "z", scatter_dimension=self.dim, tiled=True)
            return total

        def over_z_first(self, *gate):
            total = self.product(at_c * xs * part, xs * part, gate, 0)
            self.both = lax.psum_scatter(total, "z", scatter_dimension=self.dim, tiled=True)
            return total

        def over_x_last(self, *gate):
            both = after(self.both, *gate)

            def take(x):
                return lax.dynamic_slice_in_dim(both, x * wide, wide, self.dim)

            self.result = take(at_x) + swap(take(1 - at_x), "x")
            return self.result

    features = inputs.astype(F32)
    unit1, scale1 = norm_parts(features)
    normed = (unit1 * norm1_gain + norm1_bias).astype(BF16)
    queries = (mm(normed, query_weight, ((1,), (0,))) + query_bias.reshape(-1)).astype(BF16)
    keys = mm(normed, key_weight, ((1,), (0,))).astype(BF16)
    values = (mm(normed, value_weight, ((1,), (0,))) + value_bias.reshape(-1)).astype(BF16)
    totals_log, attn_parts, mixed_blocks = [], [], []
    for block in range(block_count):
        mixed_block, log_total = attend(queries, keys, values, prefix_len, block, block_rows, head_dim)
        totals_log.append(log_total)
        mixed_blocks.append(mixed_block)
        for begin in range(0, block_rows, chunk):
            attn_parts.append(mm(mixed_block[begin : begin + chunk], out_weight, ((1,), (0,))))
    mixed = jnp.concatenate(mixed_blocks, 0)
    attn_others = [swap(piece, "mp") for piece in attn_parts]

    resids, units2, scales2, normeds2 = [], [], [], []
    shares, pull_sums, kept = [], [], None
    for index in range(CHUNKS):
        rows = slice(index * chunk, (index + 1) * chunk)
        attn_other = attn_others[index]
        if index == 0:
            attn_other = after(attn_other, attn_parts[-1])
        else:
            attn_other = after(attn_other, pull_sums[-1])
        resid = features[rows] + ((attn_parts[index] + attn_other) + out_bias)
        unit2, scale2 = norm_parts(resid)
        normed2 = (unit2 * norm2_gain + norm2_bias).astype(BF16)
        kept = hidden_step(
            normed2, out_grad, up_weight, up_bias.reshape(1, -1), down_weight, index, CHUNKS, kept
        )
        if index % 2:
            shares.append(kept[2])
        pull_sums.append(kept[3])
        resids.append(resid)
        units2.append(unit2)
        scales2.append(scale2)
        normeds2.append(normed2)
    acts, hidden_grads = kept[0], kept[1]
    up_bias_grad = sum(pull_sums)[0]
    share_others = [swap(after(shares[0], attn_others[-1]), "mp")]
    share_others.append(swap(shares[1], "mp"))

    grad_float = out_grad.astype(F32)
    down_bias_grad = jnp.sum(grad_float, 0)
    half = up_weight.shape[1] // 2
    normed2_pieces = pieces(jnp.concatenate(normeds2, 0))
    downs = [
        Sum(pieces(out_grad, begin == 0), acts, False, begin, half) for begin in (0, half)
    ]
    ups = [Sum(normed2_pieces, hidden_grads, True, begin, half) for begin in (0, half)]

    resid_grads, attn_grads, mixed_grads = [], [], []
    norm2_gain_grad, norm2_bias_grad, out_bias_grad = 0.0, 0.0, 0.0

    def norm2_pull(pair, *gate):
        nonlocal norm2_gain_grad, norm2_bias_grad, out_bias_grad
        rows = slice(pair * 2 * chunk, (pair + 1) * 2 * chunk)
        unit2 = jnp.concatenate(units2[2 * pair : 2 * pair + 2], 0)
        scale2 = jnp.concatenate(scales2[2 * pair : 2 * pair + 2], 0)
        norm2_in = shares[pair] + after(share_others[pair], *gate)
        norm2_bias_grad = norm2_bias_grad + jnp.sum(norm2_in, 0)
        norm2_gain_grad = norm2_gain_grad + jnp.sum(norm2_in * unit2, 0)
        resid_grad = grad_float[rows] + norm_pull(norm2_in, unit2, scale2, norm2_gain)
        attn_grad = resid_grad.astype(BF16)
        out_bias_grad = out_bias_grad + jnp.sum(attn_grad.astype(F32), 0)
        mixed_grads.append(mm(attn_grad, out_weight, ((1,), (1,))).astype(BF16))
        resid_grads.append(resid_grad)
        attn_grads.append(attn_grad)
        return mixed_grads[-1]

    gate = downs[0].over_cores(kept[3])
    gate = downs[0].meet(gate)
    gate = downs[0].over_z_first(gate)
    gate = downs[1].over_cores(gate)
    branch = product_down(after(acts, gate), down_weight)
    gate = downs[1].meet(branch, share_others[0])
    gate = downs[1].over_x(gate)
    gate = norm2_pull(0, gate)
    gate = ups[0].over_cores(gate)
    gate = ups[1].over_cores(gate)
    gate = norm2_pull(1, gate)
    branch_other = swap(after(branch, share_others[-1]), "mp")
    gate = downs[1].over_z(gate)
    gate = ups[0].meet(gate)
    gate = ups[0].over_x(gate)
    gate = ups[1].meet(gate)
    mixed_grad = jnp.concatenate(mixed_grads, 0)
    attn_grad = jnp.concatenate(attn_grads, 0)
    query_grad, key_grad, value_grad, query_bias_grad, value_bias_grad = attend_pull(
        queries, keys, values, after(mixed_grad, gate), totals_log, prefix_len, head_dim
    )
    gate = query_bias_grad

    half_rows = length // 2
    norm1_parts = []
    pulls = [after(query_grad, gate), key_grad, value_grad]
    for index in range(2):
        norm1_parts.append(product_back(pulls, [query_weight, key_weight, value_weight], half_rows, index))
    norm1_others = [swap(piece, "mp") for piece in norm1_parts]

    normed_pieces = pieces(normed)
    out_sum = Sum(pieces(attn_grad), mixed, False)
    query_sum, key_sum, value_sum = [
        Sum(normed_pieces, pull, True) for pull in (query_grad, key_grad, value_grad)
    ]
    gate = ups[1].over_x(*norm1_parts)
    sums = [out_sum, query_sum, key_sum, value_sum]
    for item in sums:
        gate = item.over_cores(gate)
    for item in sums:
        gate = item.meet(gate)
    gate = ups[0].over_z(gate)
    gate = out_sum.over_x(gate)
    outputs = (jnp.concatenate(resids, 0) + ((branch + after(branch_other, gate)) + down_bias)).astype(BF16)
    gate = ups[1].over_z(outputs)
    gate = query_sum.over_x(gate)
    gate = out_sum.over_z(gate)
    gate = key_sum.over_x(gate)

    norm1_gain_grad, norm1_bias_grad = 0.0, 0.0
    in_grads = []

    def norm1_pull(index, gate):
        nonlocal norm1_gain_grad, norm1_bias_grad
        rows = slice(index * half_rows, (index + 1) * half_rows)
        norm1_in = norm1_parts[index] + after(norm1_others[index], gate)
        norm1_bias_grad = norm1_bias_grad + jnp.sum(norm1_in, 0)
        norm1_gain_grad = norm1_gain_grad + jnp.sum(norm1_in * unit1[rows], 0)
        pulled = norm_pull(norm1_in, unit1[rows], scale1[rows], norm1_gain)
        in_grads.append((resid_grads[index] + pulled).astype(BF16))
        return in_grads[-1]

    gate = norm1_pull(0, gate)
    gate = query_sum.over_z(gate)
    gate = value_sum.over_x(gate)
    gate = downs[0].over_x_last(gate)
    gate = key_sum.over_z(gate)
    gate = norm1_pull(1, gate)
    in_grad = jnp.concatenate(in_grads, 0)

    def blocks(vector, lead):
        return jnp.transpose(vector.reshape(lead, dps, -1), (1, 0, 2)).reshape(dps, -1)

    small = jnp.concatenate(
        [
            blocks(norm1_gain_grad, 1),
            blocks(norm1_bias_grad, 1),
            blocks(query_bias_grad, heads_local),
            blocks(value_bias_grad, heads_local),
            blocks(out_bias_grad, 1),
            blocks(norm2_gain_grad, 1),
            blocks(norm2_bias_grad, 1),
            blocks(up_bias_grad, up_bias.shape[0]),
            blocks(down_bias_grad, 1),
        ],
        1,
    )
    small = small.reshape(zs, xs, cs, -1)

    def fold(field, axis, at, dim):
        def take(index):
            return lax.dynamic_index_in_dim(field, index, dim, keepdims=False)

        return take(at) + swap(take(1 - at), axis)

    small = fold(small, "c", at_c, 2)
    small = fold(small, "x", at_x, 1)
    at_z, span = lax.axis_index("z"), zs
    while span > 1:
        span //= 2
        halved = small.reshape(2, span, -1)
        side = (at_z // span) % 2
        pairs = [(i, i ^ span) for i in range(zs)]
        mine = lax.dynamic_index_in_dim(halved, side, 0, keepdims=False)
        other = lax.dynamic_index_in_dim(halved, 1 - side, 0, keepdims=False)
        small = mine + lax.ppermute(other, "z", pairs)
    small = small.reshape(-1)

    gate = value_sum.over_z(gate)
    down_weight_grad = jnp.concatenate([item.result for item in downs], 0)
    up_weight_grad = jnp.concatenate([item.result for item in ups], 1)

    thin = head_dim // dps
    sizes = [wide, wide, heads_local * thin, heads_local * thin, wide, wide, wide]
    sizes += [up_bias.shape[0] * thin, wide]
    split, begin = [], 0
    for size in sizes:
        split.append(small[begin : begin + size])
        begin += size
    gain1, bias1, query_b, value_b, out_b, gain2, bias2, up_b, down_b = split
    return (
        outputs,
        in_grad,
        gain1,
        bias1,
        query_sum.result,
        query_b.reshape(heads_local, thin),
        key_sum.result,
        value_sum.result,
        value_b.reshape(heads_local, thin),
        out_sum.result,
        out_b,
        gain2,
        bias2,
        up_weight_grad,
        up_b.reshape(-1, thin),
        down_weight_grad,
        down_b,
    )


def solution(mesh):
    dps = mesh.shape["dp"]
    fine = Mesh(mesh.devices.reshape(dps // 4, 2, 2, mesh.shape["mp"]), ("z", "x", "c", "mp"))
    dp = ("z", "x", "c")
    in_specs = (
        P(dp, None),
        P(dp),
        P(),
        P(),
        P(None, "mp"),
        P("mp", None),
        P(None, "mp"),
        P(None, "mp"),
        P("mp", None),
        P("mp", None),
        P(),
        P(),
        P(),
        P(None, "mp"),
        P("mp", None),
        P("mp", None),
        P(),
        P(dp, None),
    )
    out_specs = (
        P(dp, None),
        P(dp, None),
        P(dp),
        P(dp),
        P(dp, "mp"),
        P("mp", dp),
        P(dp, "mp"),
        P(dp, "mp"),
        P("mp", dp),
        P("mp", dp),
        P(dp),
        P(dp),
        P(dp),
        P(dp, "mp"),
        P("mp", dp),
        P("mp", dp),
        P(dp),
    )
    return jax.shard_map(body, mesh=fine, in_specs=in_specs, out_specs=out_specs, check_vma=False)
```

time: 1290 us -> 1090 us (0.84)
  matrix products: 574 us -> 35.9 us
  Pallas kernels: 0 us -> 424 us
  local copies, waits for them, and re-layouts: 101 us -> 13.3 us
  waiting for transfers between devices: 388 us -> 439 us
  other arithmetic: 165 us -> 124 us
    pallas_call x0 -> x46, Pallas kernels: none -> 424 us  [the longest x23 179 us: paired(): pl.pallas_call(kernel, grid_spec=pltpu.PrefetchScalarGridSpec(num_scalar_...]
    dot_general x57 -> x9, matrix products: 432 us -> 35.9 us  [mm(): lax.dot_general(left, right, (contract, ((), ())), preferred_element_type...]
    dot_general x12 -> x0, matrix products: 142 us -> none  [the longest x2 51.3 us: body(): jnp.einsum('hqk,khd->qhd', score_grad, keys[:seen], preferred_element_typ...]
    unnamed x421 -> x108, local copies, waits for them, and re-layouts: 78.9 us -> 5.42 us
    reduce_scatter x8 -> x7, waiting for transfers between devices: 26.5 us -> 80.8 us  [over_z(): lax.psum_scatter(total, 'z', scatter_dimension=self.dim, tiled=True)]
    add x13 -> x3, other arithmetic: 38.1 us -> 1.71 us  [the longest x1 1.65 us: over_x_last(): self.result = take(at_x) + swap(take(1 - at_x), 'x')]
    concatenate x7 -> x3, other arithmetic: 20.9 us -> 1.5 us  [the longest x1 1.49 us: body(): mixed_grad = jnp.concatenate(mixed_grads, 0)]
    ppermute x29 -> x27, waiting for transfers between devices: 361 us -> 358 us  [swap(): return lax.ppermute(value, axis, [(0, 1), (1, 0)])]
  transfers between devices with their start and end apart: 39 -> 37, of which waited for: 13 -> 24; matrix products, arithmetic and copies ran while one was open for 56% -> 12% of each run, Pallas kernels for 0% -> 34%
where the time goes in v3:
time: 1090 us; the launch traced here: 1080 us
  waiting for transfers between devices  439 us (40%)
  Pallas kernels  424 us (39%)
  other arithmetic  124 us (11%)
  matrix products  35.9 us (3%)
  starting transfers between devices  29.1 us (3%)
  between operations  16.1 us (1%)
  local copies, waits for them, and re-layouts  13.3 us (1%)
    ppermute x27, waiting for transfers between devices, swap(): return lax.ppermute(value, axis, [(0, 1), (1, 0)])  358 us
    pallas_call x23, Pallas kernels, paired(): pl.pallas_call(kernel, grid_spec=pltpu.PrefetchScalarGridSpec(num_scalar_...  179 us
    pallas_call x4, Pallas kernels, hidden_step(): pl.pallas_call(kernel, grid=(local // block,), in_specs=[same, pl.BlockSp...  89.5 us
    reduce_scatter x7, waiting for transfers between devices, over_z(): lax.psum_scatter(total, 'z', scatter_dimension=self.dim, tiled=True)  80.8 us
    pallas_call x5, Pallas kernels, pieces(): pl.pallas_call(kernel, grid=(dps,), in_specs=[pl.BlockSpec((length, wide)...  51.9 us
    dot_general x9, matrix products, mm(): lax.dot_general(left, right, (contract, ((), ())), preferred_element_type...  35.9 us
    pallas_call x1, Pallas kernels, attend_pull(): pl.pallas_call(kernel, grid=(heads,), in_specs=[pl.BlockSpec(memory_space...  27.9 us
    pallas_call x1, Pallas kernels, product_down(): pl.pallas_call(kernel, grid=(cols // wide, inner // deep), in_specs=[pl.B...  27.9 us
  transfers between devices with their start and end apart: 37, of which 24 were waited for; matrix products, arithmetic and copies ran while one was open for 12% of the time, Pallas kernels for 34%

profile of v3, /device:TPU:0, one launch (start us, length us, event | category | flops | bytes accessed | tf_op | source)
XLA Modules:
  0.0 1081.5 jit_solution(11607658667947234364)
XLA Ops:
  34.0 10.4 shard_map.305
  53.9 13.4 %shard_map.306 = (bf16[512,1024]{1,0:T(8,128)(2,1)}, f32[8,512,1]{2,1,0:T(8,128)}) custom-call(s32[1]{0:T(128)S(6)} %copy.114.boundary_ref, bf16[1024,1024]{1,0:T(8,128)(2,1)} %add_convert_fusion.4.query_ref, bf16[1024,1024]{1,0:T(8,128)(2,1)} %convolution_convert_fusion.key_ref, bf16[1024,1024]{1,0:T(8,128)(2,1)} %add_convert_fusion.3.value_ref), custom_call_target="tpu_custom_call" | custom-call | tf_op jit(solution)/shard_map/pallas_call | solution.py:178
  81.3 10.4 shard_map.312.right_ref
  103.2 22.3 %shard_map.307 = (bf16[1024,4096]{1,0:T(8,128)(2,1)}, bf16[1024,4096]{1,0:T(8,128)(2,1)}, f32[512,2048]{1,0:T(8,128)}, f32[1,4096]{1,0:T(1,128)}) custom-call(bf16[256,2048]{1,0:T(8,128)(2,1)} %get-tuple-element.484.normed_ref, bf16[1024,2048]{1,0:T(8,128)(2,1)} %field_ref.3, bf16[2048,4096]{1,0:T(8,128)(2,1)} %up_ref.7, f32[1,4096]{1,0:T(1,128)} %bitcast.69, ...), custom_call_target="tpu_custom_call" | custom-call | tf_op jit(solution)/shard_map/pallas_call | solution.py:280
  125.5 17.2 %collective-permute-done.9 = f32[256,2048]{1,0:T(8,128)} collective-permute-done((f32[256,2048]{1,0:T(8,128)}, f32[256,2048]{1,0:T(8,128)}, u32[]{:S(2)}, u32[]{:S(2)}) %collective-permute-start.9) | collective-permute-done | bytes 2097184 | tf_op jit(solution)/shard_map/ppermute | solution.py:17
  149.4 22.3 %shard_map.308 = (bf16[1024,4096]{1,0:T(8,128)(2,1)}, bf16[1024,4096]{1,0:T(8,128)(2,1)}, f32[512,2048]{1,0:T(8,128)}, f32[1,4096]{1,0:T(1,128)}) custom-call(bf16[256,2048]{1,0:T(8,128)(2,1)} %get-tuple-element.480.normed_ref, bf16[1024,2048]{1,0:T(8,128)(2,1)} %field_ref.3, ...), custom_call_target="tpu_custom_call", output_to_operand_aliasing={{0}: (5, {}), {1}: (6, {}), {2}: (7, {})} | custom-call | tf_op jit(solution)/shard_map/pallas_call | solution.py:280
  171.7 15.9 %collective-permute-done.10 = f32[256,2048]{1,0:T(8,128)} collective-permute-done((f32[256,2048]{1,0:T(8,128)}, f32[256,2048]{1,0:T(8,128)}, u32[]{:S(2)}, u32[]{:S(2)}) %collective-permute-start.10) | collective-permute-done | bytes 2097184 | tf_op jit(solution)/shard_map/ppermute | solution.py:17
  194.4 22.5 %shard_map.309 = (bf16[1024,4096]{1,0:T(8,128)(2,1)}, bf16[1024,4096]{1,0:T(8,128)(2,1)}, f32[512,2048]{1,0:T(8,128)}, f32[1,4096]{1,0:T(1,128)}) custom-call(bf16[256,2048]{1,0:T(8,128)(2,1)} %get-tuple-element.476.normed_ref, bf16[1024,2048]{1,0:T(8,128)(2,1)} %field_ref.3, ...), custom_call_target="tpu_custom_call", output_to_operand_aliasing={{0}: (5, {}), {1}: (6, {})} | custom-call | tf_op jit(solution)/shard_map/pallas_call | solution.py:280
  216.9 14.8 %collective-permute-done.11 = f32[256,2048]{1,0:T(8,128)} collective-permute-done((f32[256,2048]{1,0:T(8,128)}, f32[256,2048]{1,0:T(8,128)}, u32[]{:S(2)}, u32[]{:S(2)}) %collective-permute-start.11) | collective-permute-done | bytes 2097184 | tf_op jit(solution)/shard_map/ppermute | solution.py:17
  238.5 22.3 %shard_map.310 = (bf16[1024,4096]{1,0:T(8,128)(2,1)}, bf16[1024,4096]{1,0:T(8,128)(2,1)}, f32[512,2048]{1,0:T(8,128)}, f32[1,4096]{1,0:T(1,128)}) custom-call(bf16[256,2048]{1,0:T(8,128)(2,1)} %get-tuple-element.472.normed_ref, bf16[1024,2048]{1,0:T(8,128)(2,1)} %field_ref.3, ...), custom_call_target="tpu_custom_call", output_to_operand_aliasing={{0}: (5, {}), {1}: (6, {}), {2}: (7, {})} | custom-call | tf_op jit(solution)/shard_map/pallas_call | solution.py:280
  260.9 9.8 shard_map.313
  270.7 13.5 %while.80 = (s32[]{:T(128)}, f32[2048,1024]{1,0:T(8,128)}, s32[]{:T(128)}, f32[2048,1024]{1,0:T(8,128)}, s32[]{:T(128)}) while((s32[]{:T(128)}, f32[2048,1024]{1,0:T(8,128)}, s32[]{:T(128)}, f32[2048,1024]{1,0:T(8,128)}, s32[]{:T(128)}) %tuple.285), condition=%wide.region_11.12_spmd, body=%wide.region_10.0_spmd.sunk | while | flops 2 | bytes 33554532 | solution.py:362
  270.7 13.5 %collective-permute-done = f32[2048,1024]{1,0:T(8,128)} collective-permute-done((f32[2048,1024]{1,0:T(8,128)}, f32[2048,1024]{1,0:T(8,128)}, u32[]{:S(2)}, u32[]{:S(2)}) %collective-permute-start) | collective-permute-done | bytes 8388640 | tf_op jit(solution)/shard_map/while/body/ppermute | solution.py:17
  284.2 11.9 %shard_map.314 = f32[2048,1024]{1,0:T(8,128)} custom-call(s32[4]{0:T(128)} %get-tuple-element.503.starts_ref, bf16[1024,4096]{1,0:T(8,128)(2,1)} %get-tuple-element.314.left_ref, bf16[1024,2048]{1,0:T(8,128)(2,1)} %shard_map.312.right_ref, f32[2048,1024]{1,0:T(8,128)} %get-tuple-element.298.rest_0_), custom_call_target="tpu_custom_call" | custom-call | tf_op jit(solution)/shard_map/pallas_call | solution.py:89
  298.2 10.4 shard_map.315.right_ref
  308.6 6.5 convert_element_type.66
  316.9 9.9 shard_map.316
  326.8 27.9 %shard_map.317 = f32[1024,2048]{1,0:T(8,128)} custom-call(bf16[1024,4096]{1,0:T(8,128)(2,1)} %get-tuple-element.314.left_ref, bf16[4096,2048]{1,0:T(8,128)(2,1)} %right_ref.1), custom_call_target="tpu_custom_call" | custom-call | tf_op jit(solution)/shard_map/pallas_call | solution.py:117
  358.2 10.4 shard_map.318.left_ref
  368.6 21.4 %collective-permute-done.14 = f32[512,2048]{1,0:T(8,128)} collective-permute-done((f32[512,2048]{1,0:T(8,128)}, f32[512,2048]{1,0:T(8,128)}, u32[]{:S(2)}, u32[]{:S(2)}) %collective-permute-start.14) | collective-permute-done | bytes 4194336 | tf_op jit(solution)/shard_map/ppermute | solution.py:17
  390.0 13.5 %while.81 = (s32[]{:T(128)}, f32[2048,1024]{1,0:T(8,128)}, s32[]{:T(128)}, f32[2048,1024]{1,0:T(8,128)}, s32[]{:T(128)}) while((s32[]{:T(128)}, f32[2048,1024]{1,0:T(8,128)}, s32[]{:T(128)}, f32[2048,1024]{1,0:T(8,128)}, s32[]{:T(128)}) %tuple.288), condition=%wide.region_13.14_spmd, body=%wide.region_12.13_spmd.sunk | while | flops 2 | bytes 33554532 | solution.py:362
  390.0 13.5 %collective-permute-done.1 = f32[2048,1024]{1,0:T(8,128)} collective-permute-done((f32[2048,1024]{1,0:T(8,128)}, f32[2048,1024]{1,0:T(8,128)}, u32[]{:S(2)}, u32[]{:S(2)}) %collective-permute-start.1) | collective-permute-done | bytes 8388640 | tf_op jit(solution)/shard_map/while/body/ppermute | solution.py:17
  403.5 8.5 shard_map.322
  427.4 11.4 %shard_map.323 = f32[1024,2048]{1,0:T(8,128)} custom-call(s32[4]{0:T(128)} %get-tuple-element.505.starts_ref, bf16[1024,2048]{1,0:T(8,128)(2,1)} %shard_map.318.left_ref, bf16[1024,4096]{1,0:T(8,128)(2,1)} %get-tuple-element.346.right_ref), custom_call_target="tpu_custom_call" | custom-call | tf_op jit(solution)/shard_map/pallas_call | solution.py:89
  438.8 11.5 %shard_map.324 = f32[1024,2048]{1,0:T(8,128)} custom-call(s32[4]{0:T(128)} %get-tuple-element.502.starts_ref, bf16[1024,2048]{1,0:T(8,128)(2,1)} %shard_map.318.left_ref, bf16[1024,4096]{1,0:T(8,128)(2,1)} %get-tuple-element.346.right_ref), custom_call_target="tpu_custom_call" | custom-call | tf_op jit(solution)/shard_map/pallas_call | solution.py:89
  450.3 28.8 %collective-permute-done.12 = f32[512,2048]{1,0:T(8,128)} collective-permute-done((f32[512,2048]{1,0:T(8,128)}, f32[512,2048]{1,0:T(8,128)}, u32[]{:S(2)}, u32[]{:S(2)}) %collective-permute-start.12) | collective-permute-done | bytes 4194336 | tf_op jit(solution)/shard_map/ppermute | solution.py:17
  494.5 10.5 collective-permute-done.15.rest_1_
  505.0 9.3 shard_map.327
  515.0 13.5 %while.82 = (s32[]{:T(128)}, f32[1024,2048]{1,0:T(8,128)}, s32[]{:T(128)}, f32[1024,2048]{1,0:T(8,128)}, s32[]{:T(128)}) while((s32[]{:T(128)}, f32[1024,2048]{1,0:T(8,128)}, s32[]{:T(128)}, f32[1024,2048]{1,0:T(8,128)}, s32[]{:T(128)}) %tuple.291), condition=%wide.region_19.20_spmd, body=%wide.region_18.19_spmd.sunk | while | flops 2 | bytes 33554532 | solution.py:362
  515.0 13.5 %collective-permute-done.2 = f32[1024,2048]{1,0:T(8,128)} collective-permute-done((f32[1024,2048]{1,0:T(8,128)}, f32[1024,2048]{1,0:T(8,128)}, u32[]{:S(2)}, u32[]{:S(2)}) %collective-permute-start.2) | collective-permute-done | bytes 8388640 | tf_op jit(solution)/shard_map/while/body/ppermute | solution.py:17
  528.5 7.5 shard_map.328
  539.8 13.5 %while.83 = (s32[]{:T(128)}, f32[1024,2048]{1,0:T(8,128)}, s32[]{:T(128)}, f32[1024,2048]{1,0:T(8,128)}, s32[]{:T(128)}) while((s32[]{:T(128)}, f32[1024,2048]{1,0:T(8,128)}, s32[]{:T(128)}, f32[1024,2048]{1,0:T(8,128)}, s32[]{:T(128)}) %tuple.294), condition=%wide.region_21.22_spmd, body=%wide.region_20.21_spmd.sunk | while | flops 2 | bytes 33554532 | solution.py:362
  539.8 13.5 %collective-permute-done.3 = f32[1024,2048]{1,0:T(8,128)} collective-permute-done((f32[1024,2048]{1,0:T(8,128)}, f32[1024,2048]{1,0:T(8,128)}, u32[]{:S(2)}, u32[]{:S(2)}) %collective-permute-start.3) | collective-permute-done | bytes 8388640 | tf_op jit(solution)/shard_map/while/body/ppermute | solution.py:17
  553.3 27.9 %shard_map.329 = (bf16[1024,1024]{1,0:T(8,128)(2,1)}, bf16[1024,1024]{1,0:T(8,128)(2,1)}, bf16[1024,1024]{1,0:T(8,128)(2,1)}, f32[8,1,128]{2,1,0:T(1,128)}, f32[8,1,128]{2,1,0:T(1,128)}) custom-call(s32[1]{0:T(128)S(6)} %copy.114.boundary_ref, bf16[1024,1024]{1,0:T(8,128)(2,1)} %add_convert_fusion.4.query_ref, ...), custom_call_target="tpu_custom_call" | custom-call | tf_op jit(solution)/shard_map/pallas_call | solution.py:237
  581.2 12.1 %shard_map.331 = f32[512,2048]{1,0:T(8,128)} custom-call(bf16[1024,1024]{1,0:T(8,128)(2,1)} %get-tuple-element.353.refs_0_.right_ref, bf16[1024,1024]{1,0:T(8,128)(2,1)} %get-tuple-element.357.refs_1_.right_ref, bf16[1024,1024]{1,0:T(8,128)(2,1)} %get-tuple-element.361.refs_2_.right_ref, bf16[2048,1024]{1,0:T(8,128)(2,1)} %refs_3_.3, ...), custom_call_target="tpu_custom_call" | custom-call | tf_op jit(solution)/shard_map/pallas_call | solution.py:141
  593.3 12.0 %shard_map.330 = f32[512,2048]{1,0:T(8,128)} custom-call(bf16[1024,1024]{1,0:T(8,128)(2,1)} %get-tuple-element.353.refs_0_.right_ref, bf16[1024,1024]{1,0:T(8,128)(2,1)} %get-tuple-element.357.refs_1_.right_ref, bf16[1024,1024]{1,0:T(8,128)(2,1)} %get-tuple-element.361.refs_2_.right_ref, bf16[2048,1024]{1,0:T(8,128)(2,1)} %refs_3_.3, ...), custom_call_target="tpu_custom_call" | custom-call | tf_op jit(solution)/shard_map/pallas_call | solution.py:141
  605.3 7.2 shard_map.332
  613.0 10.4 shard_map.320.left_ref
  632.1 10.4 shard_map.333.right_ref
  642.5 6.5 shard_map.334
  649.0 6.5 shard_map.335
  655.5 6.5 shard_map.336
  662.0 6.6 shard_map.337
  668.5 7.5 while.84
  668.5 7.5 collective-permute-done.4
  676.0 7.7 while.85
  676.2 7.4 collective-permute-done.5
  683.7 7.6 while.86
  684.0 7.4 collective-permute-done.6
  691.3 7.5 while.87
  691.5 7.4 collective-permute-done.7
  698.8 8.5 shard_map.341
  712.5 11.4 %fusion = bf16[1024,2048]{1,0:T(8,128)(2,1)} fusion(f32[256,2048]{1,0:T(8,128)} %copy-done.6, f32[256,2048]{1,0:T(8,128)} %copy-done.5, f32[256,2048]{1,0:T(8,128)} %copy-done.4, f32[256,2048]{1,0:T(8,128)S(1)} %copy-done.3, f32[1024,2048]{1,0:T(8,128)} %shard_map.317, f32[1024,2048]{1,0:T(8,128)} %collective-permute-done.13, f32[2048]{0:T(1024)S(1)} %copy-done.43), kind=kLoop, calls=%fused_computation.1 | loop fusion | flops 14680064 | bytes 29368320 | tf_op jit(solution)/shard_map/convert_element_type | solution.py:529
  723.9 8.5 shard_map.343
  743.4 40.0 %collective-permute-done.19.rest_1_ = f32[1024,512]{1,0:T(8,128)} collective-permute-done((f32[1024,512]{1,0:T(8,128)S(1)}, f32[1024,512]{1,0:T(8,128)}, u32[]{:S(2)}, u32[]{:S(2)}) %collective-permute-start.19) | collective-permute-done | bytes 2097184 | tf_op jit(solution)/shard_map/ppermute | solution.py:17
  795.1 30.9 %collective-permute-done.17 = f32[512,2048]{1,0:T(8,128)} collective-permute-done((f32[512,2048]{1,0:T(8,128)}, f32[512,2048]{1,0:T(8,128)}, u32[]{:S(2)}, u32[]{:S(2)}) %collective-permute-start.17) | collective-permute-done | bytes 4194336 | tf_op jit(solution)/shard_map/ppermute | solution.py:17
  834.9 6.5 shard_map.347
  854.4 60.5 %collective-permute-done.22 = f32[2048,128]{1,0:T(8,128)} collective-permute-done((f32[2048,128]{1,0:T(8,128)S(1)}, f32[2048,128]{1,0:T(8,128)}, u32[]{:S(2)}, u32[]{:S(2)}) %collective-permute-start.22) | collective-permute-done | bytes 1048608 | tf_op jit(solution)/shard_map/ppermute | solution.py:17
  916.6 6.5 shard_map.349
  923.0 10.6 collective-permute-done.20
  943.1 14.8 %collective-permute-done.28.rest_1_ = f32[512,1024]{1,0:T(8,128)} collective-permute-done((f32[512,1024]{1,0:T(8,128)}, f32[512,1024]{1,0:T(8,128)}, u32[]{:S(2)}, u32[]{:S(2)}) %collective-permute-start.28) | collective-permute-done | bytes 2097184 | tf_op jit(solution)/shard_map/ppermute | solution.py:17
  957.9 6.6 shard_map.350
  993.4 35.1 %reduce-scatter.15.cloned.1.call-done = f32[128,1024]{1,0:T(8,128)} async-done(((f32[512,1024]{1,0:T(8,128)}), f32[128,1024]{1,0:T(8,128)}) %reduce-scatter.15.cloned.1.call-update) | async-done | bytes 524304 | tf_op jit(solution)/shard_map/reduce_scatter | solution.py:398
  1028.5 45.7 %reduce-scatter.13.cloned.1.call-done = f32[128,1024]{1,0:T(8,128)} async-done(((f32[512,1024]{1,0:T(8,128)}), f32[128,1024]{1,0:T(8,128)}) %reduce-scatter.13.cloned.1.call-update) | async-done | bytes 524304 | tf_op jit(solution)/shard_map/reduce_scatter | solution.py:398
  (290 shorter events, 222.9 us)
Async XLA Ops:
  7.2 5.4 copy-start.26
  7.2 843.8 %reduce-scatter.9.cloned.1.call-start = ((), (), s32[]{:S(2)}) async-start(), calls=%async_computation.8 | async-start | bytes 10485760 | tf_op jit(solution)/shard_map/reduce_scatter | solution.py:403
  7.3 5.4 copy-start.42
  16.8 11.5 %copy-start.11 = (bf16[1024,2048]{1,0:T(8,128)(2,1)}, bf16[1024,2048]{1,0:T(8,128)(2,1)S(1)}, u32[]{:S(2)}) copy-start(bf16[1024,2048]{1,0:T(8,128)(2,1)S(1)} %get-tuple-element.489.field_ref) | copy-start | bytes 12582916
  16.8 5.7 copy-start.14
  16.8 5.7 copy-start.50
  22.5 5.8 copy-start.12
  22.5 5.8 copy-start.51
  44.4 6.8 copy-start.22
  44.4 6.8 copy-start.46
  48.1 49.6 %collective-permute-start.8 = (f32[256,2048]{1,0:T(8,128)S(1)}, f32[256,2048]{1,0:T(8,128)}, u32[]{:S(2)}, u32[]{:S(2)}) collective-permute-start(f32[256,2048]{1,0:T(8,128)S(1)} %fusion.7), channel_id=1, source_target_pairs={{0,1},{1,0},{2,3},{3,2},{4,5},{5,4},{6,7},{7,6},{8,9},{9,8},{10,11... | collective-permute-start | bytes 6291464 | tf_op jit(solution)/shard_map/ppermute | solution.py:17
  53.8 88.9 %collective-permute-start.9 = (f32[256,2048]{1,0:T(8,128)}, f32[256,2048]{1,0:T(8,128)}, u32[]{:S(2)}, u32[]{:S(2)}) collective-permute-start(f32[256,2048]{1,0:T(8,128)} %fusion.3), channel_id=1, source_target_pairs={{0,1},{1,0},{2,3},{3,2},{4,5},{5,4},{6,7},{7,6},{8,9},{9,8},{10,11... | collective-permute-start | bytes 6291464 | tf_op jit(solution)/shard_map/ppermute | solution.py:17
  67.3 7.0 copy-start.24
  67.3 7.0 copy-start.47
  72.4 115.3 %collective-permute-start.10 = (f32[256,2048]{1,0:T(8,128)}, f32[256,2048]{1,0:T(8,128)}, u32[]{:S(2)}, u32[]{:S(2)}) collective-permute-start(f32[256,2048]{1,0:T(8,128)} %fusion.1), channel_id=1, source_target_pairs={{0,1},{1,0},{2,3},{3,2},{4,5},{5,4},{6,7},{7,6},{8,9},{9,8},{10,11... | collective-permute-start | bytes 6291464 | tf_op jit(solution)/shard_map/ppermute | solution.py:17
  76.9 154.8 %collective-permute-start.11 = (f32[256,2048]{1,0:T(8,128)}, f32[256,2048]{1,0:T(8,128)}, u32[]{:S(2)}, u32[]{:S(2)}) collective-permute-start(f32[256,2048]{1,0:T(8,128)} %fusion.5), channel_id=1, source_target_pairs={{0,1},{1,0},{2,3},{3,2},{4,5},{5,4},{6,7},{7,6},{8,9},{9,8},{10,11... | collective-permute-start | bytes 6291464 | tf_op jit(solution)/shard_map/ppermute | solution.py:17
  81.3 16.5 %copy-start.28 = (f32[2048]{0:T(1024)S(1)}, f32[2048]{0:T(1024)}, u32[]{:S(2)}) copy-start(f32[2048]{0:T(1024)} %param.44) | copy-start | bytes 24580
  92.3 9.4 copy-start.25
  92.3 9.4 copy-start.29
  270.7 13.5 %collective-permute-start = (f32[2048,1024]{1,0:T(8,128)}, f32[2048,1024]{1,0:T(8,128)}, u32[]{:S(2)}, u32[]{:S(2)}) collective-permute-start(f32[2048,1024]{1,0:T(8,128)} %get-tuple-element.688), channel_id=1, source_target_pairs={{0,2},{2,0},{1,3},{3,1},{4,6},{6,4},{5,7},{7,5},{8,10},{10,8},{9,1... | collective-permute-start | bytes 25165832 | tf_op jit(solution)/shard_map/while/body/ppermute | solution.py:17
  296.1 684.1 %reduce-scatter.23.cloned.1.call-start = ((), (), s32[]{:S(2)}) async-start(), calls=%async_computation.15 | async-start | bytes 5242880 | tf_op jit(solution)/shard_map/reduce_scatter | solution.py:398
  296.2 93.8 %collective-permute-start.14 = (f32[512,2048]{1,0:T(8,128)}, f32[512,2048]{1,0:T(8,128)}, u32[]{:S(2)}, u32[]{:S(2)}) collective-permute-start(f32[512,2048]{1,0:T(8,128)} %get-tuple-element.306), channel_id=1, source_target_pairs={{0,1},{1,0},{2,3},{3,2},{4,5},{5,4},{6,7},{7,6},{8,9},{9,8},{10,11... | collective-permute-start | bytes 12582920 | tf_op jit(solution)/shard_map/ppermute | solution.py:17
  297.9 181.1 %collective-permute-start.12 = (f32[512,2048]{1,0:T(8,128)}, f32[512,2048]{1,0:T(8,128)}, u32[]{:S(2)}, u32[]{:S(2)}) collective-permute-start(f32[512,2048]{1,0:T(8,128)} %get-tuple-element.302), channel_id=1, source_target_pairs={{0,1},{1,0},{2,3},{3,2},{4,5},{5,4},{6,7},{7,6},{8,9},{9,8},{10,11... | collective-permute-start | bytes 12582920 | tf_op jit(solution)/shard_map/ppermute | solution.py:17
  326.8 27.9 %copy-start.17 = (bf16[256,2048]{1,0:T(8,128)(2,1)S(1)}, bf16[256,2048]{1,0:T(8,128)(2,1)}, u32[]{:S(2)}) copy-start(bf16[256,2048]{1,0:T(8,128)(2,1)} %get-tuple-element.480.normed_ref) | copy-start | bytes 3145732
  390.0 13.5 %collective-permute-start.1 = (f32[2048,1024]{1,0:T(8,128)}, f32[2048,1024]{1,0:T(8,128)}, u32[]{:S(2)}, u32[]{:S(2)}) collective-permute-start(f32[2048,1024]{1,0:T(8,128)} %get-tuple-element.692), channel_id=1, source_target_pairs={{0,2},{2,0},{1,3},{3,1},{4,6},{6,4},{5,7},{7,5},{8,10},{10,8},{9,1... | collective-permute-start | bytes 25165832 | tf_op jit(solution)/shard_map/while/body/ppermute | solution.py:17
  412.0 93.0 %collective-permute-start.15 = (f32[2048,512]{1,0:T(8,128)}, f32[2048,512]{1,0:T(8,128)}, u32[]{:S(2)}, u32[]{:S(2)}) collective-permute-start(f32[2048,512]{1,0:T(8,128)} %shard_map.322), channel_id=1, source_target_pairs={{0,4},{4,0},{1,5},{5,1},{2,6},{6,2},{3,7},{7,3},{8,12},{12,8},{9,1... | collective-permute-start | bytes 12582920 | tf_op jit(solution)/shard_map/ppermute | solution.py:17
  413.7 5.7 copy-start.9
  419.4 5.6 copy-start.48
  438.8 42.0 %copy-start.8 = (f32[256,2048]{1,0:T(8,128)S(1)}, f32[256,2048]{1,0:T(8,128)}, u32[]{:S(2)}) copy-start(f32[256,2048]{1,0:T(8,128)} %get-tuple-element.477) | copy-start | bytes 6291460
  479.0 233.4 %collective-permute-start.13 = (f32[1024,2048]{1,0:T(8,128)}, f32[1024,2048]{1,0:T(8,128)}, u32[]{:S(2)}, u32[]{:S(2)}) collective-permute-start(f32[1024,2048]{1,0:T(8,128)} %shard_map.317), channel_id=1, source_target_pairs={{0,1},{1,0},{2,3},{3,2},{4,5},{5,4},{6,7},{7,6},{8,9},{9,8},{10,11... | collective-permute-start | bytes 25165832 | tf_op jit(solution)/shard_map/ppermute | solution.py:17
  480.8 5.7 copy-start.10
  486.5 5.6 copy-start.49
  514.3 475.7 %reduce-scatter.21.cloned.1.call-start = ((), (), s32[]{:S(2)}) async-start(), calls=%async_computation.14 | async-start | bytes 5242880 | tf_op jit(solution)/shard_map/reduce_scatter | solution.py:398
  515.0 13.5 %collective-permute-start.2 = (f32[1024,2048]{1,0:T(8,128)}, f32[1024,2048]{1,0:T(8,128)}, u32[]{:S(2)}, u32[]{:S(2)}) collective-permute-start(f32[1024,2048]{1,0:T(8,128)} %get-tuple-element.696), channel_id=1, source_target_pairs={{0,2},{2,0},{1,3},{3,1},{4,6},{6,4},{5,7},{7,5},{8,10},{10,8},{9,1... | collective-permute-start | bytes 25165832 | tf_op jit(solution)/shard_map/while/body/ppermute | solution.py:17
  536.0 162.8 %collective-permute-start.16 = (f32[512,2048]{1,0:T(8,128)}, f32[512,2048]{1,0:T(8,128)}, u32[]{:S(2)}, u32[]{:S(2)}) collective-permute-start(f32[512,2048]{1,0:T(8,128)} %shard_map.328), channel_id=1, source_target_pairs={{0,4},{4,0},{1,5},{5,1},{2,6},{6,2},{3,7},{7,3},{8,12},{12,8},{9,1... | collective-permute-start | bytes 12582920 | tf_op jit(solution)/shard_map/ppermute | solution.py:17
  539.8 13.5 %collective-permute-start.3 = (f32[1024,2048]{1,0:T(8,128)}, f32[1024,2048]{1,0:T(8,128)}, u32[]{:S(2)}, u32[]{:S(2)}) collective-permute-start(f32[1024,2048]{1,0:T(8,128)} %get-tuple-element.700), channel_id=1, source_target_pairs={{0,2},{2,0},{1,3},{3,1},{4,6},{6,4},{5,7},{7,5},{8,10},{10,8},{9,1... | collective-permute-start | bytes 25165832 | tf_op jit(solution)/shard_map/while/body/ppermute | solution.py:17
  612.6 111.3 %collective-permute-start.18 = (f32[512,2048]{1,0:T(8,128)}, f32[512,2048]{1,0:T(8,128)}, u32[]{:S(2)}, u32[]{:S(2)}) collective-permute-start(f32[512,2048]{1,0:T(8,128)} %shard_map.332), channel_id=1, source_target_pairs={{0,4},{4,0},{1,5},{5,1},{2,6},{6,2},{3,7},{7,3},{8,12},{12,8},{9,1... | collective-permute-start | bytes 12582920 | tf_op jit(solution)/shard_map/ppermute | solution.py:17
  626.5 5.6 copy-start.7
  668.5 7.5 collective-permute-start.4
  676.0 7.5 collective-permute-start.5
  683.8 7.6 collective-permute-start.6
  691.3 7.5 collective-permute-start.7
  732.4 257.7 %reduce-scatter.19.cloned.1.call-start = ((), (), s32[]{:S(2)}) async-start(), calls=%async_computation.13 | async-start | bytes 5242880 | tf_op jit(solution)/shard_map/reduce_scatter | solution.py:398
  733.0 260.4 %reduce-scatter.11.cloned.1.call-start = ((), (), s32[]{:S(2)}) async-start(), calls=%async_computation.9 | async-start | bytes 2621440 | tf_op jit(solution)/shard_map/reduce_scatter | solution.py:398
  733.0 93.0 %collective-permute-start.17 = (f32[512,2048]{1,0:T(8,128)}, f32[512,2048]{1,0:T(8,128)}, u32[]{:S(2)}, u32[]{:S(2)}) collective-permute-start(f32[512,2048]{1,0:T(8,128)} %shard_map.330), channel_id=1, source_target_pairs={{0,1},{1,0},{2,3},{3,2},{4,5},{5,4},{6,7},{7,6},{8,9},{9,8},{10,11... | collective-permute-start | bytes 12582920 | tf_op jit(solution)/shard_map/ppermute | solution.py:17
  734.8 48.6 %collective-permute-start.19 = (f32[1024,512]{1,0:T(8,128)S(1)}, f32[1024,512]{1,0:T(8,128)}, u32[]{:S(2)}, u32[]{:S(2)}) collective-permute-start(f32[1024,512]{1,0:T(8,128)S(1)} %copy-done.21), channel_id=1, source_target_pairs={{0,4},{4,0},{1,5},{5,1},{2,6},{6,2},{3,7},{7,3},{8,12},{12,8},{9,1... | collective-permute-start | bytes 6291464 | tf_op jit(solution)/shard_map/ppermute | solution.py:17
  736.8 6.5 copy-start.31
  743.1 91.8 %collective-permute-start.21 = (f32[512,1024]{1,0:T(8,128)}, f32[512,1024]{1,0:T(8,128)}, u32[]{:S(2)}, u32[]{:S(2)}) collective-permute-start(f32[512,1024]{1,0:T(8,128)} %shard_map.344), channel_id=1, source_target_pairs={{0,4},{4,0},{1,5},{5,1},{2,6},{6,2},{3,7},{7,3},{8,12},{12,8},{9,1... | collective-permute-start | bytes 6291464 | tf_op jit(solution)/shard_map/ppermute | solution.py:17
  789.2 36.9 %copy-start.27 = (f32[2048]{0:T(1024)S(1)}, f32[2048]{0:T(1024)}, u32[]{:S(2)}) copy-start(f32[2048]{0:T(1024)} %param.36) | copy-start | bytes 24580
  826.0 5.9 copy-start.16
  841.4 152.0 %reduce-scatter.17.cloned.1.call-start = ((), (), s32[]{:S(2)}) async-start(), calls=%async_computation.12 | async-start | bytes 2621440 | tf_op jit(solution)/shard_map/reduce_scatter | solution.py:398
  841.4 92.1 %collective-permute-start.20 = (f32[512,2048]{1,0:T(8,128)}, f32[512,2048]{1,0:T(8,128)}, u32[]{:S(2)}, u32[]{:S(2)}) collective-permute-start(f32[512,2048]{1,0:T(8,128)} %shard_map.331), channel_id=1, source_target_pairs={{0,1},{1,0},{2,3},{3,2},{4,5},{5,4},{6,7},{7,6},{8,9},{9,8},{10,11... | collective-permute-start | bytes 12582920 | tf_op jit(solution)/shard_map/ppermute | solution.py:17
  843.3 185.2 %reduce-scatter.15.cloned.1.call-start = ((), (), s32[]{:S(2)}) async-start(), calls=%async_computation.11 | async-start | bytes 2621440 | tf_op jit(solution)/shard_map/reduce_scatter | solution.py:398
  843.6 73.0 %collective-permute-start.23 = (f32[512,1024]{1,0:T(8,128)}, f32[512,1024]{1,0:T(8,128)}, u32[]{:S(2)}, u32[]{:S(2)}) collective-permute-start(f32[512,1024]{1,0:T(8,128)} %shard_map.346), channel_id=1, source_target_pairs={{0,4},{4,0},{1,5},{5,1},{2,6},{6,2},{3,7},{7,3},{8,12},{12,8},{9,1... | collective-permute-start | bytes 6291464 | tf_op jit(solution)/shard_map/ppermute | solution.py:17
  852.3 62.6 %collective-permute-start.22 = (f32[2048,128]{1,0:T(8,128)S(1)}, f32[2048,128]{1,0:T(8,128)}, u32[]{:S(2)}, u32[]{:S(2)}) collective-permute-start(f32[2048,128]{1,0:T(8,128)S(1)} %constant_dynamic-slice_fusion.5), channel_id=1, source_target_pairs={{0,4},{4,0},{1,5},{5,1},{2,6},{6,2},{3,7},{7,3},{8,12},{12,8},{9,1... | collective-permute-start | bytes 3145736 | tf_op jit(solution)/shard_map/ppermute | solution.py:17
  852.8 105.1 %collective-permute-start.28 = (f32[512,1024]{1,0:T(8,128)}, f32[512,1024]{1,0:T(8,128)}, u32[]{:S(2)}, u32[]{:S(2)}) collective-permute-start(f32[512,1024]{1,0:T(8,128)} %shard_map.348), channel_id=1, source_target_pairs={{0,4},{4,0},{1,5},{5,1},{2,6},{6,2},{3,7},{7,3},{8,12},{12,8},{9,1... | collective-permute-start | bytes 6291464 | tf_op jit(solution)/shard_map/ppermute | solution.py:17
  923.0 16.2 %copy-start.15 = (f32[512,2048]{1,0:T(8,128)S(1)}, f32[512,2048]{1,0:T(8,128)}, u32[]{:S(2)}) copy-start(f32[512,2048]{1,0:T(8,128)} %get-tuple-element.464) | copy-start | bytes 12582916
  964.5 5.8 copy-start.45
  964.5 6.6 copy-start.44
  964.6 109.6 %reduce-scatter.13.cloned.1.call-start = ((), (), s32[]{:S(2)}) async-start(), calls=%async_computation.10 | async-start | bytes 2621440 | tf_op jit(solution)/shard_map/reduce_scatter | solution.py:398
  972.3 1.3 collective-permute-start.24
  973.7 3.8 collective-permute-start.25
  977.6 5.5 collective-permute-start.26
  983.1 4.2 collective-permute-start.27
  (25 other events, 90.2 us)
Sparse Core Ops, SparseCore 0:
  296.2 146.0 reduce-scatter.8
  514.4 78.2 reduce-scatter.22
  732.5 78.1 reduce-scatter.20
  812.9 77.2 reduce-scatter.18
  892.9 44.1 reduce-scatter.10
  939.8 42.8 reduce-scatter.16
  985.5 42.9 reduce-scatter.14
  1031.3 42.8 reduce-scatter.12

commit v4 on v3

--- a/solution.py
+++ b/solution.py
@@ -354,9 +354,9 @@
 
     once = jnp.minimum(prefix_len[0], 1)
 
-    def swap_now(value):
+    def swap_now(value, axis):
         def step(state):
-            return (state[0] + 1, state[1], swap(after(state[1], state[0]), "c"))
+            return (state[0] + 1, state[1], swap(after(state[1], state[0]), axis))
 
         start = (jnp.int32(0), value, blank(value.shape))
         return lax.while_loop(lambda state: state[0] < once, step, start)[2]
@@ -383,7 +383,7 @@
             return own
 
         def meet(self, *gate):
-            self.near = swap_now(after(self.own, *gate))
+            self.near = swap_now(after(self.own, *gate), "c")
             return self.near
 
         def over_x(self, *gate):
@@ -487,18 +487,20 @@
     gate = downs[0].meet(gate)
     gate = downs[0].over_z_first(gate)
     gate = downs[1].over_cores(gate)
+    gate = downs[1].meet(gate)
+    gate = downs[1].over_x(gate)
+    gate = ups[0].over_cores(gate)
+    gate = ups[0].meet(gate)
+    gate = ups[0].over_x(gate)
+    gate = downs[1].over_z(gate, share_others[0])
+    gate = norm2_pull(0, gate)
     branch = product_down(after(acts, gate), down_weight)
-    gate = downs[1].meet(branch, share_others[0])
-    gate = downs[1].over_x(gate)
-    gate = norm2_pull(0, gate)
-    gate = ups[0].over_cores(gate)
-    gate = ups[1].over_cores(gate)
+    gate = ups[1].over_cores(branch)
     gate = norm2_pull(1, gate)
     branch_other = swap(after(branch, share_others[-1]), "mp")
-    gate = downs[1].over_z(gate)
-    gate = ups[0].meet(gate)
-    gate = ups[0].over_x(gate)
     gate = ups[1].meet(gate)
+    gate = ups[1].over_x(gate)
+    gate = ups[0].over_z(gate)
     mixed_grad = jnp.concatenate(mixed_grads, 0)
     attn_grad = jnp.concatenate(attn_grads, 0)
     query_grad, key_grad, value_grad, query_bias_grad, value_bias_grad = attend_pull(
@@ -506,11 +508,13 @@
     )
     gate = query_bias_grad
 
-    half_rows = length // 2
+    spans = [(0, 3 * length // 4), (3 * length // 4, length)]
+    resid_grad = jnp.concatenate(resid_grads, 0)
     norm1_parts = []
     pulls = [after(query_grad, gate), key_grad, value_grad]
-    for index in range(2):
-        norm1_parts.append(product_back(pulls, [query_weight, key_weight, value_weight], half_rows, index))
+    for begin, end in spans:
+        rows = end - begin
+        norm1_parts.append(product_back(pulls, [query_weight, key_weight, value_weight], rows, begin // rows))
     norm1_others = [swap(piece, "mp") for piece in norm1_parts]
 
     normed_pieces = pieces(normed)
@@ -518,13 +522,12 @@
     query_sum, key_sum, value_sum = [
         Sum(normed_pieces, pull, True) for pull in (query_grad, key_grad, value_grad)
     ]
-    gate = ups[1].over_x(*norm1_parts)
     sums = [out_sum, query_sum, key_sum, value_sum]
     for item in sums:
-        gate = item.over_cores(gate)
+        gate = item.over_cores(*norm1_parts)
+    gate = sums[-1].own
     for item in sums:
         gate = item.meet(gate)
-    gate = ups[0].over_z(gate)
     gate = out_sum.over_x(gate)
     outputs = (jnp.concatenate(resids, 0) + ((branch + after(branch_other, gate)) + down_bias)).astype(BF16)
     gate = ups[1].over_z(outputs)
@@ -537,20 +540,21 @@
 
     def norm1_pull(index, gate):
         nonlocal norm1_gain_grad, norm1_bias_grad
-        rows = slice(index * half_rows, (index + 1) * half_rows)
+        rows = slice(*spans[index])
         norm1_in = norm1_parts[index] + after(norm1_others[index], gate)
         norm1_bias_grad = norm1_bias_grad + jnp.sum(norm1_in, 0)
         norm1_gain_grad = norm1_gain_grad + jnp.sum(norm1_in * unit1[rows], 0)
         pulled = norm_pull(norm1_in, unit1[rows], scale1[rows], norm1_gain)
-        in_grads.append((resid_grads[index] + pulled).astype(BF16))
+        in_grads.append((resid_grad[rows] + pulled).astype(BF16))
         return in_grads[-1]
 
-    gate = norm1_pull(0, gate)
     gate = query_sum.over_z(gate)
     gate = value_sum.over_x(gate)
-    gate = downs[0].over_x_last(gate)
+    downs[0].over_x_last(gate)
+    gate = norm1_pull(0, gate)
     gate = key_sum.over_z(gate)
     gate = norm1_pull(1, gate)
+    gate = value_sum.over_z(gate)
     in_grad = jnp.concatenate(in_grads, 0)
 
     def blocks(vector, lead):
@@ -591,7 +595,6 @@
         small = mine + lax.ppermute(other, "z", pairs)
     small = small.reshape(-1)
 
-    gate = value_sum.over_z(gate)
     down_weight_grad = jnp.concatenate([item.result for item in downs], 0)
     up_weight_grad = jnp.concatenate([item.result for item in ups], 1)
 

time: 1090 us -> 1060 us (0.972)
  waiting for transfers between devices: 439 us -> 401 us
    reduce_scatter x7, waiting for transfers between devices: 80.8 us -> 29.8 us  [over_z(): lax.psum_scatter(total, 'z', scatter_dimension=self.dim, tiled=True)]
  transfers between devices with their start and end apart: 37 -> 37, of which waited for: 24 -> 23; matrix products, arithmetic and copies ran while one was open for 12% -> 13% of each run, Pallas kernels for 34% -> 35%
where the time goes in v4:
time: 1060 us; the launch traced here: 1050 us
  Pallas kernels  423 us (40%)
  waiting for transfers between devices  401 us (38%)
  other arithmetic  126 us (12%)
  matrix products  37.9 us (4%)
  starting transfers between devices  24.2 us (2%)
  local copies, waits for them, and re-layouts  19.2 us (2%)
  between operations  16.1 us (2%)
    ppermute x27, waiting for transfers between devices, swap(): return lax.ppermute(value, axis, [(0, 1), (1, 0)])  367 us
    pallas_call x23, Pallas kernels, paired(): pl.pallas_call(kernel, grid_spec=pltpu.PrefetchScalarGridSpec(num_scalar_...  177 us
    pallas_call x4, Pallas kernels, hidden_step(): pl.pallas_call(kernel, grid=(local // block,), in_specs=[same, pl.BlockSp...  89.5 us
    pallas_call x5, Pallas kernels, pieces(): pl.pallas_call(kernel, grid=(dps,), in_specs=[pl.BlockSpec((length, wide)...  52 us
    dot_general x9, matrix products, mm(): lax.dot_general(left, right, (contract, ((), ())), preferred_element_type...  37.9 us
    reduce_scatter x7, waiting for transfers between devices, over_z(): lax.psum_scatter(total, 'z', scatter_dimension=self.dim, tiled=True)  29.8 us
    pallas_call x1, Pallas kernels, attend_pull(): pl.pallas_call(kernel, grid=(heads,), in_specs=[pl.BlockSpec(memory_space...  27.9 us
    pallas_call x1, Pallas kernels, product_down(): pl.pallas_call(kernel, grid=(cols // wide, inner // deep), in_specs=[pl.B...  27.7 us
  transfers between devices with their start and end apart: 37, of which 23 were waited for; matrix products, arithmetic and copies ran while one was open for 13% of the time, Pallas kernels for 35%

profile of v4, /device:TPU:0, one launch (start us, length us, event | category | flops | bytes accessed | tf_op | source)
XLA Modules:
  0.0 1047.2 jit_solution(1124877495781415539)
XLA Ops:
  34.0 10.4 shard_map.305
  53.9 13.4 %shard_map.306 = (bf16[512,1024]{1,0:T(8,128)(2,1)}, f32[8,512,1]{2,1,0:T(8,128)}) custom-call(s32[1]{0:T(128)S(6)} %copy.114.boundary_ref, bf16[1024,1024]{1,0:T(8,128)(2,1)} %add_convert_fusion.2.query_ref, bf16[1024,1024]{1,0:T(8,128)(2,1)} %convolution_convert_fusion.key_ref, bf16[1024,1024]{1,0:T(8,128)(2,1)} %add_convert_fusion.1.value_ref), custom_call_target="tpu_custom_call" | custom-call | tf_op jit(solution)/shard_map/pallas_call | solution.py:178
  81.3 10.4 shard_map.315.right_ref
  103.2 22.3 %shard_map.307 = (bf16[1024,4096]{1,0:T(8,128)(2,1)}, bf16[1024,4096]{1,0:T(8,128)(2,1)}, f32[512,2048]{1,0:T(8,128)}, f32[1,4096]{1,0:T(1,128)}) custom-call(bf16[256,2048]{1,0:T(8,128)(2,1)} %get-tuple-element.480.normed_ref, bf16[1024,2048]{1,0:T(8,128)(2,1)} %field_ref.3, bf16[2048,4096]{1,0:T(8,128)(2,1)} %up_ref.7, f32[1,4096]{1,0:T(1,128)} %bitcast.72, ...), custom_call_target="tpu_custom_call" | custom-call | tf_op jit(solution)/shard_map/pallas_call | solution.py:280
  125.6 17.1 %collective-permute-done.9 = f32[256,2048]{1,0:T(8,128)} collective-permute-done((f32[256,2048]{1,0:T(8,128)}, f32[256,2048]{1,0:T(8,128)}, u32[]{:S(2)}, u32[]{:S(2)}) %collective-permute-start.9) | collective-permute-done | bytes 2097184 | tf_op jit(solution)/shard_map/ppermute | solution.py:17
  149.4 22.3 %shard_map.308 = (bf16[1024,4096]{1,0:T(8,128)(2,1)}, bf16[1024,4096]{1,0:T(8,128)(2,1)}, f32[512,2048]{1,0:T(8,128)}, f32[1,4096]{1,0:T(1,128)}) custom-call(bf16[256,2048]{1,0:T(8,128)(2,1)} %get-tuple-element.476.normed_ref, bf16[1024,2048]{1,0:T(8,128)(2,1)} %field_ref.3, ...), custom_call_target="tpu_custom_call", output_to_operand_aliasing={{0}: (5, {}), {1}: (6, {}), {2}: (7, {})} | custom-call | tf_op jit(solution)/shard_map/pallas_call | solution.py:280
  171.7 15.9 %collective-permute-done.10 = f32[256,2048]{1,0:T(8,128)} collective-permute-done((f32[256,2048]{1,0:T(8,128)}, f32[256,2048]{1,0:T(8,128)}, u32[]{:S(2)}, u32[]{:S(2)}) %collective-permute-start.10) | collective-permute-done | bytes 2097184 | tf_op jit(solution)/shard_map/ppermute | solution.py:17
  194.5 22.5 %shard_map.309 = (bf16[1024,4096]{1,0:T(8,128)(2,1)}, bf16[1024,4096]{1,0:T(8,128)(2,1)}, f32[512,2048]{1,0:T(8,128)}, f32[1,4096]{1,0:T(1,128)}) custom-call(bf16[256,2048]{1,0:T(8,128)(2,1)} %get-tuple-element.472.normed_ref, bf16[1024,2048]{1,0:T(8,128)(2,1)} %field_ref.3, ...), custom_call_target="tpu_custom_call", output_to_operand_aliasing={{0}: (5, {}), {1}: (6, {})} | custom-call | tf_op jit(solution)/shard_map/pallas_call | solution.py:280
  217.0 14.7 %collective-permute-done.11 = f32[256,2048]{1,0:T(8,128)} collective-permute-done((f32[256,2048]{1,0:T(8,128)}, f32[256,2048]{1,0:T(8,128)}, u32[]{:S(2)}, u32[]{:S(2)}) %collective-permute-start.11) | collective-permute-done | bytes 2097184 | tf_op jit(solution)/shard_map/ppermute | solution.py:17
  238.5 22.3 %shard_map.310 = (bf16[1024,4096]{1,0:T(8,128)(2,1)}, bf16[1024,4096]{1,0:T(8,128)(2,1)}, f32[512,2048]{1,0:T(8,128)}, f32[1,4096]{1,0:T(1,128)}) custom-call(bf16[256,2048]{1,0:T(8,128)(2,1)} %get-tuple-element.468.normed_ref, bf16[1024,2048]{1,0:T(8,128)(2,1)} %field_ref.3, ...), custom_call_target="tpu_custom_call", output_to_operand_aliasing={{0}: (5, {}), {1}: (6, {}), {2}: (7, {})} | custom-call | tf_op jit(solution)/shard_map/pallas_call | solution.py:280
  260.9 9.8 shard_map.316
  270.7 13.5 %while.80 = (s32[]{:T(128)}, f32[2048,1024]{1,0:T(8,128)}, s32[]{:T(128)}, f32[2048,1024]{1,0:T(8,128)}, s32[]{:T(128)}) while((s32[]{:T(128)}, f32[2048,1024]{1,0:T(8,128)}, s32[]{:T(128)}, f32[2048,1024]{1,0:T(8,128)}, s32[]{:T(128)}) %tuple.282), condition=%wide.region_11.12_spmd, body=%wide.region_10.0_spmd.sunk | while | flops 2 | bytes 33554532 | solution.py:362
  270.7 13.5 %collective-permute-done = f32[2048,1024]{1,0:T(8,128)} collective-permute-done((f32[2048,1024]{1,0:T(8,128)}, f32[2048,1024]{1,0:T(8,128)}, u32[]{:S(2)}, u32[]{:S(2)}) %collective-permute-start) | collective-permute-done | bytes 8388640 | tf_op jit(solution)/shard_map/while/body/ppermute | solution.py:17
  284.2 11.9 %shard_map.317 = f32[2048,1024]{1,0:T(8,128)} custom-call(s32[4]{0:T(128)} %get-tuple-element.498.starts_ref, bf16[1024,4096]{1,0:T(8,128)(2,1)} %get-tuple-element.310.left_ref, bf16[1024,2048]{1,0:T(8,128)(2,1)} %shard_map.315.right_ref, f32[2048,1024]{1,0:T(8,128)} %get-tuple-element.299.rest_0_), custom_call_target="tpu_custom_call" | custom-call | tf_op jit(solution)/shard_map/pallas_call | solution.py:89
  296.2 10.5 %shard_map.318.right_ref = bf16[1024,2048]{1,0:T(8,128)(2,1)} custom-call(bf16[1024,2048]{1,0:T(8,128)(2,1)} %field_ref.3), custom_call_target="tpu_custom_call" | custom-call | tf_op jit(solution)/shard_map/pallas_call | solution.py:347
  307.2 9.9 shard_map.319
  317.2 13.5 %while.81 = (s32[]{:T(128)}, f32[2048,1024]{1,0:T(8,128)}, s32[]{:T(128)}, f32[2048,1024]{1,0:T(8,128)}, s32[]{:T(128)}) while((s32[]{:T(128)}, f32[2048,1024]{1,0:T(8,128)}, s32[]{:T(128)}, f32[2048,1024]{1,0:T(8,128)}, s32[]{:T(128)}) %tuple.285), condition=%wide.region_13.14_spmd, body=%wide.region_12.13_spmd.sunk | while | flops 2 | bytes 33554532 | solution.py:362
  317.3 13.4 %collective-permute-done.1 = f32[2048,1024]{1,0:T(8,128)} collective-permute-done((f32[2048,1024]{1,0:T(8,128)}, f32[2048,1024]{1,0:T(8,128)}, u32[]{:S(2)}, u32[]{:S(2)}) %collective-permute-start.1) | collective-permute-done | bytes 8388640 | tf_op jit(solution)/shard_map/while/body/ppermute | solution.py:17
  330.7 8.2 shard_map.320
  346.9 10.4 shard_map.311.left_ref
  357.3 11.4 %shard_map.321 = f32[1024,2048]{1,0:T(8,128)} custom-call(s32[4]{0:T(128)} %get-tuple-element.500.starts_ref, bf16[1024,2048]{1,0:T(8,128)(2,1)} %shard_map.311.left_ref, bf16[1024,4096]{1,0:T(8,128)(2,1)} %get-tuple-element.342.right_ref), custom_call_target="tpu_custom_call" | custom-call | tf_op jit(solution)/shard_map/pallas_call | solution.py:89
  368.7 13.5 %while.82 = (s32[]{:T(128)}, f32[1024,2048]{1,0:T(8,128)}, s32[]{:T(128)}, f32[1024,2048]{1,0:T(8,128)}, s32[]{:T(128)}) while((s32[]{:T(128)}, f32[1024,2048]{1,0:T(8,128)}, s32[]{:T(128)}, f32[1024,2048]{1,0:T(8,128)}, s32[]{:T(128)}) %tuple.288), condition=%wide.region_15.16_spmd, body=%wide.region_14.15_spmd.sunk | while | flops 2 | bytes 33554532 | solution.py:362
  368.7 13.5 %collective-permute-done.2 = f32[1024,2048]{1,0:T(8,128)} collective-permute-done((f32[1024,2048]{1,0:T(8,128)}, f32[1024,2048]{1,0:T(8,128)}, u32[]{:S(2)}, u32[]{:S(2)}) %collective-permute-start.2) | collective-permute-done | bytes 8388640 | tf_op jit(solution)/shard_map/while/body/ppermute | solution.py:17
  382.2 7.1 shard_map.322
  389.2 42.6 %collective-permute-done.13.rest_1_ = f32[2048,512]{1,0:T(8,128)} collective-permute-done((f32[2048,512]{1,0:T(8,128)}, f32[2048,512]{1,0:T(8,128)}, u32[]{:S(2)}, u32[]{:S(2)}) %collective-permute-start.13) | collective-permute-done | bytes 4194336 | tf_op jit(solution)/shard_map/ppermute | solution.py:17
  433.2 9.4 shard_map.323
  444.3 6.5 convert_element_type.66
  452.5 6.1 multiply_reduce_fusion.5
  468.3 27.7 %shard_map.324 = f32[1024,2048]{1,0:T(8,128)} custom-call(bf16[1024,4096]{1,0:T(8,128)(2,1)} %get-tuple-element.310.left_ref, bf16[4096,2048]{1,0:T(8,128)(2,1)} %right_ref.1), custom_call_target="tpu_custom_call" | custom-call | tf_op jit(solution)/shard_map/pallas_call | solution.py:117
  496.0 11.4 %shard_map.327 = f32[1024,2048]{1,0:T(8,128)} custom-call(s32[4]{0:T(128)} %get-tuple-element.496.starts_ref, bf16[1024,2048]{1,0:T(8,128)(2,1)} %shard_map.311.left_ref, bf16[1024,4096]{1,0:T(8,128)(2,1)} %get-tuple-element.342.right_ref), custom_call_target="tpu_custom_call" | custom-call | tf_op jit(solution)/shard_map/pallas_call | solution.py:89
  507.4 27.3 %collective-permute-done.14 = f32[512,2048]{1,0:T(8,128)} collective-permute-done((f32[512,2048]{1,0:T(8,128)}, f32[512,2048]{1,0:T(8,128)}, u32[]{:S(2)}, u32[]{:S(2)}) %collective-permute-start.14) | collective-permute-done | bytes 4194336 | tf_op jit(solution)/shard_map/ppermute | solution.py:17
  549.8 13.5 %while.83 = (s32[]{:T(128)}, f32[1024,2048]{1,0:T(8,128)}, s32[]{:T(128)}, f32[1024,2048]{1,0:T(8,128)}, s32[]{:T(128)}) while((s32[]{:T(128)}, f32[1024,2048]{1,0:T(8,128)}, s32[]{:T(128)}, f32[1024,2048]{1,0:T(8,128)}, s32[]{:T(128)}) %tuple.291), condition=%wide.region_21.22_spmd, body=%wide.region_20.21_spmd.sunk | while | flops 2 | bytes 33554532 | solution.py:362
  549.8 13.5 %collective-permute-done.3 = f32[1024,2048]{1,0:T(8,128)} collective-permute-done((f32[1024,2048]{1,0:T(8,128)}, f32[1024,2048]{1,0:T(8,128)}, u32[]{:S(2)}, u32[]{:S(2)}) %collective-permute-start.3) | collective-permute-done | bytes 8388640 | tf_op jit(solution)/shard_map/while/body/ppermute | solution.py:17
  563.3 7.3 shard_map.329
  570.5 8.3 shard_map.330
  579.4 10.4 shard_map.326.left_ref
  596.2 27.9 %shard_map.331 = (bf16[1024,1024]{1,0:T(8,128)(2,1)}, bf16[1024,1024]{1,0:T(8,128)(2,1)}, bf16[1024,1024]{1,0:T(8,128)(2,1)}, f32[8,1,128]{2,1,0:T(1,128)}, f32[8,1,128]{2,1,0:T(1,128)}) custom-call(s32[1]{0:T(128)S(6)} %copy.114.boundary_ref, bf16[1024,1024]{1,0:T(8,128)(2,1)} %add_convert_fusion.2.query_ref, ...), custom_call_target="tpu_custom_call" | custom-call | tf_op jit(solution)/shard_map/pallas_call | solution.py:237
  624.2 8.9 shard_map.333
  633.1 15.6 %shard_map.332 = f32[768,2048]{1,0:T(8,128)} custom-call(bf16[1024,1024]{1,0:T(8,128)(2,1)} %get-tuple-element.348.refs_0_.right_ref, bf16[1024,1024]{1,0:T(8,128)(2,1)} %get-tuple-element.352.refs_1_.right_ref, bf16[1024,1024]{1,0:T(8,128)(2,1)} %get-tuple-element.356.refs_2_.right_ref, bf16[2048,1024]{1,0:T(8,128)(2,1)} %refs_3_.3, ...), custom_call_target="tpu_custom_call" | custom-call | tf_op jit(solution)/shard_map/pallas_call | solution.py:141
  653.0 10.3 shard_map.340.right_ref
  663.3 6.5 shard_map.341
  669.8 6.5 shard_map.334
  676.3 6.5 shard_map.338
  682.8 7.5 while.84
  682.8 7.5 collective-permute-done.4
  690.3 6.5 shard_map.336
  696.8 7.7 while.85
  696.9 7.4 collective-permute-done.5
  704.5 7.6 while.86
  704.7 7.4 collective-permute-done.6
  712.1 7.5 while.87
  712.2 7.4 collective-permute-done.7
  724.8 11.4 %fusion = bf16[1024,2048]{1,0:T(8,128)(2,1)} fusion(f32[256,2048]{1,0:T(8,128)} %copy-done.6, f32[256,2048]{1,0:T(8,128)} %copy-done.5, f32[256,2048]{1,0:T(8,128)} %copy-done.4, f32[256,2048]{1,0:T(8,128)S(1)} %copy-done.3, f32[1024,2048]{1,0:T(8,128)} %shard_map.324, f32[1024,2048]{1,0:T(8,128)} %collective-permute-done.15, f32[2048]{0:T(1024)S(1)} %copy-done.43), kind=kLoop, calls=%fused_computation.1 | loop fusion | flops 14680064 | bytes 29368320 | tf_op jit(solution)/shard_map/convert_element_type | solution.py:532
  736.1 8.3 shard_map.343
  754.5 40.2 %collective-permute-done.19.rest_1_ = f32[1024,512]{1,0:T(8,128)} collective-permute-done((f32[1024,512]{1,0:T(8,128)S(1)}, f32[1024,512]{1,0:T(8,128)}, u32[]{:S(2)}, u32[]{:S(2)}) %collective-permute-start.19) | collective-permute-done | bytes 2097184 | tf_op jit(solution)/shard_map/ppermute | solution.py:17
  807.9 31.6 %collective-permute-done.20.rest_1_ = f32[512,1024]{1,0:T(8,128)} collective-permute-done((f32[512,1024]{1,0:T(8,128)}, f32[512,1024]{1,0:T(8,128)}, u32[]{:S(2)}, u32[]{:S(2)}) %collective-permute-start.20) | collective-permute-done | bytes 2097184 | tf_op jit(solution)/shard_map/ppermute | solution.py:17
  839.6 6.4 shard_map.347
  852.0 30.5 %collective-permute-done.17 = f32[768,2048]{1,0:T(8,128)} collective-permute-done((f32[768,2048]{1,0:T(8,128)}, f32[768,2048]{1,0:T(8,128)}, u32[]{:S(2)}, u32[]{:S(2)}) %collective-permute-start.17) | collective-permute-done | bytes 6291488 | tf_op jit(solution)/shard_map/ppermute | solution.py:17
  882.5 7.9 multiply_reduce_fusion.1
  897.5 6.6 shard_map.349
  912.6 38.6 %collective-permute-done.21 = f32[256,2048]{1,0:T(8,128)} collective-permute-done((f32[256,2048]{1,0:T(8,128)S(1)}, f32[256,2048]{1,0:T(8,128)}, u32[]{:S(2)}, u32[]{:S(2)}) %collective-permute-start.21) | collective-permute-done | bytes 2097184 | tf_op jit(solution)/shard_map/ppermute | solution.py:17
  963.1 6.5 shard_map.350
  985.2 17.4 %collective-permute-done.28 = f32[2048,128]{1,0:T(8,128)} collective-permute-done((f32[2048,128]{1,0:T(8,128)}, f32[2048,128]{1,0:T(8,128)}, u32[]{:S(2)}, u32[]{:S(2)}) %collective-permute-start.28) | collective-permute-done | bytes 1048608 | tf_op jit(solution)/shard_map/ppermute | solution.py:17
  1010.1 29.8 %reduce-scatter.13.cloned.1.call-done = f32[128,1024]{1,0:T(8,128)} async-done(((f32[512,1024]{1,0:T(8,128)}), f32[128,1024]{1,0:T(8,128)}) %reduce-scatter.13.cloned.1.call-update) | async-done | bytes 524304 | tf_op jit(solution)/shard_map/reduce_scatter | solution.py:398
  (295 shorter events, 215.7 us)
Async XLA Ops:
  7.2 969.0 %reduce-scatter.21.cloned.1.call-start = ((), (), s32[]{:S(2)}) async-start(), calls=%async_computation.14 | async-start | bytes 10485760 | tf_op jit(solution)/shard_map/reduce_scatter | solution.py:403
  16.8 11.5 %copy-start.13 = (bf16[1024,2048]{1,0:T(8,128)(2,1)}, bf16[1024,2048]{1,0:T(8,128)(2,1)S(1)}, u32[]{:S(2)}) copy-start(bf16[1024,2048]{1,0:T(8,128)(2,1)S(1)} %get-tuple-element.485.field_ref) | copy-start | bytes 12582916
  22.5 5.8 copy-start.14
  22.5 5.8 copy-start.51
  44.4 6.8 copy-start.25
  44.4 6.8 copy-start.46
  48.1 49.6 %collective-permute-start.8 = (f32[256,2048]{1,0:T(8,128)S(1)}, f32[256,2048]{1,0:T(8,128)}, u32[]{:S(2)}, u32[]{:S(2)}) collective-permute-start(f32[256,2048]{1,0:T(8,128)S(1)} %fusion.10), channel_id=1, source_target_pairs={{0,1},{1,0},{2,3},{3,2},{4,5},{5,4},{6,7},{7,6},{8,9},{9,8},{10,11... | collective-permute-start | bytes 6291464 | tf_op jit(solution)/shard_map/ppermute | solution.py:17
  53.8 88.9 %collective-permute-start.9 = (f32[256,2048]{1,0:T(8,128)}, f32[256,2048]{1,0:T(8,128)}, u32[]{:S(2)}, u32[]{:S(2)}) collective-permute-start(f32[256,2048]{1,0:T(8,128)} %fusion.6), channel_id=1, source_target_pairs={{0,1},{1,0},{2,3},{3,2},{4,5},{5,4},{6,7},{7,6},{8,9},{9,8},{10,11... | collective-permute-start | bytes 6291464 | tf_op jit(solution)/shard_map/ppermute | solution.py:17
  67.3 7.0 copy-start.27
  67.3 7.0 copy-start.47
  72.4 115.3 %collective-permute-start.10 = (f32[256,2048]{1,0:T(8,128)}, f32[256,2048]{1,0:T(8,128)}, u32[]{:S(2)}, u32[]{:S(2)}) collective-permute-start(f32[256,2048]{1,0:T(8,128)} %fusion.4), channel_id=1, source_target_pairs={{0,1},{1,0},{2,3},{3,2},{4,5},{5,4},{6,7},{7,6},{8,9},{9,8},{10,11... | collective-permute-start | bytes 6291464 | tf_op jit(solution)/shard_map/ppermute | solution.py:17
  76.9 154.9 %collective-permute-start.11 = (f32[256,2048]{1,0:T(8,128)}, f32[256,2048]{1,0:T(8,128)}, u32[]{:S(2)}, u32[]{:S(2)}) collective-permute-start(f32[256,2048]{1,0:T(8,128)} %fusion.8), channel_id=1, source_target_pairs={{0,1},{1,0},{2,3},{3,2},{4,5},{5,4},{6,7},{7,6},{8,9},{9,8},{10,11... | collective-permute-start | bytes 6291464 | tf_op jit(solution)/shard_map/ppermute | solution.py:17
  81.3 16.5 %copy-start.31 = (f32[2048]{0:T(1024)S(1)}, f32[2048]{0:T(1024)}, u32[]{:S(2)}) copy-start(f32[2048]{0:T(1024)} %param.44) | copy-start | bytes 24580
  92.9 8.8 copy-start.28
  92.9 8.8 copy-start.32
  270.7 13.5 %collective-permute-start = (f32[2048,1024]{1,0:T(8,128)}, f32[2048,1024]{1,0:T(8,128)}, u32[]{:S(2)}, u32[]{:S(2)}) collective-permute-start(f32[2048,1024]{1,0:T(8,128)} %get-tuple-element.682), channel_id=1, source_target_pairs={{0,2},{2,0},{1,3},{3,1},{4,6},{6,4},{5,7},{7,5},{8,10},{10,8},{9,1... | collective-permute-start | bytes 25165832 | tf_op jit(solution)/shard_map/while/body/ppermute | solution.py:17
  296.1 708.2 %reduce-scatter.23.cloned.1.call-start = ((), (), s32[]{:S(2)}) async-start(), calls=%async_computation.15 | async-start | bytes 5242880 | tf_op jit(solution)/shard_map/reduce_scatter | solution.py:398
  317.2 13.5 %collective-permute-start.1 = (f32[2048,1024]{1,0:T(8,128)}, f32[2048,1024]{1,0:T(8,128)}, u32[]{:S(2)}, u32[]{:S(2)}) collective-permute-start(f32[2048,1024]{1,0:T(8,128)} %get-tuple-element.686), channel_id=1, source_target_pairs={{0,2},{2,0},{1,3},{3,1},{4,6},{6,4},{5,7},{7,5},{8,10},{10,8},{9,1... | collective-permute-start | bytes 25165832 | tf_op jit(solution)/shard_map/while/body/ppermute | solution.py:17
  338.9 93.0 %collective-permute-start.13 = (f32[2048,512]{1,0:T(8,128)}, f32[2048,512]{1,0:T(8,128)}, u32[]{:S(2)}, u32[]{:S(2)}) collective-permute-start(f32[2048,512]{1,0:T(8,128)} %shard_map.320), channel_id=1, source_target_pairs={{0,4},{4,0},{1,5},{5,1},{2,6},{6,2},{3,7},{7,3},{8,12},{12,8},{9,1... | collective-permute-start | bytes 12582920 | tf_op jit(solution)/shard_map/ppermute | solution.py:17
  340.5 92.7 %collective-permute-start.12 = (f32[512,2048]{1,0:T(8,128)}, f32[512,2048]{1,0:T(8,128)}, u32[]{:S(2)}, u32[]{:S(2)}) collective-permute-start(f32[512,2048]{1,0:T(8,128)} %get-tuple-element.295), channel_id=1, source_target_pairs={{0,1},{1,0},{2,3},{3,2},{4,5},{5,4},{6,7},{7,6},{8,9},{9,8},{10,11... | collective-permute-start | bytes 12582920 | tf_op jit(solution)/shard_map/ppermute | solution.py:17
  368.7 13.5 %collective-permute-start.2 = (f32[1024,2048]{1,0:T(8,128)}, f32[1024,2048]{1,0:T(8,128)}, u32[]{:S(2)}, u32[]{:S(2)}) collective-permute-start(f32[1024,2048]{1,0:T(8,128)} %get-tuple-element.690), channel_id=1, source_target_pairs={{0,2},{2,0},{1,3},{3,1},{4,6},{6,4},{5,7},{7,5},{8,10},{10,8},{9,1... | collective-permute-start | bytes 25165832 | tf_op jit(solution)/shard_map/while/body/ppermute | solution.py:17
  442.6 564.4 %reduce-scatter.17.cloned.1.call-start = ((), (), s32[]{:S(2)}) async-start(), calls=%async_computation.12 | async-start | bytes 5242880 | tf_op jit(solution)/shard_map/reduce_scatter | solution.py:398
  442.7 92.0 %collective-permute-start.14 = (f32[512,2048]{1,0:T(8,128)}, f32[512,2048]{1,0:T(8,128)}, u32[]{:S(2)}, u32[]{:S(2)}) collective-permute-start(f32[512,2048]{1,0:T(8,128)} %get-tuple-element.311), channel_id=1, source_target_pairs={{0,1},{1,0},{2,3},{3,2},{4,5},{5,4},{6,7},{7,6},{8,9},{9,8},{10,11... | collective-permute-start | bytes 12582920 | tf_op jit(solution)/shard_map/ppermute | solution.py:17
  452.0 118.6 %collective-permute-start.16 = (f32[512,2048]{1,0:T(8,128)}, f32[512,2048]{1,0:T(8,128)}, u32[]{:S(2)}, u32[]{:S(2)}) collective-permute-start(f32[512,2048]{1,0:T(8,128)} %shard_map.322), channel_id=1, source_target_pairs={{0,4},{4,0},{1,5},{5,1},{2,6},{6,2},{3,7},{7,3},{8,12},{12,8},{9,1... | collective-permute-start | bytes 12582920 | tf_op jit(solution)/shard_map/ppermute | solution.py:17
  452.5 6.4 copy-start.7
  452.5 7.0 copy-start.11
  496.0 40.2 %copy-start.10 = (f32[256,2048]{1,0:T(8,128)S(1)}, f32[256,2048]{1,0:T(8,128)}, u32[]{:S(2)}) copy-start(f32[256,2048]{1,0:T(8,128)} %get-tuple-element.473) | copy-start | bytes 6291460
  534.7 190.0 %collective-permute-start.15 = (f32[1024,2048]{1,0:T(8,128)}, f32[1024,2048]{1,0:T(8,128)}, u32[]{:S(2)}, u32[]{:S(2)}) collective-permute-start(f32[1024,2048]{1,0:T(8,128)} %shard_map.324), channel_id=1, source_target_pairs={{0,1},{1,0},{2,3},{3,2},{4,5},{5,4},{6,7},{7,6},{8,9},{9,8},{10,11... | collective-permute-start | bytes 25165832 | tf_op jit(solution)/shard_map/ppermute | solution.py:17
  549.8 13.5 %collective-permute-start.3 = (f32[1024,2048]{1,0:T(8,128)}, f32[1024,2048]{1,0:T(8,128)}, u32[]{:S(2)}, u32[]{:S(2)}) collective-permute-start(f32[1024,2048]{1,0:T(8,128)} %get-tuple-element.694), channel_id=1, source_target_pairs={{0,2},{2,0},{1,3},{3,1},{4,6},{6,4},{5,7},{7,5},{8,10},{10,8},{9,1... | collective-permute-start | bytes 25165832 | tf_op jit(solution)/shard_map/while/body/ppermute | solution.py:17
  578.9 428.1 %reduce-scatter.19.cloned.1.call-start = ((), (), s32[]{:S(2)}) async-start(), calls=%async_computation.13 | async-start | bytes 5242880 | tf_op jit(solution)/shard_map/reduce_scatter | solution.py:398
  578.9 157.2 %collective-permute-start.18 = (f32[512,2048]{1,0:T(8,128)}, f32[512,2048]{1,0:T(8,128)}, u32[]{:S(2)}, u32[]{:S(2)}) collective-permute-start(f32[512,2048]{1,0:T(8,128)} %shard_map.329), channel_id=1, source_target_pairs={{0,4},{4,0},{1,5},{5,1},{2,6},{6,2},{3,7},{7,3},{8,12},{12,8},{9,1... | collective-permute-start | bytes 12582920 | tf_op jit(solution)/shard_map/ppermute | solution.py:17
  592.4 31.8 %copy-start.9 = (bf16[1024,1024]{1,0:T(8,128)(2,1)}, bf16[1024,1024]{1,0:T(8,128)(2,1)S(1)}, u32[]{:S(2)}) copy-start(bf16[1024,1024]{1,0:T(8,128)(2,1)S(1)} %constant_dynamic-update-slice_fusion.left_ref) | copy-start | bytes 6291460
  633.1 15.6 %copy-start.22 = (bf16[512,2048]{1,0:T(8,128)(2,1)S(1)}, bf16[512,2048]{1,0:T(8,128)(2,1)}, u32[]{:S(2)}) copy-start(bf16[512,2048]{1,0:T(8,128)(2,1)} %copy-done.21) | copy-start | bytes 6291460
  682.8 7.5 collective-permute-start.4
  696.8 7.5 collective-permute-start.5
  704.5 7.6 collective-permute-start.6
  712.1 7.5 collective-permute-start.7
  744.5 265.6 %reduce-scatter.15.cloned.1.call-start = ((), (), s32[]{:S(2)}) async-start(), calls=%async_computation.11 | async-start | bytes 2621440 | tf_op jit(solution)/shard_map/reduce_scatter | solution.py:398
  744.5 137.9 %collective-permute-start.17 = (f32[768,2048]{1,0:T(8,128)}, f32[768,2048]{1,0:T(8,128)}, u32[]{:S(2)}, u32[]{:S(2)}) collective-permute-start(f32[768,2048]{1,0:T(8,128)} %shard_map.332), channel_id=1, source_target_pairs={{0,1},{1,0},{2,3},{3,2},{4,5},{5,4},{6,7},{7,6},{8,9},{9,8},{10,11... | collective-permute-start | bytes 18874376 | tf_op jit(solution)/shard_map/ppermute | solution.py:17
  746.0 48.6 %collective-permute-start.19 = (f32[1024,512]{1,0:T(8,128)S(1)}, f32[1024,512]{1,0:T(8,128)}, u32[]{:S(2)}, u32[]{:S(2)}) collective-permute-start(f32[1024,512]{1,0:T(8,128)S(1)} %copy-done.24), channel_id=1, source_target_pairs={{0,4},{4,0},{1,5},{5,1},{2,6},{6,2},{3,7},{7,3},{8,12},{12,8},{9,1... | collective-permute-start | bytes 6291464 | tf_op jit(solution)/shard_map/ppermute | solution.py:17
  753.5 86.1 %collective-permute-start.20 = (f32[512,1024]{1,0:T(8,128)}, f32[512,1024]{1,0:T(8,128)}, u32[]{:S(2)}, u32[]{:S(2)}) collective-permute-start(f32[512,1024]{1,0:T(8,128)} %shard_map.344), channel_id=1, source_target_pairs={{0,4},{4,0},{1,5},{5,1},{2,6},{6,2},{3,7},{7,3},{8,12},{12,8},{9,1... | collective-permute-start | bytes 6291464 | tf_op jit(solution)/shard_map/ppermute | solution.py:17
  800.5 209.5 %reduce-scatter.11.cloned.1.call-start = ((), (), s32[]{:S(2)}) async-start(), calls=%async_computation.9 | async-start | bytes 2621440 | tf_op jit(solution)/shard_map/reduce_scatter | solution.py:398
  806.4 91.1 %collective-permute-start.22 = (f32[512,1024]{1,0:T(8,128)}, f32[512,1024]{1,0:T(8,128)}, u32[]{:S(2)}, u32[]{:S(2)}) collective-permute-start(f32[512,1024]{1,0:T(8,128)} %shard_map.346), channel_id=1, source_target_pairs={{0,4},{4,0},{1,5},{5,1},{2,6},{6,2},{3,7},{7,3},{8,12},{12,8},{9,1... | collective-permute-start | bytes 6291464 | tf_op jit(solution)/shard_map/ppermute | solution.py:17
  846.0 36.4 %copy-start.30 = (f32[2048]{0:T(1024)S(1)}, f32[2048]{0:T(1024)}, u32[]{:S(2)}) copy-start(f32[2048]{0:T(1024)} %param.36) | copy-start | bytes 24580
  882.5 7.9 slice-start
  882.5 8.9 slice-start.1
  882.5 10.1 copy-start.8
  882.5 11.3 %copy-start.17 = (f32[512,2048]{1,0:T(8,128)S(1)}, f32[512,2048]{1,0:T(8,128)}, u32[]{:S(2)}) copy-start(f32[512,2048]{1,0:T(8,128)} %get-tuple-element.463) | copy-start | bytes 12582916
  882.5 11.3 %copy-start.34 = (f32[1024]{0:T(1024)S(1)}, f32[1024]{0:T(1024)}, u32[]{:S(2)}) copy-start(f32[1024]{0:T(1024)} %copy-done.33) | copy-start | bytes 12292
  897.5 6.7 copy-start.20
  904.1 5.9 copy-start.44
  904.1 6.8 copy-start.36
  904.1 6.8 copy-start.35
  904.1 6.8 copy-start.37
  904.1 105.9 %reduce-scatter.9.cloned.1.call-start = ((), (), s32[]{:S(2)}) async-start(), calls=%async_computation.8 | async-start | bytes 2621440 | tf_op jit(solution)/shard_map/reduce_scatter | solution.py:398
  904.2 47.0 %collective-permute-start.21 = (f32[256,2048]{1,0:T(8,128)S(1)}, f32[256,2048]{1,0:T(8,128)}, u32[]{:S(2)}, u32[]{:S(2)}) collective-permute-start(f32[256,2048]{1,0:T(8,128)S(1)} %copy-done.20), channel_id=1, source_target_pairs={{0,1},{1,0},{2,3},{3,2},{4,5},{5,4},{6,7},{7,6},{8,9},{9,8},{10,11... | collective-permute-start | bytes 6291464 | tf_op jit(solution)/shard_map/ppermute | solution.py:17
  904.9 135.0 %reduce-scatter.13.cloned.1.call-start = ((), (), s32[]{:S(2)}) async-start(), calls=%async_computation.10 | async-start | bytes 2621440 | tf_op jit(solution)/shard_map/reduce_scatter | solution.py:398
  911.0 52.2 %collective-permute-start.27 = (f32[512,1024]{1,0:T(8,128)}, f32[512,1024]{1,0:T(8,128)}, u32[]{:S(2)}, u32[]{:S(2)}) collective-permute-start(f32[512,1024]{1,0:T(8,128)} %shard_map.348), channel_id=1, source_target_pairs={{0,4},{4,0},{1,5},{5,1},{2,6},{6,2},{3,7},{7,3},{8,12},{12,8},{9,1... | collective-permute-start | bytes 6291464 | tf_op jit(solution)/shard_map/ppermute | solution.py:17
  955.7 1.3 collective-permute-start.23
  957.0 12.6 %collective-permute-start.24 = (f32[4,1152]{1,0:T(4,128)S(1)}, f32[4,1152]{1,0:T(4,128)S(1)}, u32[]{:S(2)}, u32[]{:S(2)}) collective-permute-start(f32[4,1152]{1,0:T(4,128)S(1)} %bitcast.84), channel_id=1, source_target_pairs={{0,4},{4,0},{1,5},{5,1},{2,6},{6,2},{3,7},{7,3},{8,12},{12,8},{9,1... | collective-permute-start | bytes 55304 | tf_op jit(solution)/shard_map/ppermute | solution.py:17
  969.6 9.2 copy-start.18
  969.7 6.3 collective-permute-start.25
  976.1 6.4 collective-permute-start.26
  978.5 24.2 %collective-permute-start.28 = (f32[2048,128]{1,0:T(8,128)}, f32[2048,128]{1,0:T(8,128)}, u32[]{:S(2)}, u32[]{:S(2)}) collective-permute-start(f32[2048,128]{1,0:T(8,128)} %constant_dynamic-slice_fusion), channel_id=1, source_target_pairs={{0,4},{4,0},{1,5},{5,1},{2,6},{6,2},{3,7},{7,3},{8,12},{12,8},{9,1... | collective-permute-start | bytes 3145736 | tf_op jit(solution)/shard_map/ppermute | solution.py:17
  (27 other events, 101.8 us)
Sparse Core Ops, SparseCore 0:
  296.2 146.0 reduce-scatter.20
  444.6 77.4 reduce-scatter.22
  579.0 76.0 reduce-scatter.16
  744.6 77.0 reduce-scatter.18
  824.4 44.1 reduce-scatter.14
  904.2 43.8 reduce-scatter.10
  951.0 43.0 reduce-scatter.8
  997.0 42.8 reduce-scatter.12

commit v5 on v4

--- a/solution.py
+++ b/solution.py
@@ -428,6 +428,9 @@
     mixed = jnp.concatenate(mixed_blocks, 0)
     attn_others = [swap(piece, "mp") for piece in attn_parts]
 
+    normed_pieces = pieces(normed)
+    grad_pieces = [pieces(out_grad, True), pieces(out_grad)]
+    early = [None, normed_pieces, *grad_pieces]
     resids, units2, scales2, normeds2 = [], [], [], []
     shares, pull_sums, kept = [], [], None
     for index in range(CHUNKS):
@@ -436,7 +439,7 @@
         if index == 0:
             attn_other = after(attn_other, attn_parts[-1])
         else:
-            attn_other = after(attn_other, pull_sums[-1])
+            attn_other = after(attn_other, pull_sums[-1], early[index % 4])
         resid = features[rows] + ((attn_parts[index] + attn_other) + out_bias)
         unit2, scale2 = norm_parts(resid)
         normed2 = (unit2 * norm2_gain + norm2_bias).astype(BF16)
@@ -460,7 +463,7 @@
     half = up_weight.shape[1] // 2
     normed2_pieces = pieces(jnp.concatenate(normeds2, 0))
     downs = [
-        Sum(pieces(out_grad, begin == 0), acts, False, begin, half) for begin in (0, half)
+        Sum(parts, acts, False, begin, half) for parts, begin in zip(grad_pieces, (0, half))
     ]
     ups = [Sum(normed2_pieces, hidden_grads, True, begin, half) for begin in (0, half)]
 
@@ -492,17 +495,21 @@
     gate = ups[0].over_cores(gate)
     gate = ups[0].meet(gate)
     gate = ups[0].over_x(gate)
-    gate = downs[1].over_z(gate, share_others[0])
     gate = norm2_pull(0, gate)
+    gate = downs[1].over_z(gate)
     branch = product_down(after(acts, gate), down_weight)
     gate = ups[1].over_cores(branch)
     gate = norm2_pull(1, gate)
     branch_other = swap(after(branch, share_others[-1]), "mp")
+    gate = ups[0].over_z(gate)
+    attn_grad = jnp.concatenate(attn_grads, 0)
+    out_sum = Sum(pieces(attn_grad), mixed, False)
+    gate = out_sum.over_cores(gate)
+    gate = out_sum.meet(gate)
+    gate = out_sum.over_x(gate)
     gate = ups[1].meet(gate)
     gate = ups[1].over_x(gate)
-    gate = ups[0].over_z(gate)
     mixed_grad = jnp.concatenate(mixed_grads, 0)
-    attn_grad = jnp.concatenate(attn_grads, 0)
     query_grad, key_grad, value_grad, query_bias_grad, value_bias_grad = attend_pull(
         queries, keys, values, after(mixed_grad, gate), totals_log, prefix_len, head_dim
     )
@@ -517,23 +524,22 @@
         norm1_parts.append(product_back(pulls, [query_weight, key_weight, value_weight], rows, begin // rows))
     norm1_others = [swap(piece, "mp") for piece in norm1_parts]
 
-    normed_pieces = pieces(normed)
-    out_sum = Sum(pieces(attn_grad), mixed, False)
     query_sum, key_sum, value_sum = [
         Sum(normed_pieces, pull, True) for pull in (query_grad, key_grad, value_grad)
     ]
-    sums = [out_sum, query_sum, key_sum, value_sum]
+    sums = [query_sum, key_sum, value_sum]
+    gate = out_sum.over_z(*norm1_parts)
     for item in sums:
-        gate = item.over_cores(*norm1_parts)
+        gate = item.over_cores(gate)
     gate = sums[-1].own
     for item in sums:
         gate = item.meet(gate)
-    gate = out_sum.over_x(gate)
+    gate = query_sum.over_x(gate)
+    gate = key_sum.over_x(gate)
+    gate = ups[1].over_z(gate, branch_other)
+    gate = value_sum.over_x(gate)
     outputs = (jnp.concatenate(resids, 0) + ((branch + after(branch_other, gate)) + down_bias)).astype(BF16)
-    gate = ups[1].over_z(outputs)
-    gate = query_sum.over_x(gate)
-    gate = out_sum.over_z(gate)
-    gate = key_sum.over_x(gate)
+    gate = outputs
 
     norm1_gain_grad, norm1_bias_grad = 0.0, 0.0
     in_grads = []
@@ -549,12 +555,11 @@
         return in_grads[-1]
 
     gate = query_sum.over_z(gate)
-    gate = value_sum.over_x(gate)
+    gate = key_sum.over_z(gate)
     downs[0].over_x_last(gate)
     gate = norm1_pull(0, gate)
-    gate = key_sum.over_z(gate)
+    gate = value_sum.over_z(gate)
     gate = norm1_pull(1, gate)
-    gate = value_sum.over_z(gate)
     in_grad = jnp.concatenate(in_grads, 0)
 
     def blocks(vector, lead):

time: 1060 us -> 1090 us (1.028)
  waiting for transfers between devices: 401 us -> 425 us
    ppermute x27, waiting for transfers between devices: 367 us -> 399 us  [swap(): return lax.ppermute(value, axis, [(0, 1), (1, 0)])]
  transfers between devices with their start and end apart: 37 -> 37, of which waited for: 23 -> 23; matrix products, arithmetic and copies ran while one was open for 13% -> 12% of each run, Pallas kernels for 35% -> 35%
where the time goes in v5:
time: 1090 us; the launch traced here: 1080 us
  Pallas kernels  433 us (40%)
  waiting for transfers between devices  425 us (39%)
  other arithmetic  124 us (11%)
  matrix products  38 us (3%)
  starting transfers between devices  28.4 us (3%)
  between operations  16 us (1%)
  local copies, waits for them, and re-layouts  15.9 us (1%)
    ppermute x27, waiting for transfers between devices, swap(): return lax.ppermute(value, axis, [(0, 1), (1, 0)])  399 us
    pallas_call x23, Pallas kernels, paired(): pl.pallas_call(kernel, grid_spec=pltpu.PrefetchScalarGridSpec(num_scalar_...  177 us
    pallas_call x4, Pallas kernels, hidden_step(): pl.pallas_call(kernel, grid=(local // block,), in_specs=[same, pl.BlockSp...  99.2 us
    pallas_call x5, Pallas kernels, pieces(): pl.pallas_call(kernel, grid=(dps,), in_specs=[pl.BlockSpec((length, wide)...  51.7 us
    dot_general x9, matrix products, mm(): lax.dot_general(left, right, (contract, ((), ())), preferred_element_type...  38 us
    pallas_call x1, Pallas kernels, product_down(): pl.pallas_call(kernel, grid=(cols // wide, inner // deep), in_specs=[pl.B...  28.7 us
    pallas_call x1, Pallas kernels, attend_pull(): pl.pallas_call(kernel, grid=(heads,), in_specs=[pl.BlockSpec(memory_space...  27.9 us
    reduce_scatter x7, waiting for transfers between devices, over_z(): lax.psum_scatter(total, 'z', scatter_dimension=self.dim, tiled=True)  24.7 us
  transfers between devices with their start and end apart: 37, of which 23 were waited for; matrix products, arithmetic and copies ran while one was open for 12% of the time, Pallas kernels for 35%

profile of v5, /device:TPU:0, one launch (start us, length us, event | category | flops | bytes accessed | tf_op | source)
XLA Modules:
  0.0 1080.1 jit_solution(13629230733851569632)
XLA Ops:
  34.0 10.4 shard_map.305
  55.1 13.5 %shard_map.306 = (bf16[512,1024]{1,0:T(8,128)(2,1)}, f32[8,512,1]{2,1,0:T(8,128)}) custom-call(s32[1]{0:T(128)S(6)} %copy.114.boundary_ref, bf16[1024,1024]{1,0:T(8,128)(2,1)} %add_convert_fusion.2.query_ref, bf16[1024,1024]{1,0:T(8,128)(2,1)} %convolution_convert_fusion.key_ref, bf16[1024,1024]{1,0:T(8,128)(2,1)} %add_convert_fusion.1.value_ref), custom_call_target="tpu_custom_call" | custom-call | tf_op jit(solution)/shard_map/pallas_call | solution.py:178
  81.5 10.3 shard_map.308.left_ref
  91.8 10.3 shard_map.310.right_ref
  102.1 10.4 shard_map.312.right_ref
  120.5 22.3 %shard_map.307 = (bf16[1024,4096]{1,0:T(8,128)(2,1)}, bf16[1024,4096]{1,0:T(8,128)(2,1)}, f32[512,2048]{1,0:T(8,128)}, f32[1,4096]{1,0:T(1,128)}) custom-call(bf16[256,2048]{1,0:T(8,128)(2,1)} %get-tuple-element.478.normed_ref, bf16[1024,2048]{1,0:T(8,128)(2,1)} %dy_ref.7, bf16[2048,4096]{1,0:T(8,128)(2,1)} %up_ref.7, f32[1,4096]{1,0:T(1,128)} %bitcast.72, ...), custom_call_target="tpu_custom_call" | custom-call | tf_op jit(solution)/shard_map/pallas_call | solution.py:280
  150.9 22.4 %shard_map.309 = (bf16[1024,4096]{1,0:T(8,128)(2,1)}, bf16[1024,4096]{1,0:T(8,128)(2,1)}, f32[512,2048]{1,0:T(8,128)}, f32[1,4096]{1,0:T(1,128)}) custom-call(bf16[256,2048]{1,0:T(8,128)(2,1)} %get-tuple-element.474.normed_ref, bf16[1024,2048]{1,0:T(8,128)(2,1)} %dy_ref.7, ...), custom_call_target="tpu_custom_call", output_to_operand_aliasing={{0}: (5, {}), {1}: (6, {}), {2}: (7, {})} | custom-call | tf_op jit(solution)/shard_map/pallas_call | solution.py:280
  173.3 15.8 %collective-permute-done.10 = f32[256,2048]{1,0:T(8,128)} collective-permute-done((f32[256,2048]{1,0:T(8,128)S(1)}, f32[256,2048]{1,0:T(8,128)}, u32[]{:S(2)}, u32[]{:S(2)}) %collective-permute-start.10) | collective-permute-done | bytes 2097184 | tf_op jit(solution)/shard_map/ppermute | solution.py:17
  194.6 32.2 %shard_map.311 = (bf16[1024,4096]{1,0:T(8,128)(2,1)}, bf16[1024,4096]{1,0:T(8,128)(2,1)}, f32[512,2048]{1,0:T(8,128)}, f32[1,4096]{1,0:T(1,128)}) custom-call(bf16[256,2048]{1,0:T(8,128)(2,1)} %get-tuple-element.470.normed_ref, bf16[1024,2048]{1,0:T(8,128)(2,1)} %dy_ref.7, bf16[2048,4096]{1,0:T(8,128)(2,1)} %up_ref.7, ...), custom_call_target="tpu_custom_call", output_to_operand_aliasing={{0}: (5, {}), {1}: (6, {})} | custom-call | tf_op jit(solution)/shard_map/pallas_call | solution.py:280
  226.8 6.5 collective-permute-done.11
  240.0 22.3 %shard_map.313 = (bf16[1024,4096]{1,0:T(8,128)(2,1)}, bf16[1024,4096]{1,0:T(8,128)(2,1)}, f32[512,2048]{1,0:T(8,128)}, f32[1,4096]{1,0:T(1,128)}) custom-call(bf16[256,2048]{1,0:T(8,128)(2,1)} %get-tuple-element.466.normed_ref, bf16[1024,2048]{1,0:T(8,128)(2,1)} %dy_ref.7, ...), custom_call_target="tpu_custom_call", output_to_operand_aliasing={{0}: (5, {}), {1}: (6, {}), {2}: (7, {})} | custom-call | tf_op jit(solution)/shard_map/pallas_call | solution.py:280
  262.3 9.9 shard_map.318
  272.2 13.5 %while.80 = (s32[]{:T(128)}, f32[2048,1024]{1,0:T(8,128)}, s32[]{:T(128)}, f32[2048,1024]{1,0:T(8,128)}, s32[]{:T(128)}) while((s32[]{:T(128)}, f32[2048,1024]{1,0:T(8,128)}, s32[]{:T(128)}, f32[2048,1024]{1,0:T(8,128)}, s32[]{:T(128)}) %tuple.281), condition=%wide.region_11.12_spmd, body=%wide.region_10.0_spmd.sunk | while | flops 2 | bytes 33554532 | solution.py:362
  272.2 13.5 %collective-permute-done = f32[2048,1024]{1,0:T(8,128)} collective-permute-done((f32[2048,1024]{1,0:T(8,128)}, f32[2048,1024]{1,0:T(8,128)}, u32[]{:S(2)}, u32[]{:S(2)}) %collective-permute-start) | collective-permute-done | bytes 8388640 | tf_op jit(solution)/shard_map/while/body/ppermute | solution.py:17
  285.7 11.9 %shard_map.319 = f32[2048,1024]{1,0:T(8,128)} custom-call(s32[4]{0:T(128)} %get-tuple-element.496.starts_ref, bf16[1024,4096]{1,0:T(8,128)(2,1)} %get-tuple-element.309.left_ref, bf16[1024,2048]{1,0:T(8,128)(2,1)} %shard_map.310.right_ref, f32[2048,1024]{1,0:T(8,128)} %get-tuple-element.298.rest_0_), custom_call_target="tpu_custom_call" | custom-call | tf_op jit(solution)/shard_map/pallas_call | solution.py:89
  300.1 10.0 shard_map.320
  310.1 13.5 %while.81 = (s32[]{:T(128)}, f32[2048,1024]{1,0:T(8,128)}, s32[]{:T(128)}, f32[2048,1024]{1,0:T(8,128)}, s32[]{:T(128)}) while((s32[]{:T(128)}, f32[2048,1024]{1,0:T(8,128)}, s32[]{:T(128)}, f32[2048,1024]{1,0:T(8,128)}, s32[]{:T(128)}) %tuple.284), condition=%wide.region_13.14_spmd, body=%wide.region_12.13_spmd.sunk | while | flops 2 | bytes 33554532 | solution.py:362
  310.1 13.5 %collective-permute-done.1 = f32[2048,1024]{1,0:T(8,128)} collective-permute-done((f32[2048,1024]{1,0:T(8,128)}, f32[2048,1024]{1,0:T(8,128)}, u32[]{:S(2)}, u32[]{:S(2)}) %collective-permute-start.1) | collective-permute-done | bytes 8388640 | tf_op jit(solution)/shard_map/while/body/ppermute | solution.py:17
  323.6 8.1 shard_map.321
  333.3 6.8 convert_element_type.66
  343.0 10.3 shard_map.314.left_ref
  353.3 11.3 %shard_map.322 = f32[1024,2048]{1,0:T(8,128)} custom-call(s32[4]{0:T(128)} %get-tuple-element.498.starts_ref, bf16[1024,2048]{1,0:T(8,128)(2,1)} %shard_map.314.left_ref, bf16[1024,4096]{1,0:T(8,128)(2,1)} %get-tuple-element.343.right_ref), custom_call_target="tpu_custom_call" | custom-call | tf_op jit(solution)/shard_map/pallas_call | solution.py:89
  364.7 13.5 %while.82 = (s32[]{:T(128)}, f32[1024,2048]{1,0:T(8,128)}, s32[]{:T(128)}, f32[1024,2048]{1,0:T(8,128)}, s32[]{:T(128)}) while((s32[]{:T(128)}, f32[1024,2048]{1,0:T(8,128)}, s32[]{:T(128)}, f32[1024,2048]{1,0:T(8,128)}, s32[]{:T(128)}) %tuple.287), condition=%wide.region_15.16_spmd, body=%wide.region_14.15_spmd.sunk | while | flops 2 | bytes 33554532 | solution.py:362
  364.7 13.5 %collective-permute-done.2 = f32[1024,2048]{1,0:T(8,128)} collective-permute-done((f32[1024,2048]{1,0:T(8,128)}, f32[1024,2048]{1,0:T(8,128)}, u32[]{:S(2)}, u32[]{:S(2)}) %collective-permute-start.2) | collective-permute-done | bytes 8388640 | tf_op jit(solution)/shard_map/while/body/ppermute | solution.py:17
  378.2 7.1 shard_map.323
  390.7 6.4 multiply_reduce_fusion.5
  405.7 19.1 %collective-permute-done.13.rest_1_ = f32[2048,512]{1,0:T(8,128)} collective-permute-done((f32[2048,512]{1,0:T(8,128)}, f32[2048,512]{1,0:T(8,128)}, u32[]{:S(2)}, u32[]{:S(2)}) %collective-permute-start.13) | collective-permute-done | bytes 4194336 | tf_op jit(solution)/shard_map/ppermute | solution.py:17
  424.7 9.4 shard_map.324
  436.8 28.7 %shard_map.325 = f32[1024,2048]{1,0:T(8,128)} custom-call(bf16[1024,4096]{1,0:T(8,128)(2,1)} %get-tuple-element.309.left_ref, bf16[4096,2048]{1,0:T(8,128)(2,1)} %right_ref.1), custom_call_target="tpu_custom_call" | custom-call | tf_op jit(solution)/shard_map/pallas_call | solution.py:117
  465.5 11.2 %shard_map.326 = f32[1024,2048]{1,0:T(8,128)} custom-call(s32[4]{0:T(128)} %get-tuple-element.494.starts_ref, bf16[1024,2048]{1,0:T(8,128)(2,1)} %shard_map.314.left_ref, bf16[1024,4096]{1,0:T(8,128)(2,1)} %get-tuple-element.343.right_ref), custom_call_target="tpu_custom_call" | custom-call | tf_op jit(solution)/shard_map/pallas_call | solution.py:89
  476.7 49.8 %collective-permute-done.14 = f32[512,2048]{1,0:T(8,128)} collective-permute-done((f32[512,2048]{1,0:T(8,128)}, f32[512,2048]{1,0:T(8,128)}, u32[]{:S(2)}, u32[]{:S(2)}) %collective-permute-start.14) | collective-permute-done | bytes 4194336 | tf_op jit(solution)/shard_map/ppermute | solution.py:17
  540.3 8.3 shard_map.329
  554.2 10.4 shard_map.330.right_ref
  564.6 6.5 shard_map.331
  571.1 7.5 while.83
  571.1 7.5 collective-permute-done.3
  583.6 13.5 %while.84 = (s32[]{:T(128)}, f32[1024,2048]{1,0:T(8,128)}, s32[]{:T(128)}, f32[1024,2048]{1,0:T(8,128)}, s32[]{:T(128)}) while((s32[]{:T(128)}, f32[1024,2048]{1,0:T(8,128)}, s32[]{:T(128)}, f32[1024,2048]{1,0:T(8,128)}, s32[]{:T(128)}) %tuple.293), condition=%wide.region_23.24_spmd, body=%wide.region_22.23_spmd.sunk | while | flops 2 | bytes 33554532 | solution.py:362
  583.8 13.4 %collective-permute-done.4 = f32[1024,2048]{1,0:T(8,128)} collective-permute-done((f32[1024,2048]{1,0:T(8,128)}, f32[1024,2048]{1,0:T(8,128)}, u32[]{:S(2)}, u32[]{:S(2)}) %collective-permute-start.4) | collective-permute-done | bytes 8388640 | tf_op jit(solution)/shard_map/while/body/ppermute | solution.py:17
  597.2 7.6 shard_map.333
  610.8 27.9 %shard_map.334 = (bf16[1024,1024]{1,0:T(8,128)(2,1)}, bf16[1024,1024]{1,0:T(8,128)(2,1)}, bf16[1024,1024]{1,0:T(8,128)(2,1)}, f32[8,1,128]{2,1,0:T(1,128)}, f32[8,1,128]{2,1,0:T(1,128)}) custom-call(s32[1]{0:T(128)S(6)} %copy.114.boundary_ref, bf16[1024,1024]{1,0:T(8,128)(2,1)} %add_convert_fusion.2.query_ref, ...), custom_call_target="tpu_custom_call" | custom-call | tf_op jit(solution)/shard_map/pallas_call | solution.py:237
  638.8 8.8 shard_map.337
  647.6 15.4 %shard_map.336 = f32[768,2048]{1,0:T(8,128)} custom-call(bf16[1024,1024]{1,0:T(8,128)(2,1)} %get-tuple-element.347.refs_0_.right_ref, bf16[1024,1024]{1,0:T(8,128)(2,1)} %get-tuple-element.349.refs_1_.right_ref, bf16[1024,1024]{1,0:T(8,128)(2,1)} %get-tuple-element.352.refs_2_.right_ref, bf16[2048,1024]{1,0:T(8,128)(2,1)} %refs_3_.3, ...), custom_call_target="tpu_custom_call" | custom-call | tf_op jit(solution)/shard_map/pallas_call | solution.py:141
  663.0 79.6 %collective-permute-done.17.rest_1_ = f32[1024,512]{1,0:T(8,128)} collective-permute-done((f32[1024,512]{1,0:T(8,128)S(1)}, f32[1024,512]{1,0:T(8,128)}, u32[]{:S(2)}, u32[]{:S(2)}) %collective-permute-start.17) | collective-permute-done | bytes 2097184 | tf_op jit(solution)/shard_map/ppermute | solution.py:17
  748.3 6.5 shard_map.339
  754.9 6.5 shard_map.340
  761.4 6.6 shard_map.341
  767.9 7.5 while.85
  767.9 7.5 collective-permute-done.5
  775.4 7.5 while.86
  775.6 7.4 collective-permute-done.6
  782.9 7.5 while.87
  783.1 7.4 collective-permute-done.7
  802.1 8.5 shard_map.346
  821.2 11.4 %fusion = bf16[1024,2048]{1,0:T(8,128)(2,1)} fusion(f32[256,2048]{1,0:T(8,128)} %copy-done.6, f32[256,2048]{1,0:T(8,128)} %copy-done.5, f32[256,2048]{1,0:T(8,128)} %copy-done.4, f32[256,2048]{1,0:T(8,128)S(1)} %copy-done.3, f32[1024,2048]{1,0:T(8,128)} %shard_map.325, f32[1024,2048]{1,0:T(8,128)} %collective-permute-done.15, f32[2048]{0:T(1024)S(1)} %copy-done.46), kind=kLoop, calls=%fused_computation.1 | loop fusion | flops 14680064 | bytes 29368320 | tf_op jit(solution)/shard_map/convert_element_type | solution.py:541
  832.7 27.5 %collective-permute-done.20.rest_1_ = f32[512,1024]{1,0:T(8,128)} collective-permute-done((f32[512,1024]{1,0:T(8,128)}, f32[512,1024]{1,0:T(8,128)}, u32[]{:S(2)}, u32[]{:S(2)}) %collective-permute-start.20) | collective-permute-done | bytes 2097184 | tf_op jit(solution)/shard_map/ppermute | solution.py:17
  860.2 6.5 shard_map.348
  866.6 37.6 %collective-permute-done.21.rest_1_ = f32[512,1024]{1,0:T(8,128)} collective-permute-done((f32[512,1024]{1,0:T(8,128)}, f32[512,1024]{1,0:T(8,128)}, u32[]{:S(2)}, u32[]{:S(2)}) %collective-permute-start.21) | collective-permute-done | bytes 2097184 | tf_op jit(solution)/shard_map/ppermute | solution.py:17
  904.3 6.4 shard_map.349
  920.9 31.2 %collective-permute-done.19 = f32[768,2048]{1,0:T(8,128)} collective-permute-done((f32[768,2048]{1,0:T(8,128)}, f32[768,2048]{1,0:T(8,128)}, u32[]{:S(2)}, u32[]{:S(2)}) %collective-permute-start.19) | collective-permute-done | bytes 6291488 | tf_op jit(solution)/shard_map/ppermute | solution.py:17
  952.1 8.2 multiply_reduce_fusion.1
  967.3 6.4 shard_map.350
  973.7 21.9 %collective-permute-done.22 = f32[256,2048]{1,0:T(8,128)} collective-permute-done((f32[256,2048]{1,0:T(8,128)S(1)}, f32[256,2048]{1,0:T(8,128)}, u32[]{:S(2)}, u32[]{:S(2)}) %collective-permute-start.22) | collective-permute-done | bytes 2097184 | tf_op jit(solution)/shard_map/ppermute | solution.py:17
  1024.7 16.3 %collective-permute-done.28 = f32[2048,128]{1,0:T(8,128)} collective-permute-done((f32[2048,128]{1,0:T(8,128)}, f32[2048,128]{1,0:T(8,128)}, u32[]{:S(2)}, u32[]{:S(2)}) %collective-permute-start.28) | collective-permute-done | bytes 1048608 | tf_op jit(solution)/shard_map/ppermute | solution.py:17
  1048.4 24.7 %reduce-scatter.13.cloned.1.call-done = f32[128,1024]{1,0:T(8,128)} async-done(((f32[512,1024]{1,0:T(8,128)}), f32[128,1024]{1,0:T(8,128)}) %reduce-scatter.13.cloned.1.call-update) | async-done | bytes 524304 | tf_op jit(solution)/shard_map/reduce_scatter | solution.py:398
  (301 shorter events, 213.3 us)
Async XLA Ops:
  7.2 1007.3 %reduce-scatter.21.cloned.1.call-start = ((), (), s32[]{:S(2)}) async-start(), calls=%async_computation.14 | async-start | bytes 10485760 | tf_op jit(solution)/shard_map/reduce_scatter | solution.py:403
  16.8 11.5 %copy-start.12 = (bf16[1024,2048]{1,0:T(8,128)(2,1)}, bf16[1024,2048]{1,0:T(8,128)(2,1)S(1)}, u32[]{:S(2)}) copy-start(bf16[1024,2048]{1,0:T(8,128)(2,1)S(1)} %get-tuple-element.483.field_ref) | copy-start | bytes 12582916
  16.8 5.7 copy-start.15
  22.5 5.8 copy-start.13
  22.5 5.8 copy-start.54
  44.4 8.1 copy-start.28
  44.4 8.1 copy-start.49
  49.5 64.2 %collective-permute-start.8 = (f32[256,2048]{1,0:T(8,128)}, f32[256,2048]{1,0:T(8,128)}, u32[]{:S(2)}, u32[]{:S(2)}) collective-permute-start(f32[256,2048]{1,0:T(8,128)} %fusion.10), channel_id=1, source_target_pairs={{0,1},{1,0},{2,3},{3,2},{4,5},{5,4},{6,7},{7,6},{8,9},{9,8},{10,11... | collective-permute-start | bytes 6291464 | tf_op jit(solution)/shard_map/ppermute | solution.py:17
  55.1 89.1 %collective-permute-start.9 = (f32[256,2048]{1,0:T(8,128)}, f32[256,2048]{1,0:T(8,128)}, u32[]{:S(2)}, u32[]{:S(2)}) collective-permute-start(f32[256,2048]{1,0:T(8,128)} %fusion.6), channel_id=1, source_target_pairs={{0,1},{1,0},{2,3},{3,2},{4,5},{5,4},{6,7},{7,6},{8,9},{9,8},{10,11... | collective-permute-start | bytes 6291464 | tf_op jit(solution)/shard_map/ppermute | solution.py:17
  68.6 5.9 copy-start.30
  68.6 5.9 copy-start.50
  72.3 116.8 %collective-permute-start.10 = (f32[256,2048]{1,0:T(8,128)S(1)}, f32[256,2048]{1,0:T(8,128)}, u32[]{:S(2)}, u32[]{:S(2)}) collective-permute-start(f32[256,2048]{1,0:T(8,128)S(1)} %fusion.4), channel_id=1, source_target_pairs={{0,1},{1,0},{2,3},{3,2},{4,5},{5,4},{6,7},{7,6},{8,9},{9,8},{10,11... | collective-permute-start | bytes 6291464 | tf_op jit(solution)/shard_map/ppermute | solution.py:17
  77.1 156.2 %collective-permute-start.11 = (f32[256,2048]{1,0:T(8,128)}, f32[256,2048]{1,0:T(8,128)}, u32[]{:S(2)}, u32[]{:S(2)}) collective-permute-start(f32[256,2048]{1,0:T(8,128)} %fusion.8), channel_id=1, source_target_pairs={{0,1},{1,0},{2,3},{3,2},{4,5},{5,4},{6,7},{7,6},{8,9},{9,8},{10,11... | collective-permute-start | bytes 6291464 | tf_op jit(solution)/shard_map/ppermute | solution.py:17
  272.2 13.5 %collective-permute-start = (f32[2048,1024]{1,0:T(8,128)}, f32[2048,1024]{1,0:T(8,128)}, u32[]{:S(2)}, u32[]{:S(2)}) collective-permute-start(f32[2048,1024]{1,0:T(8,128)} %get-tuple-element.680), channel_id=1, source_target_pairs={{0,2},{2,0},{1,3},{3,1},{4,6},{6,4},{5,7},{7,5},{8,10},{10,8},{9,1... | collective-permute-start | bytes 25165832 | tf_op jit(solution)/shard_map/while/body/ppermute | solution.py:17
  297.7 745.0 %reduce-scatter.23.cloned.1.call-start = ((), (), s32[]{:S(2)}) async-start(), calls=%async_computation.15 | async-start | bytes 5242880 | tf_op jit(solution)/shard_map/reduce_scatter | solution.py:398
  297.7 93.0 %collective-permute-start.12 = (f32[512,2048]{1,0:T(8,128)}, f32[512,2048]{1,0:T(8,128)}, u32[]{:S(2)}, u32[]{:S(2)}) collective-permute-start(f32[512,2048]{1,0:T(8,128)} %get-tuple-element.294), channel_id=1, source_target_pairs={{0,1},{1,0},{2,3},{3,2},{4,5},{5,4},{6,7},{7,6},{8,9},{9,8},{10,11... | collective-permute-start | bytes 12582920 | tf_op jit(solution)/shard_map/ppermute | solution.py:17
  310.1 13.5 %collective-permute-start.1 = (f32[2048,1024]{1,0:T(8,128)}, f32[2048,1024]{1,0:T(8,128)}, u32[]{:S(2)}, u32[]{:S(2)}) collective-permute-start(f32[2048,1024]{1,0:T(8,128)} %get-tuple-element.684), channel_id=1, source_target_pairs={{0,2},{2,0},{1,3},{3,1},{4,6},{6,4},{5,7},{7,5},{8,10},{10,8},{9,1... | collective-permute-start | bytes 25165832 | tf_op jit(solution)/shard_map/while/body/ppermute | solution.py:17
  331.8 93.0 %collective-permute-start.13 = (f32[2048,512]{1,0:T(8,128)}, f32[2048,512]{1,0:T(8,128)}, u32[]{:S(2)}, u32[]{:S(2)}) collective-permute-start(f32[2048,512]{1,0:T(8,128)} %shard_map.321), channel_id=1, source_target_pairs={{0,4},{4,0},{1,5},{5,1},{2,6},{6,2},{3,7},{7,3},{8,12},{12,8},{9,1... | collective-permute-start | bytes 12582920 | tf_op jit(solution)/shard_map/ppermute | solution.py:17
  333.3 7.4 copy-start.18
  333.3 7.4 copy-start.19
  333.3 7.4 copy-start.20
  333.3 7.4 copy-start.21
  364.7 13.5 %collective-permute-start.2 = (f32[1024,2048]{1,0:T(8,128)}, f32[1024,2048]{1,0:T(8,128)}, u32[]{:S(2)}, u32[]{:S(2)}) collective-permute-start(f32[1024,2048]{1,0:T(8,128)} %get-tuple-element.688), channel_id=1, source_target_pairs={{0,2},{2,0},{1,3},{3,1},{4,6},{6,4},{5,7},{7,5},{8,10},{10,8},{9,1... | collective-permute-start | bytes 25165832 | tf_op jit(solution)/shard_map/while/body/ppermute | solution.py:17
  390.7 6.4 copy-start.9
  390.7 6.4 copy-start.11
  434.2 611.2 %reduce-scatter.17.cloned.1.call-start = ((), (), s32[]{:S(2)}) async-start(), calls=%async_computation.12 | async-start | bytes 5242880 | tf_op jit(solution)/shard_map/reduce_scatter | solution.py:398
  434.2 92.2 %collective-permute-start.14 = (f32[512,2048]{1,0:T(8,128)}, f32[512,2048]{1,0:T(8,128)}, u32[]{:S(2)}, u32[]{:S(2)}) collective-permute-start(f32[512,2048]{1,0:T(8,128)} %get-tuple-element.310), channel_id=1, source_target_pairs={{0,1},{1,0},{2,3},{3,2},{4,5},{5,4},{6,7},{7,6},{8,9},{9,8},{10,11... | collective-permute-start | bytes 12582920 | tf_op jit(solution)/shard_map/ppermute | solution.py:17
  434.4 105.8 %collective-permute-start.16 = (f32[512,2048]{1,0:T(8,128)}, f32[512,2048]{1,0:T(8,128)}, u32[]{:S(2)}, u32[]{:S(2)}) collective-permute-start(f32[512,2048]{1,0:T(8,128)} %shard_map.323), channel_id=1, source_target_pairs={{0,4},{4,0},{1,5},{5,1},{2,6},{6,2},{3,7},{7,3},{8,12},{12,8},{9,1... | collective-permute-start | bytes 12582920 | tf_op jit(solution)/shard_map/ppermute | solution.py:17
  540.0 262.1 %collective-permute-start.15 = (f32[1024,2048]{1,0:T(8,128)}, f32[1024,2048]{1,0:T(8,128)}, u32[]{:S(2)}, u32[]{:S(2)}) collective-permute-start(f32[1024,2048]{1,0:T(8,128)} %shard_map.325), channel_id=1, source_target_pairs={{0,1},{1,0},{2,3},{3,2},{4,5},{5,4},{6,7},{7,6},{8,9},{9,8},{10,11... | collective-permute-start | bytes 25165832 | tf_op jit(solution)/shard_map/ppermute | solution.py:17
  548.6 496.8 %reduce-scatter.19.cloned.1.call-start = ((), (), s32[]{:S(2)}) async-start(), calls=%async_computation.13 | async-start | bytes 5242880 | tf_op jit(solution)/shard_map/reduce_scatter | solution.py:398
  571.1 7.5 collective-permute-start.3
  583.6 13.5 %collective-permute-start.4 = (f32[1024,2048]{1,0:T(8,128)}, f32[1024,2048]{1,0:T(8,128)}, u32[]{:S(2)}, u32[]{:S(2)}) collective-permute-start(f32[1024,2048]{1,0:T(8,128)} %get-tuple-element.696), channel_id=1, source_target_pairs={{0,2},{2,0},{1,3},{3,1},{4,6},{6,4},{5,7},{7,5},{8,10},{10,8},{9,1... | collective-permute-start | bytes 25165832 | tf_op jit(solution)/shard_map/while/body/ppermute | solution.py:17
  597.1 9.2 copy-start.27
  604.8 197.4 %collective-permute-start.18 = (f32[512,2048]{1,0:T(8,128)}, f32[512,2048]{1,0:T(8,128)}, u32[]{:S(2)}, u32[]{:S(2)}) collective-permute-start(f32[512,2048]{1,0:T(8,128)} %shard_map.333), channel_id=1, source_target_pairs={{0,4},{4,0},{1,5},{5,1},{2,6},{6,2},{3,7},{7,3},{8,12},{12,8},{9,1... | collective-permute-start | bytes 12582920 | tf_op jit(solution)/shard_map/ppermute | solution.py:17
  606.3 136.3 %collective-permute-start.17 = (f32[1024,512]{1,0:T(8,128)S(1)}, f32[1024,512]{1,0:T(8,128)}, u32[]{:S(2)}, u32[]{:S(2)}) collective-permute-start(f32[1024,512]{1,0:T(8,128)S(1)} %copy-done.27), channel_id=1, source_target_pairs={{0,4},{4,0},{1,5},{5,1},{2,6},{6,2},{3,7},{7,3},{8,12},{12,8},{9,1... | collective-permute-start | bytes 6291464 | tf_op jit(solution)/shard_map/ppermute | solution.py:17
  767.9 7.5 collective-permute-start.5
  775.4 7.5 collective-permute-start.6
  782.9 7.5 collective-permute-start.7
  810.6 237.8 %reduce-scatter.15.cloned.1.call-start = ((), (), s32[]{:S(2)}) async-start(), calls=%async_computation.11 | async-start | bytes 2621440 | tf_op jit(solution)/shard_map/reduce_scatter | solution.py:398
  811.2 10.0 copy-start.3
  811.2 10.0 copy-start.46
  811.2 237.2 %reduce-scatter.11.cloned.1.call-start = ((), (), s32[]{:S(2)}) async-start(), calls=%async_computation.9 | async-start | bytes 2621440 | tf_op jit(solution)/shard_map/reduce_scatter | solution.py:398
  811.3 48.9 %collective-permute-start.20 = (f32[512,1024]{1,0:T(8,128)}, f32[512,1024]{1,0:T(8,128)}, u32[]{:S(2)}, u32[]{:S(2)}) collective-permute-start(f32[512,1024]{1,0:T(8,128)} %shard_map.344), channel_id=1, source_target_pairs={{0,4},{4,0},{1,5},{5,1},{2,6},{6,2},{3,7},{7,3},{8,12},{12,8},{9,1... | collective-permute-start | bytes 6291464 | tf_op jit(solution)/shard_map/ppermute | solution.py:17
  812.9 91.4 %collective-permute-start.21 = (f32[512,1024]{1,0:T(8,128)}, f32[512,1024]{1,0:T(8,128)}, u32[]{:S(2)}, u32[]{:S(2)}) collective-permute-start(f32[512,1024]{1,0:T(8,128)} %shard_map.345), channel_id=1, source_target_pairs={{0,4},{4,0},{1,5},{5,1},{2,6},{6,2},{3,7},{7,3},{8,12},{12,8},{9,1... | collective-permute-start | bytes 6291464 | tf_op jit(solution)/shard_map/ppermute | solution.py:17
  813.4 138.7 %collective-permute-start.19 = (f32[768,2048]{1,0:T(8,128)}, f32[768,2048]{1,0:T(8,128)}, u32[]{:S(2)}, u32[]{:S(2)}) collective-permute-start(f32[768,2048]{1,0:T(8,128)} %shard_map.336), channel_id=1, source_target_pairs={{0,1},{1,0},{2,3},{3,2},{4,5},{5,4},{6,7},{7,6},{8,9},{9,8},{10,11... | collective-permute-start | bytes 18874376 | tf_op jit(solution)/shard_map/ppermute | solution.py:17
  910.8 6.7 copy-start.48
  910.8 7.6 copy-start.47
  910.8 8.4 copy-start.40
  910.8 8.4 copy-start.39
  910.8 41.2 %copy-start.34 = (f32[2048]{0:T(1024)S(1)}, f32[2048]{0:T(1024)}, u32[]{:S(2)}) copy-start(f32[2048]{0:T(1024)} %param.36) | copy-start | bytes 24580
  910.8 137.6 %reduce-scatter.9.cloned.1.call-start = ((), (), s32[]{:S(2)}) async-start(), calls=%async_computation.8 | async-start | bytes 2621440 | tf_op jit(solution)/shard_map/reduce_scatter | solution.py:398
  911.6 161.5 %reduce-scatter.13.cloned.1.call-start = ((), (), s32[]{:S(2)}) async-start(), calls=%async_computation.10 | async-start | bytes 2621440 | tf_op jit(solution)/shard_map/reduce_scatter | solution.py:398
  915.1 80.5 %collective-permute-start.22 = (f32[256,2048]{1,0:T(8,128)S(1)}, f32[256,2048]{1,0:T(8,128)}, u32[]{:S(2)}, u32[]{:S(2)}) collective-permute-start(f32[256,2048]{1,0:T(8,128)S(1)} %copy-done.22), channel_id=1, source_target_pairs={{0,1},{1,0},{2,3},{3,2},{4,5},{5,4},{6,7},{7,6},{8,9},{9,8},{10,11... | collective-permute-start | bytes 6291464 | tf_op jit(solution)/shard_map/ppermute | solution.py:17
  919.3 48.0 %collective-permute-start.23 = (f32[512,1024]{1,0:T(8,128)}, f32[512,1024]{1,0:T(8,128)}, u32[]{:S(2)}, u32[]{:S(2)}) collective-permute-start(f32[512,1024]{1,0:T(8,128)} %shard_map.347), channel_id=1, source_target_pairs={{0,4},{4,0},{1,5},{5,1},{2,6},{6,2},{3,7},{7,3},{8,12},{12,8},{9,1... | collective-permute-start | bytes 6291464 | tf_op jit(solution)/shard_map/ppermute | solution.py:17
  952.1 8.2 slice-start
  952.1 9.1 slice-start.1
  952.1 10.3 copy-start.7
  952.1 11.5 %copy-start.16 = (f32[512,2048]{1,0:T(8,128)S(1)}, f32[512,2048]{1,0:T(8,128)}, u32[]{:S(2)}) copy-start(f32[512,2048]{1,0:T(8,128)} %get-tuple-element.461) | copy-start | bytes 12582916
  1000.2 1.3 collective-permute-start.24
  1001.5 3.8 collective-permute-start.25
  1005.4 7.3 collective-permute-start.26
  1008.1 10.1 copy-start.17
  1012.7 9.2 collective-permute-start.27
  1016.7 24.2 %collective-permute-start.28 = (f32[2048,128]{1,0:T(8,128)}, f32[2048,128]{1,0:T(8,128)}, u32[]{:S(2)}, u32[]{:S(2)}) collective-permute-start(f32[2048,128]{1,0:T(8,128)} %constant_dynamic-slice_fusion), channel_id=1, source_target_pairs={{0,4},{4,0},{1,5},{5,1},{2,6},{6,2},{3,7},{7,3},{8,12},{12,8},{9,1... | collective-permute-start | bytes 3145736 | tf_op jit(solution)/shard_map/ppermute | solution.py:17
  (30 other events, 106.3 us)
Sparse Core Ops, SparseCore 0:
  297.8 146.0 reduce-scatter.20
  446.2 77.3 reduce-scatter.22
  548.7 78.1 reduce-scatter.16
  810.7 78.0 reduce-scatter.18
  891.6 44.1 reduce-scatter.14
  938.5 42.8 reduce-scatter.10
  984.2 43.1 reduce-scatter.8
  1030.2 42.8 reduce-scatter.12

commit v6 on v4

--- a/solution.py
+++ b/solution.py
@@ -428,6 +428,9 @@
     mixed = jnp.concatenate(mixed_blocks, 0)
     attn_others = [swap(piece, "mp") for piece in attn_parts]
 
+    normed_pieces = pieces(normed)
+    grad_pieces = [pieces(out_grad, True), pieces(out_grad)]
+    early = [None, normed_pieces, *grad_pieces]
     resids, units2, scales2, normeds2 = [], [], [], []
     shares, pull_sums, kept = [], [], None
     for index in range(CHUNKS):
@@ -436,7 +439,7 @@
         if index == 0:
             attn_other = after(attn_other, attn_parts[-1])
         else:
-            attn_other = after(attn_other, pull_sums[-1])
+            attn_other = after(attn_other, pull_sums[-1], early[index % 4])
         resid = features[rows] + ((attn_parts[index] + attn_other) + out_bias)
         unit2, scale2 = norm_parts(resid)
         normed2 = (unit2 * norm2_gain + norm2_bias).astype(BF16)
@@ -460,7 +463,7 @@
     half = up_weight.shape[1] // 2
     normed2_pieces = pieces(jnp.concatenate(normeds2, 0))
     downs = [
-        Sum(pieces(out_grad, begin == 0), acts, False, begin, half) for begin in (0, half)
+        Sum(parts, acts, False, begin, half) for parts, begin in zip(grad_pieces, (0, half))
     ]
     ups = [Sum(normed2_pieces, hidden_grads, True, begin, half) for begin in (0, half)]
 
@@ -492,8 +495,8 @@
     gate = ups[0].over_cores(gate)
     gate = ups[0].meet(gate)
     gate = ups[0].over_x(gate)
-    gate = downs[1].over_z(gate, share_others[0])
     gate = norm2_pull(0, gate)
+    gate = downs[1].over_z(gate)
     branch = product_down(after(acts, gate), down_weight)
     gate = ups[1].over_cores(branch)
     gate = norm2_pull(1, gate)
@@ -517,7 +520,6 @@
         norm1_parts.append(product_back(pulls, [query_weight, key_weight, value_weight], rows, begin // rows))
     norm1_others = [swap(piece, "mp") for piece in norm1_parts]
 
-    normed_pieces = pieces(normed)
     out_sum = Sum(pieces(attn_grad), mixed, False)
     query_sum, key_sum, value_sum = [
         Sum(normed_pieces, pull, True) for pull in (query_grad, key_grad, value_grad)

time: 1060 us -> 1040 us (0.981)
  waiting for transfers between devices: 401 us -> 382 us
    ppermute x27, waiting for transfers between devices: 367 us -> 348 us  [swap(): return lax.ppermute(value, axis, [(0, 1), (1, 0)])]
  transfers between devices with their start and end apart: 37 -> 37, of which waited for: 23 -> 23; matrix products, arithmetic and copies ran while one was open for 13% -> 13% of each run, Pallas kernels for 35% -> 36%
where the time goes in v6:
time: 1040 us; the launch traced here: 1030 us
  Pallas kernels  423 us (41%)
  waiting for transfers between devices  382 us (37%)
  other arithmetic  126 us (12%)
  matrix products  37.9 us (4%)
  starting transfers between devices  25.6 us (2%)
  local copies, waits for them, and re-layouts  16.9 us (2%)
  between operations  16.1 us (2%)
    ppermute x27, waiting for transfers between devices, swap(): return lax.ppermute(value, axis, [(0, 1), (1, 0)])  348 us
    pallas_call x23, Pallas kernels, paired(): pl.pallas_call(kernel, grid_spec=pltpu.PrefetchScalarGridSpec(num_scalar_...  177 us
    pallas_call x4, Pallas kernels, hidden_step(): pl.pallas_call(kernel, grid=(local // block,), in_specs=[same, pl.BlockSp...  89.5 us
    pallas_call x5, Pallas kernels, pieces(): pl.pallas_call(kernel, grid=(dps,), in_specs=[pl.BlockSpec((length, wide)...  51.9 us
    dot_general x9, matrix products, mm(): lax.dot_general(left, right, (contract, ((), ())), preferred_element_type...  37.9 us
    reduce_scatter x7, waiting for transfers between devices, over_z(): lax.psum_scatter(total, 'z', scatter_dimension=self.dim, tiled=True)  31.1 us
    pallas_call x1, Pallas kernels, product_down(): pl.pallas_call(kernel, grid=(cols // wide, inner // deep), in_specs=[pl.B...  28.2 us
    pallas_call x1, Pallas kernels, attend_pull(): pl.pallas_call(kernel, grid=(heads,), in_specs=[pl.BlockSpec(memory_space...  28 us
  transfers between devices with their start and end apart: 37, of which 23 were waited for; matrix products, arithmetic and copies ran while one was open for 13% of the time, Pallas kernels for 36%

profile of v6, /device:TPU:0, one launch (start us, length us, event | category | flops | bytes accessed | tf_op | source)
XLA Modules:
  0.0 1028.8 jit_solution(14172502522030250792)
XLA Ops:
  33.9 10.4 %shard_map.305 = (bf16[512,1024]{1,0:T(8,128)(2,1)}, f32[8,512,1]{2,1,0:T(8,128)}) custom-call(s32[1]{0:T(128)S(6)} %copy.114.boundary_ref, bf16[1024,1024]{1,0:T(8,128)(2,1)} %add_convert_fusion.2.query_ref, bf16[1024,1024]{1,0:T(8,128)(2,1)} %convolution_convert_fusion.key_ref, bf16[1024,1024]{1,0:T(8,128)(2,1)} %add_convert_fusion.1.value_ref), custom_call_target="tpu_custom_call" | custom-call | tf_op jit(solution)/shard_map/pallas_call | solution.py:178
  55.1 13.4 %shard_map.306 = (bf16[512,1024]{1,0:T(8,128)(2,1)}, f32[8,512,1]{2,1,0:T(8,128)}) custom-call(s32[1]{0:T(128)S(6)} %copy.114.boundary_ref, bf16[1024,1024]{1,0:T(8,128)(2,1)} %add_convert_fusion.2.query_ref, bf16[1024,1024]{1,0:T(8,128)(2,1)} %convolution_convert_fusion.key_ref, bf16[1024,1024]{1,0:T(8,128)(2,1)} %add_convert_fusion.1.value_ref), custom_call_target="tpu_custom_call" | custom-call | tf_op jit(solution)/shard_map/pallas_call | solution.py:178
  81.3 10.4 %shard_map.308.left_ref = bf16[1024,2048]{1,0:T(8,128)(2,1)} custom-call(bf16[1024,2048]{1,0:T(8,128)(2,1)} %copy-done.12), custom_call_target="tpu_custom_call" | custom-call | tf_op jit(solution)/shard_map/pallas_call | solution.py:347
  91.7 10.5 %shard_map.310.right_ref = bf16[1024,2048]{1,0:T(8,128)(2,1)} custom-call(bf16[1024,2048]{1,0:T(8,128)(2,1)} %dy_ref.7), custom_call_target="tpu_custom_call" | custom-call | tf_op jit(solution)/shard_map/pallas_call | solution.py:347
  102.1 10.3 %shard_map.312.right_ref = bf16[1024,2048]{1,0:T(8,128)(2,1)} custom-call(bf16[1024,2048]{1,0:T(8,128)(2,1)} %dy_ref.7), custom_call_target="tpu_custom_call" | custom-call | tf_op jit(solution)/shard_map/pallas_call | solution.py:347
  120.5 22.3 %shard_map.307 = (bf16[1024,4096]{1,0:T(8,128)(2,1)}, bf16[1024,4096]{1,0:T(8,128)(2,1)}, f32[512,2048]{1,0:T(8,128)}, f32[1,4096]{1,0:T(1,128)}) custom-call(bf16[256,2048]{1,0:T(8,128)(2,1)} %get-tuple-element.480.normed_ref, bf16[1024,2048]{1,0:T(8,128)(2,1)} %dy_ref.7, bf16[2048,4096]{1,0:T(8,128)(2,1)} %up_ref.7, f32[1,4096]{1,0:T(1,128)} %bitcast.72, ...), custom_call_target="tpu_custom_call" | custom-call | tf_op jit(solution)/shard_map/pallas_call | solution.py:280
  151.0 22.3 %shard_map.309 = (bf16[1024,4096]{1,0:T(8,128)(2,1)}, bf16[1024,4096]{1,0:T(8,128)(2,1)}, f32[512,2048]{1,0:T(8,128)}, f32[1,4096]{1,0:T(1,128)}) custom-call(bf16[256,2048]{1,0:T(8,128)(2,1)} %get-tuple-element.476.normed_ref, bf16[1024,2048]{1,0:T(8,128)(2,1)} %dy_ref.7, ...), custom_call_target="tpu_custom_call", output_to_operand_aliasing={{0}: (5, {}), {1}: (6, {}), {2}: (7, {})} | custom-call | tf_op jit(solution)/shard_map/pallas_call | solution.py:280
  173.3 15.9 %collective-permute-done.10 = f32[256,2048]{1,0:T(8,128)} collective-permute-done((f32[256,2048]{1,0:T(8,128)S(1)}, f32[256,2048]{1,0:T(8,128)}, u32[]{:S(2)}, u32[]{:S(2)}) %collective-permute-start.10) | collective-permute-done | bytes 2097184 | tf_op jit(solution)/shard_map/ppermute | solution.py:17
  194.7 22.5 %shard_map.311 = (bf16[1024,4096]{1,0:T(8,128)(2,1)}, bf16[1024,4096]{1,0:T(8,128)(2,1)}, f32[512,2048]{1,0:T(8,128)}, f32[1,4096]{1,0:T(1,128)}) custom-call(bf16[256,2048]{1,0:T(8,128)(2,1)} %get-tuple-element.472.normed_ref, bf16[1024,2048]{1,0:T(8,128)(2,1)} %dy_ref.7, bf16[2048,4096]{1,0:T(8,128)(2,1)} %up_ref.7, ...), custom_call_target="tpu_custom_call", output_to_operand_aliasing={{0}: (5, {}), {1}: (6, {})} | custom-call | tf_op jit(solution)/shard_map/pallas_call | solution.py:280
  217.2 16.0 %collective-permute-done.11 = f32[256,2048]{1,0:T(8,128)} collective-permute-done((f32[256,2048]{1,0:T(8,128)}, f32[256,2048]{1,0:T(8,128)}, u32[]{:S(2)}, u32[]{:S(2)}) %collective-permute-start.11) | collective-permute-done | bytes 2097184 | tf_op jit(solution)/shard_map/ppermute | solution.py:17
  240.1 22.3 %shard_map.313 = (bf16[1024,4096]{1,0:T(8,128)(2,1)}, bf16[1024,4096]{1,0:T(8,128)(2,1)}, f32[512,2048]{1,0:T(8,128)}, f32[1,4096]{1,0:T(1,128)}) custom-call(bf16[256,2048]{1,0:T(8,128)(2,1)} %get-tuple-element.468.normed_ref, bf16[1024,2048]{1,0:T(8,128)(2,1)} %dy_ref.7, ...), custom_call_target="tpu_custom_call", output_to_operand_aliasing={{0}: (5, {}), {1}: (6, {}), {2}: (7, {})} | custom-call | tf_op jit(solution)/shard_map/pallas_call | solution.py:280
  262.4 9.9 shard_map.318
  272.3 13.5 %while.80 = (s32[]{:T(128)}, f32[2048,1024]{1,0:T(8,128)}, s32[]{:T(128)}, f32[2048,1024]{1,0:T(8,128)}, s32[]{:T(128)}) while((s32[]{:T(128)}, f32[2048,1024]{1,0:T(8,128)}, s32[]{:T(128)}, f32[2048,1024]{1,0:T(8,128)}, s32[]{:T(128)}) %tuple.282), condition=%wide.region_11.12_spmd, body=%wide.region_10.0_spmd.sunk | while | flops 2 | bytes 33554532 | solution.py:362
  272.3 13.5 %collective-permute-done = f32[2048,1024]{1,0:T(8,128)} collective-permute-done((f32[2048,1024]{1,0:T(8,128)}, f32[2048,1024]{1,0:T(8,128)}, u32[]{:S(2)}, u32[]{:S(2)}) %collective-permute-start) | collective-permute-done | bytes 8388640 | tf_op jit(solution)/shard_map/while/body/ppermute | solution.py:17
  285.8 11.9 %shard_map.319 = f32[2048,1024]{1,0:T(8,128)} custom-call(s32[4]{0:T(128)} %get-tuple-element.498.starts_ref, bf16[1024,4096]{1,0:T(8,128)(2,1)} %get-tuple-element.310.left_ref, bf16[1024,2048]{1,0:T(8,128)(2,1)} %shard_map.310.right_ref, f32[2048,1024]{1,0:T(8,128)} %get-tuple-element.299.rest_0_), custom_call_target="tpu_custom_call" | custom-call | tf_op jit(solution)/shard_map/pallas_call | solution.py:89
  300.3 9.9 shard_map.320
  310.2 13.5 %while.81 = (s32[]{:T(128)}, f32[2048,1024]{1,0:T(8,128)}, s32[]{:T(128)}, f32[2048,1024]{1,0:T(8,128)}, s32[]{:T(128)}) while((s32[]{:T(128)}, f32[2048,1024]{1,0:T(8,128)}, s32[]{:T(128)}, f32[2048,1024]{1,0:T(8,128)}, s32[]{:T(128)}) %tuple.285), condition=%wide.region_13.14_spmd, body=%wide.region_12.13_spmd.sunk | while | flops 2 | bytes 33554532 | solution.py:362
  310.2 13.5 %collective-permute-done.1 = f32[2048,1024]{1,0:T(8,128)} collective-permute-done((f32[2048,1024]{1,0:T(8,128)}, f32[2048,1024]{1,0:T(8,128)}, u32[]{:S(2)}, u32[]{:S(2)}) %collective-permute-start.1) | collective-permute-done | bytes 8388640 | tf_op jit(solution)/shard_map/while/body/ppermute | solution.py:17
  323.7 8.1 shard_map.321
  333.3 6.7 convert_element_type.66
  342.9 10.4 %shard_map.314.left_ref = bf16[1024,2048]{1,0:T(8,128)(2,1)} custom-call(bf16[1024,2048]{1,0:T(8,128)(2,1)} %pad_maximum_fusion.1.field_ref), custom_call_target="tpu_custom_call" | custom-call | tf_op jit(solution)/shard_map/pallas_call | solution.py:347
  353.3 11.3 %shard_map.322 = f32[1024,2048]{1,0:T(8,128)} custom-call(s32[4]{0:T(128)} %get-tuple-element.500.starts_ref, bf16[1024,2048]{1,0:T(8,128)(2,1)} %shard_map.314.left_ref, bf16[1024,4096]{1,0:T(8,128)(2,1)} %get-tuple-element.342.right_ref), custom_call_target="tpu_custom_call" | custom-call | tf_op jit(solution)/shard_map/pallas_call | solution.py:89
  364.6 13.5 %while.82 = (s32[]{:T(128)}, f32[1024,2048]{1,0:T(8,128)}, s32[]{:T(128)}, f32[1024,2048]{1,0:T(8,128)}, s32[]{:T(128)}) while((s32[]{:T(128)}, f32[1024,2048]{1,0:T(8,128)}, s32[]{:T(128)}, f32[1024,2048]{1,0:T(8,128)}, s32[]{:T(128)}) %tuple.288), condition=%wide.region_15.16_spmd, body=%wide.region_14.15_spmd.sunk | while | flops 2 | bytes 33554532 | solution.py:362
  364.6 13.5 %collective-permute-done.2 = f32[1024,2048]{1,0:T(8,128)} collective-permute-done((f32[1024,2048]{1,0:T(8,128)}, f32[1024,2048]{1,0:T(8,128)}, u32[]{:S(2)}, u32[]{:S(2)}) %collective-permute-start.2) | collective-permute-done | bytes 8388640 | tf_op jit(solution)/shard_map/while/body/ppermute | solution.py:17
  378.1 7.5 shard_map.323
  390.8 6.4 multiply_reduce_fusion.5
  406.2 18.6 %collective-permute-done.13.rest_1_ = f32[2048,512]{1,0:T(8,128)} collective-permute-done((f32[2048,512]{1,0:T(8,128)}, f32[2048,512]{1,0:T(8,128)}, u32[]{:S(2)}, u32[]{:S(2)}) %collective-permute-start.13) | collective-permute-done | bytes 4194336 | tf_op jit(solution)/shard_map/ppermute | solution.py:17
  424.8 9.4 shard_map.324
  437.4 28.2 %shard_map.325 = f32[1024,2048]{1,0:T(8,128)} custom-call(bf16[1024,4096]{1,0:T(8,128)(2,1)} %get-tuple-element.310.left_ref, bf16[4096,2048]{1,0:T(8,128)(2,1)} %right_ref.1), custom_call_target="tpu_custom_call" | custom-call | tf_op jit(solution)/shard_map/pallas_call | solution.py:117
  465.6 11.3 %shard_map.327 = f32[1024,2048]{1,0:T(8,128)} custom-call(s32[4]{0:T(128)} %get-tuple-element.496.starts_ref, bf16[1024,2048]{1,0:T(8,128)(2,1)} %shard_map.314.left_ref, bf16[1024,4096]{1,0:T(8,128)(2,1)} %get-tuple-element.342.right_ref), custom_call_target="tpu_custom_call" | custom-call | tf_op jit(solution)/shard_map/pallas_call | solution.py:89
  476.9 49.6 %collective-permute-done.14 = f32[512,2048]{1,0:T(8,128)} collective-permute-done((f32[512,2048]{1,0:T(8,128)}, f32[512,2048]{1,0:T(8,128)}, u32[]{:S(2)}, u32[]{:S(2)}) %collective-permute-start.14) | collective-permute-done | bytes 4194336 | tf_op jit(solution)/shard_map/ppermute | solution.py:17
  540.3 13.6 %while.83 = (s32[]{:T(128)}, f32[1024,2048]{1,0:T(8,128)}, s32[]{:T(128)}, f32[1024,2048]{1,0:T(8,128)}, s32[]{:T(128)}) while((s32[]{:T(128)}, f32[1024,2048]{1,0:T(8,128)}, s32[]{:T(128)}, f32[1024,2048]{1,0:T(8,128)}, s32[]{:T(128)}) %tuple.291), condition=%wide.region_21.22_spmd, body=%wide.region_20.21_spmd.sunk | while | flops 2 | bytes 33554532 | solution.py:362
  540.3 13.5 %collective-permute-done.3 = f32[1024,2048]{1,0:T(8,128)} collective-permute-done((f32[1024,2048]{1,0:T(8,128)}, f32[1024,2048]{1,0:T(8,128)}, u32[]{:S(2)}, u32[]{:S(2)}) %collective-permute-start.3) | collective-permute-done | bytes 8388640 | tf_op jit(solution)/shard_map/while/body/ppermute | solution.py:17
  554.0 7.1 shard_map.329
  561.1 8.3 shard_map.330
  577.5 28.0 %shard_map.331 = (bf16[1024,1024]{1,0:T(8,128)(2,1)}, bf16[1024,1024]{1,0:T(8,128)(2,1)}, bf16[1024,1024]{1,0:T(8,128)(2,1)}, f32[8,1,128]{2,1,0:T(1,128)}, f32[8,1,128]{2,1,0:T(1,128)}) custom-call(s32[1]{0:T(128)S(6)} %copy.114.boundary_ref, bf16[1024,1024]{1,0:T(8,128)(2,1)} %add_convert_fusion.2.query_ref, ...), custom_call_target="tpu_custom_call" | custom-call | tf_op jit(solution)/shard_map/pallas_call | solution.py:237
  605.4 8.9 shard_map.333
  614.4 15.7 %shard_map.332 = f32[768,2048]{1,0:T(8,128)} custom-call(bf16[1024,1024]{1,0:T(8,128)(2,1)} %get-tuple-element.348.refs_0_.right_ref, bf16[1024,1024]{1,0:T(8,128)(2,1)} %get-tuple-element.352.refs_1_.right_ref, bf16[1024,1024]{1,0:T(8,128)(2,1)} %get-tuple-element.356.refs_2_.right_ref, bf16[2048,1024]{1,0:T(8,128)(2,1)} %refs_3_.3, ...), custom_call_target="tpu_custom_call" | custom-call | tf_op jit(solution)/shard_map/pallas_call | solution.py:141
  634.3 10.3 %shard_map.340.right_ref = bf16[1024,2048]{1,0:T(8,128)(2,1)} custom-call(bf16[1024,2048]{1,0:T(8,128)(2,1)} %pad_maximum_fusion.4.field_ref), custom_call_target="tpu_custom_call" | custom-call | tf_op jit(solution)/shard_map/pallas_call | solution.py:347
  644.6 6.5 shard_map.334
  651.1 6.5 shard_map.341
  657.6 6.5 shard_map.338
  664.1 7.5 while.84
  664.1 7.5 collective-permute-done.4
  671.6 6.5 shard_map.336
  678.1 7.5 while.85
  678.2 7.4 collective-permute-done.5
  685.6 7.8 while.86
  686.0 7.4 collective-permute-done.6
  693.3 7.5 while.87
  693.5 7.4 collective-permute-done.7
  707.6 11.3 %fusion = bf16[1024,2048]{1,0:T(8,128)(2,1)} fusion(f32[256,2048]{1,0:T(8,128)} %copy-done.6, f32[256,2048]{1,0:T(8,128)} %copy-done.5, f32[256,2048]{1,0:T(8,128)} %copy-done.4, f32[256,2048]{1,0:T(8,128)S(1)} %copy-done.3, f32[1024,2048]{1,0:T(8,128)} %shard_map.325, f32[1024,2048]{1,0:T(8,128)} %collective-permute-done.15, f32[2048]{0:T(1024)S(1)} %copy-done.45), kind=kLoop, calls=%fused_computation.1 | loop fusion | flops 14680064 | bytes 29368320 | tf_op jit(solution)/shard_map/convert_element_type | solution.py:534
  719.0 8.3 shard_map.343
  737.3 40.2 %collective-permute-done.19.rest_1_ = f32[1024,512]{1,0:T(8,128)} collective-permute-done((f32[1024,512]{1,0:T(8,128)S(1)}, f32[1024,512]{1,0:T(8,128)}, u32[]{:S(2)}, u32[]{:S(2)}) %collective-permute-start.19) | collective-permute-done | bytes 2097184 | tf_op jit(solution)/shard_map/ppermute | solution.py:17
  790.6 31.8 %collective-permute-done.20.rest_1_ = f32[512,1024]{1,0:T(8,128)} collective-permute-done((f32[512,1024]{1,0:T(8,128)}, f32[512,1024]{1,0:T(8,128)}, u32[]{:S(2)}, u32[]{:S(2)}) %collective-permute-start.20) | collective-permute-done | bytes 2097184 | tf_op jit(solution)/shard_map/ppermute | solution.py:17
  822.5 6.5 shard_map.347
  828.9 6.0 shard_map.348
  834.9 28.9 %collective-permute-done.17 = f32[768,2048]{1,0:T(8,128)} collective-permute-done((f32[768,2048]{1,0:T(8,128)}, f32[768,2048]{1,0:T(8,128)}, u32[]{:S(2)}, u32[]{:S(2)}) %collective-permute-start.17) | collective-permute-done | bytes 6291488 | tf_op jit(solution)/shard_map/ppermute | solution.py:17
  863.8 7.9 multiply_reduce_fusion.1
  878.8 6.6 shard_map.349
  894.3 38.0 %collective-permute-done.21 = f32[256,2048]{1,0:T(8,128)} collective-permute-done((f32[256,2048]{1,0:T(8,128)S(1)}, f32[256,2048]{1,0:T(8,128)}, u32[]{:S(2)}, u32[]{:S(2)}) %collective-permute-start.21) | collective-permute-done | bytes 2097184 | tf_op jit(solution)/shard_map/ppermute | solution.py:17
  942.8 6.5 shard_map.350
  966.6 16.1 %collective-permute-done.28 = f32[2048,128]{1,0:T(8,128)} collective-permute-done((f32[2048,128]{1,0:T(8,128)}, f32[2048,128]{1,0:T(8,128)}, u32[]{:S(2)}, u32[]{:S(2)}) %collective-permute-start.28) | collective-permute-done | bytes 1048608 | tf_op jit(solution)/shard_map/ppermute | solution.py:17
  990.5 31.1 %reduce-scatter.13.cloned.1.call-done = f32[128,1024]{1,0:T(8,128)} async-done(((f32[512,1024]{1,0:T(8,128)}), f32[128,1024]{1,0:T(8,128)}) %reduce-scatter.13.cloned.1.call-update) | async-done | bytes 524304 | tf_op jit(solution)/shard_map/reduce_scatter | solution.py:398
  (299 shorter events, 209.6 us)
Async XLA Ops:
  7.2 948.9 %reduce-scatter.21.cloned.1.call-start = ((), (), s32[]{:S(2)}) async-start(), calls=%async_computation.14 | async-start | bytes 10485760 | tf_op jit(solution)/shard_map/reduce_scatter | solution.py:403
  16.8 11.4 %copy-start.12 = (bf16[1024,2048]{1,0:T(8,128)(2,1)}, bf16[1024,2048]{1,0:T(8,128)(2,1)S(1)}, u32[]{:S(2)}) copy-start(bf16[1024,2048]{1,0:T(8,128)(2,1)S(1)} %get-tuple-element.485.field_ref) | copy-start | bytes 12582916
  44.4 8.1 copy-start.27
  44.4 8.1 copy-start.48
  49.5 64.2 %collective-permute-start.8 = (f32[256,2048]{1,0:T(8,128)}, f32[256,2048]{1,0:T(8,128)}, u32[]{:S(2)}, u32[]{:S(2)}) collective-permute-start(f32[256,2048]{1,0:T(8,128)} %fusion.10), channel_id=1, source_target_pairs={{0,1},{1,0},{2,3},{3,2},{4,5},{5,4},{6,7},{7,6},{8,9},{9,8},{10,11... | collective-permute-start | bytes 6291464 | tf_op jit(solution)/shard_map/ppermute | solution.py:17
  55.1 89.1 %collective-permute-start.9 = (f32[256,2048]{1,0:T(8,128)}, f32[256,2048]{1,0:T(8,128)}, u32[]{:S(2)}, u32[]{:S(2)}) collective-permute-start(f32[256,2048]{1,0:T(8,128)} %fusion.6), channel_id=1, source_target_pairs={{0,1},{1,0},{2,3},{3,2},{4,5},{5,4},{6,7},{7,6},{8,9},{9,8},{10,11... | collective-permute-start | bytes 6291464 | tf_op jit(solution)/shard_map/ppermute | solution.py:17
  68.5 5.9 copy-start.29
  72.3 116.9 %collective-permute-start.10 = (f32[256,2048]{1,0:T(8,128)S(1)}, f32[256,2048]{1,0:T(8,128)}, u32[]{:S(2)}, u32[]{:S(2)}) collective-permute-start(f32[256,2048]{1,0:T(8,128)S(1)} %fusion.4), channel_id=1, source_target_pairs={{0,1},{1,0},{2,3},{3,2},{4,5},{5,4},{6,7},{7,6},{8,9},{9,8},{10,11... | collective-permute-start | bytes 6291464 | tf_op jit(solution)/shard_map/ppermute | solution.py:17
  77.0 156.3 %collective-permute-start.11 = (f32[256,2048]{1,0:T(8,128)}, f32[256,2048]{1,0:T(8,128)}, u32[]{:S(2)}, u32[]{:S(2)}) collective-permute-start(f32[256,2048]{1,0:T(8,128)} %fusion.8), channel_id=1, source_target_pairs={{0,1},{1,0},{2,3},{3,2},{4,5},{5,4},{6,7},{7,6},{8,9},{9,8},{10,11... | collective-permute-start | bytes 6291464 | tf_op jit(solution)/shard_map/ppermute | solution.py:17
  272.3 13.5 %collective-permute-start = (f32[2048,1024]{1,0:T(8,128)}, f32[2048,1024]{1,0:T(8,128)}, u32[]{:S(2)}, u32[]{:S(2)}) collective-permute-start(f32[2048,1024]{1,0:T(8,128)} %get-tuple-element.682), channel_id=1, source_target_pairs={{0,2},{2,0},{1,3},{3,1},{4,6},{6,4},{5,7},{7,5},{8,10},{10,8},{9,1... | collective-permute-start | bytes 25165832 | tf_op jit(solution)/shard_map/while/body/ppermute | solution.py:17
  297.8 686.9 %reduce-scatter.23.cloned.1.call-start = ((), (), s32[]{:S(2)}) async-start(), calls=%async_computation.15 | async-start | bytes 5242880 | tf_op jit(solution)/shard_map/reduce_scatter | solution.py:398
  297.8 93.0 %collective-permute-start.12 = (f32[512,2048]{1,0:T(8,128)}, f32[512,2048]{1,0:T(8,128)}, u32[]{:S(2)}, u32[]{:S(2)}) collective-permute-start(f32[512,2048]{1,0:T(8,128)} %get-tuple-element.295), channel_id=1, source_target_pairs={{0,1},{1,0},{2,3},{3,2},{4,5},{5,4},{6,7},{7,6},{8,9},{9,8},{10,11... | collective-permute-start | bytes 12582920 | tf_op jit(solution)/shard_map/ppermute | solution.py:17
  310.2 13.5 %collective-permute-start.1 = (f32[2048,1024]{1,0:T(8,128)}, f32[2048,1024]{1,0:T(8,128)}, u32[]{:S(2)}, u32[]{:S(2)}) collective-permute-start(f32[2048,1024]{1,0:T(8,128)} %get-tuple-element.686), channel_id=1, source_target_pairs={{0,2},{2,0},{1,3},{3,1},{4,6},{6,4},{5,7},{7,5},{8,10},{10,8},{9,1... | collective-permute-start | bytes 25165832 | tf_op jit(solution)/shard_map/while/body/ppermute | solution.py:17
  331.8 93.0 %collective-permute-start.13 = (f32[2048,512]{1,0:T(8,128)}, f32[2048,512]{1,0:T(8,128)}, u32[]{:S(2)}, u32[]{:S(2)}) collective-permute-start(f32[2048,512]{1,0:T(8,128)} %shard_map.321), channel_id=1, source_target_pairs={{0,4},{4,0},{1,5},{5,1},{2,6},{6,2},{3,7},{7,3},{8,12},{12,8},{9,1... | collective-permute-start | bytes 12582920 | tf_op jit(solution)/shard_map/ppermute | solution.py:17
  333.3 7.3 copy-start.18
  333.3 7.3 copy-start.19
  333.3 7.3 copy-start.20
  333.3 7.3 copy-start.21
  364.6 13.5 %collective-permute-start.2 = (f32[1024,2048]{1,0:T(8,128)}, f32[1024,2048]{1,0:T(8,128)}, u32[]{:S(2)}, u32[]{:S(2)}) collective-permute-start(f32[1024,2048]{1,0:T(8,128)} %get-tuple-element.690), channel_id=1, source_target_pairs={{0,2},{2,0},{1,3},{3,1},{4,6},{6,4},{5,7},{7,5},{8,10},{10,8},{9,1... | collective-permute-start | bytes 25165832 | tf_op jit(solution)/shard_map/while/body/ppermute | solution.py:17
  390.8 6.4 copy-start.9
  390.8 6.4 copy-start.11
  434.2 553.2 %reduce-scatter.17.cloned.1.call-start = ((), (), s32[]{:S(2)}) async-start(), calls=%async_computation.12 | async-start | bytes 5242880 | tf_op jit(solution)/shard_map/reduce_scatter | solution.py:398
  434.3 92.2 %collective-permute-start.14 = (f32[512,2048]{1,0:T(8,128)}, f32[512,2048]{1,0:T(8,128)}, u32[]{:S(2)}, u32[]{:S(2)}) collective-permute-start(f32[512,2048]{1,0:T(8,128)} %get-tuple-element.311), channel_id=1, source_target_pairs={{0,1},{1,0},{2,3},{3,2},{4,5},{5,4},{6,7},{7,6},{8,9},{9,8},{10,11... | collective-permute-start | bytes 12582920 | tf_op jit(solution)/shard_map/ppermute | solution.py:17
  434.5 126.5 %collective-permute-start.16 = (f32[512,2048]{1,0:T(8,128)}, f32[512,2048]{1,0:T(8,128)}, u32[]{:S(2)}, u32[]{:S(2)}) collective-permute-start(f32[512,2048]{1,0:T(8,128)} %shard_map.323), channel_id=1, source_target_pairs={{0,4},{4,0},{1,5},{5,1},{2,6},{6,2},{3,7},{7,3},{8,12},{12,8},{9,1... | collective-permute-start | bytes 12582920 | tf_op jit(solution)/shard_map/ppermute | solution.py:17
  526.5 181.2 %collective-permute-start.15 = (f32[1024,2048]{1,0:T(8,128)}, f32[1024,2048]{1,0:T(8,128)}, u32[]{:S(2)}, u32[]{:S(2)}) collective-permute-start(f32[1024,2048]{1,0:T(8,128)} %shard_map.325), channel_id=1, source_target_pairs={{0,1},{1,0},{2,3},{3,2},{4,5},{5,4},{6,7},{7,6},{8,9},{9,8},{10,11... | collective-permute-start | bytes 25165832 | tf_op jit(solution)/shard_map/ppermute | solution.py:17
  540.3 13.5 %collective-permute-start.3 = (f32[1024,2048]{1,0:T(8,128)}, f32[1024,2048]{1,0:T(8,128)}, u32[]{:S(2)}, u32[]{:S(2)}) collective-permute-start(f32[1024,2048]{1,0:T(8,128)} %get-tuple-element.694), channel_id=1, source_target_pairs={{0,2},{2,0},{1,3},{3,1},{4,6},{6,4},{5,7},{7,5},{8,10},{10,8},{9,1... | collective-permute-start | bytes 25165832 | tf_op jit(solution)/shard_map/while/body/ppermute | solution.py:17
  569.4 418.0 %reduce-scatter.19.cloned.1.call-start = ((), (), s32[]{:S(2)}) async-start(), calls=%async_computation.13 | async-start | bytes 5242880 | tf_op jit(solution)/shard_map/reduce_scatter | solution.py:398
  569.5 149.5 %collective-permute-start.18 = (f32[512,2048]{1,0:T(8,128)}, f32[512,2048]{1,0:T(8,128)}, u32[]{:S(2)}, u32[]{:S(2)}) collective-permute-start(f32[512,2048]{1,0:T(8,128)} %shard_map.329), channel_id=1, source_target_pairs={{0,4},{4,0},{1,5},{5,1},{2,6},{6,2},{3,7},{7,3},{8,12},{12,8},{9,1... | collective-permute-start | bytes 12582920 | tf_op jit(solution)/shard_map/ppermute | solution.py:17
  573.7 31.8 %copy-start.8 = (bf16[1024,1024]{1,0:T(8,128)(2,1)}, bf16[1024,1024]{1,0:T(8,128)(2,1)S(1)}, u32[]{:S(2)}) copy-start(bf16[1024,1024]{1,0:T(8,128)(2,1)S(1)} %constant_dynamic-update-slice_fusion.left_ref) | copy-start | bytes 6291460
  614.4 15.7 %copy-start.24 = (bf16[512,2048]{1,0:T(8,128)(2,1)S(1)}, bf16[512,2048]{1,0:T(8,128)(2,1)}, u32[]{:S(2)}) copy-start(bf16[512,2048]{1,0:T(8,128)(2,1)} %copy-done.23) | copy-start | bytes 6291460
  664.1 7.5 collective-permute-start.4
  678.1 7.5 collective-permute-start.5
  685.8 7.6 collective-permute-start.6
  693.3 7.5 collective-permute-start.7
  700.8 6.8 copy-start.3
  700.8 6.8 copy-start.45
  727.3 263.1 %reduce-scatter.15.cloned.1.call-start = ((), (), s32[]{:S(2)}) async-start(), calls=%async_computation.11 | async-start | bytes 2621440 | tf_op jit(solution)/shard_map/reduce_scatter | solution.py:398
  727.4 136.4 %collective-permute-start.17 = (f32[768,2048]{1,0:T(8,128)}, f32[768,2048]{1,0:T(8,128)}, u32[]{:S(2)}, u32[]{:S(2)}) collective-permute-start(f32[768,2048]{1,0:T(8,128)} %shard_map.332), channel_id=1, source_target_pairs={{0,1},{1,0},{2,3},{3,2},{4,5},{5,4},{6,7},{7,6},{8,9},{9,8},{10,11... | collective-permute-start | bytes 18874376 | tf_op jit(solution)/shard_map/ppermute | solution.py:17
  728.9 48.6 %collective-permute-start.19 = (f32[1024,512]{1,0:T(8,128)S(1)}, f32[1024,512]{1,0:T(8,128)}, u32[]{:S(2)}, u32[]{:S(2)}) collective-permute-start(f32[1024,512]{1,0:T(8,128)S(1)} %copy-done.26), channel_id=1, source_target_pairs={{0,4},{4,0},{1,5},{5,1},{2,6},{6,2},{3,7},{7,3},{8,12},{12,8},{9,1... | collective-permute-start | bytes 6291464 | tf_op jit(solution)/shard_map/ppermute | solution.py:17
  736.2 86.3 %collective-permute-start.20 = (f32[512,1024]{1,0:T(8,128)}, f32[512,1024]{1,0:T(8,128)}, u32[]{:S(2)}, u32[]{:S(2)}) collective-permute-start(f32[512,1024]{1,0:T(8,128)} %shard_map.344), channel_id=1, source_target_pairs={{0,4},{4,0},{1,5},{5,1},{2,6},{6,2},{3,7},{7,3},{8,12},{12,8},{9,1... | collective-permute-start | bytes 6291464 | tf_op jit(solution)/shard_map/ppermute | solution.py:17
  783.3 207.1 %reduce-scatter.11.cloned.1.call-start = ((), (), s32[]{:S(2)}) async-start(), calls=%async_computation.9 | async-start | bytes 2621440 | tf_op jit(solution)/shard_map/reduce_scatter | solution.py:398
  789.2 89.5 %collective-permute-start.22 = (f32[512,1024]{1,0:T(8,128)}, f32[512,1024]{1,0:T(8,128)}, u32[]{:S(2)}, u32[]{:S(2)}) collective-permute-start(f32[512,1024]{1,0:T(8,128)} %shard_map.346), channel_id=1, source_target_pairs={{0,4},{4,0},{1,5},{5,1},{2,6},{6,2},{3,7},{7,3},{8,12},{12,8},{9,1... | collective-permute-start | bytes 6291464 | tf_op jit(solution)/shard_map/ppermute | solution.py:17
  828.9 34.8 %copy-start.32 = (f32[2048]{0:T(1024)S(1)}, f32[2048]{0:T(1024)}, u32[]{:S(2)}) copy-start(f32[2048]{0:T(1024)} %param.36) | copy-start | bytes 24580
  863.8 7.9 slice-start
  863.8 8.9 slice-start.1
  863.8 10.1 copy-start.7
  863.8 11.3 %copy-start.16 = (f32[512,2048]{1,0:T(8,128)S(1)}, f32[512,2048]{1,0:T(8,128)}, u32[]{:S(2)}) copy-start(f32[512,2048]{1,0:T(8,128)} %get-tuple-element.463) | copy-start | bytes 12582916
  863.8 11.3 %copy-start.36 = (f32[1024]{0:T(1024)S(1)}, f32[1024]{0:T(1024)}, u32[]{:S(2)}) copy-start(f32[1024]{0:T(1024)} %copy-done.35) | copy-start | bytes 12292
  878.7 6.8 copy-start.22
  885.4 6.1 copy-start.47
  885.4 7.0 copy-start.46
  885.4 7.9 copy-start.38
  885.5 7.9 copy-start.37
  885.5 7.9 copy-start.39
  885.5 105.0 %reduce-scatter.9.cloned.1.call-start = ((), (), s32[]{:S(2)}) async-start(), calls=%async_computation.8 | async-start | bytes 2621440 | tf_op jit(solution)/shard_map/reduce_scatter | solution.py:398
  885.5 46.7 %collective-permute-start.21 = (f32[256,2048]{1,0:T(8,128)S(1)}, f32[256,2048]{1,0:T(8,128)}, u32[]{:S(2)}, u32[]{:S(2)}) collective-permute-start(f32[256,2048]{1,0:T(8,128)S(1)} %copy-done.22), channel_id=1, source_target_pairs={{0,1},{1,0},{2,3},{3,2},{4,5},{5,4},{6,7},{7,6},{8,9},{9,8},{10,11... | collective-permute-start | bytes 6291464 | tf_op jit(solution)/shard_map/ppermute | solution.py:17
  887.3 134.2 %reduce-scatter.13.cloned.1.call-start = ((), (), s32[]{:S(2)}) async-start(), calls=%async_computation.10 | async-start | bytes 2621440 | tf_op jit(solution)/shard_map/reduce_scatter | solution.py:398
  893.4 49.5 %collective-permute-start.27 = (f32[512,1024]{1,0:T(8,128)}, f32[512,1024]{1,0:T(8,128)}, u32[]{:S(2)}, u32[]{:S(2)}) collective-permute-start(f32[512,1024]{1,0:T(8,128)} %shard_map.348), channel_id=1, source_target_pairs={{0,4},{4,0},{1,5},{5,1},{2,6},{6,2},{3,7},{7,3},{8,12},{12,8},{9,1... | collective-permute-start | bytes 6291464 | tf_op jit(solution)/shard_map/ppermute | solution.py:17
  936.7 1.3 collective-permute-start.23
  938.1 11.3 %collective-permute-start.24 = (f32[4,1152]{1,0:T(4,128)S(1)}, f32[4,1152]{1,0:T(4,128)S(1)}, u32[]{:S(2)}, u32[]{:S(2)}) collective-permute-start(f32[4,1152]{1,0:T(4,128)S(1)} %bitcast.84), channel_id=1, source_target_pairs={{0,4},{4,0},{1,5},{5,1},{2,6},{6,2},{3,7},{7,3},{8,12},{12,8},{9,1... | collective-permute-start | bytes 55304 | tf_op jit(solution)/shard_map/ppermute | solution.py:17
  949.4 10.8 %copy-start.17 = (bf16[768,2048]{1,0:T(8,128)(2,1)S(1)}, bf16[768,2048]{1,0:T(8,128)(2,1)}, u32[]{:S(2)}) copy-start(bf16[768,2048]{1,0:T(8,128)(2,1)} %fusion.2) | copy-start | bytes 9437188
  949.5 5.4 collective-permute-start.25
  954.9 8.9 collective-permute-start.26
  958.4 24.3 %collective-permute-start.28 = (f32[2048,128]{1,0:T(8,128)}, f32[2048,128]{1,0:T(8,128)}, u32[]{:S(2)}, u32[]{:S(2)}) collective-permute-start(f32[2048,128]{1,0:T(8,128)} %constant_dynamic-slice_fusion), channel_id=1, source_target_pairs={{0,4},{4,0},{1,5},{5,1},{2,6},{6,2},{3,7},{7,3},{8,12},{12,8},{9,1... | collective-permute-start | bytes 3145736 | tf_op jit(solution)/shard_map/ppermute | solution.py:17
  (29 other events, 118.4 us)
Sparse Core Ops, SparseCore 0:
  297.9 146.0 reduce-scatter.20
  446.3 77.4 reduce-scatter.22
  569.5 77.9 reduce-scatter.16
  727.5 76.8 reduce-scatter.18
  807.0 44.1 reduce-scatter.14
  885.5 44.1 reduce-scatter.10
  932.6 43.1 reduce-scatter.8
  978.7 42.8 reduce-scatter.12

commit v7 on v6

--- a/solution.py
+++ b/solution.py
@@ -531,9 +531,17 @@
     for item in sums:
         gate = item.meet(gate)
     gate = out_sum.over_x(gate)
-    outputs = (jnp.concatenate(resids, 0) + ((branch + after(branch_other, gate)) + down_bias)).astype(BF16)
-    gate = ups[1].over_z(outputs)
+
+    def finish(begin, end, gate):
+        rows = slice(begin * chunk, end * chunk)
+        other = after(branch_other, gate)
+        return (jnp.concatenate(resids[begin:end], 0) + ((branch[rows] + other[rows]) + down_bias)).astype(BF16)
+
+    outputs = [finish(0, 1, gate)]
+    gate = ups[1].over_z(outputs[0])
     gate = query_sum.over_x(gate)
+    outputs.append(finish(1, CHUNKS, gate))
+    outputs = jnp.concatenate(outputs, 0)
     gate = out_sum.over_z(gate)
     gate = key_sum.over_x(gate)
 

time: 1040 us -> 1030 us (level)
  transfers between devices with their start and end apart: 37 -> 37, of which waited for: 23 -> 23; matrix products, arithmetic and copies ran while one was open for 13% -> 14% of each run, Pallas kernels for 36% -> 36%
where the time goes in v7:
time: 1030 us; the launch traced here: 1020 us
  Pallas kernels  424 us (41%)
  waiting for transfers between devices  372 us (36%)
  other arithmetic  131 us (13%)
  matrix products  37.8 us (4%)
  starting transfers between devices  24.8 us (2%)
  local copies, waits for them, and re-layouts  16.9 us (2%)
  between operations  16.1 us (2%)
    ppermute x27, waiting for transfers between devices, swap(): return lax.ppermute(value, axis, [(0, 1), (1, 0)])  346 us
    pallas_call x23, Pallas kernels, paired(): pl.pallas_call(kernel, grid_spec=pltpu.PrefetchScalarGridSpec(num_scalar_...  178 us
    pallas_call x4, Pallas kernels, hidden_step(): pl.pallas_call(kernel, grid=(local // block,), in_specs=[same, pl.BlockSp...  89.5 us
    pallas_call x5, Pallas kernels, pieces(): pl.pallas_call(kernel, grid=(dps,), in_specs=[pl.BlockSpec((length, wide)...  51.7 us
    dot_general x9, matrix products, mm(): lax.dot_general(left, right, (contract, ((), ())), preferred_element_type...  37.8 us
    pallas_call x1, Pallas kernels, product_down(): pl.pallas_call(kernel, grid=(cols // wide, inner // deep), in_specs=[pl.B...  28.2 us
    pallas_call x1, Pallas kernels, attend_pull(): pl.pallas_call(kernel, grid=(heads,), in_specs=[pl.BlockSpec(memory_space...  28 us
    reduce_scatter x7, waiting for transfers between devices, over_z(): lax.psum_scatter(total, 'z', scatter_dimension=self.dim, tiled=True)  26 us
  transfers between devices with their start and end apart: 37, of which 23 were waited for; matrix products, arithmetic and copies ran while one was open for 14% of the time, Pallas kernels for 36%

profile of v7, /device:TPU:0, one launch (start us, length us, event | category | flops | bytes accessed | tf_op | source)
XLA Modules:
  0.0 1023.0 jit_solution(2375487983413309374)
XLA Ops:
  34.0 10.4 %shard_map.305 = (bf16[512,1024]{1,0:T(8,128)(2,1)}, f32[8,512,1]{2,1,0:T(8,128)}) custom-call(s32[1]{0:T(128)S(6)} %copy.114.boundary_ref, bf16[1024,1024]{1,0:T(8,128)(2,1)} %add_convert_fusion.2.query_ref, bf16[1024,1024]{1,0:T(8,128)(2,1)} %convolution_convert_fusion.key_ref, bf16[1024,1024]{1,0:T(8,128)(2,1)} %add_convert_fusion.1.value_ref), custom_call_target="tpu_custom_call" | custom-call | tf_op jit(solution)/shard_map/pallas_call | solution.py:178
  55.1 13.3 %shard_map.306 = (bf16[512,1024]{1,0:T(8,128)(2,1)}, f32[8,512,1]{2,1,0:T(8,128)}) custom-call(s32[1]{0:T(128)S(6)} %copy.114.boundary_ref, bf16[1024,1024]{1,0:T(8,128)(2,1)} %add_convert_fusion.2.query_ref, bf16[1024,1024]{1,0:T(8,128)(2,1)} %convolution_convert_fusion.key_ref, bf16[1024,1024]{1,0:T(8,128)(2,1)} %add_convert_fusion.1.value_ref), custom_call_target="tpu_custom_call" | custom-call | tf_op jit(solution)/shard_map/pallas_call | solution.py:178
  81.4 10.3 %shard_map.308.left_ref = bf16[1024,2048]{1,0:T(8,128)(2,1)} custom-call(bf16[1024,2048]{1,0:T(8,128)(2,1)} %copy-done.13), custom_call_target="tpu_custom_call" | custom-call | tf_op jit(solution)/shard_map/pallas_call | solution.py:347
  91.7 10.4 %shard_map.310.right_ref = bf16[1024,2048]{1,0:T(8,128)(2,1)} custom-call(bf16[1024,2048]{1,0:T(8,128)(2,1)} %dy_ref.7), custom_call_target="tpu_custom_call" | custom-call | tf_op jit(solution)/shard_map/pallas_call | solution.py:347
  102.1 10.2 %shard_map.312.right_ref = bf16[1024,2048]{1,0:T(8,128)(2,1)} custom-call(bf16[1024,2048]{1,0:T(8,128)(2,1)} %dy_ref.7), custom_call_target="tpu_custom_call" | custom-call | tf_op jit(solution)/shard_map/pallas_call | solution.py:347
  120.3 22.3 %shard_map.307 = (bf16[1024,4096]{1,0:T(8,128)(2,1)}, bf16[1024,4096]{1,0:T(8,128)(2,1)}, f32[512,2048]{1,0:T(8,128)}, f32[1,4096]{1,0:T(1,128)}) custom-call(bf16[256,2048]{1,0:T(8,128)(2,1)} %get-tuple-element.482.normed_ref, bf16[1024,2048]{1,0:T(8,128)(2,1)} %dy_ref.7, bf16[2048,4096]{1,0:T(8,128)(2,1)} %up_ref.7, f32[1,4096]{1,0:T(1,128)} %bitcast.72, ...), custom_call_target="tpu_custom_call" | custom-call | tf_op jit(solution)/shard_map/pallas_call | solution.py:280
  151.0 22.3 %shard_map.309 = (bf16[1024,4096]{1,0:T(8,128)(2,1)}, bf16[1024,4096]{1,0:T(8,128)(2,1)}, f32[512,2048]{1,0:T(8,128)}, f32[1,4096]{1,0:T(1,128)}) custom-call(bf16[256,2048]{1,0:T(8,128)(2,1)} %get-tuple-element.478.normed_ref, bf16[1024,2048]{1,0:T(8,128)(2,1)} %dy_ref.7, ...), custom_call_target="tpu_custom_call", output_to_operand_aliasing={{0}: (5, {}), {1}: (6, {}), {2}: (7, {})} | custom-call | tf_op jit(solution)/shard_map/pallas_call | solution.py:280
  173.4 15.8 %collective-permute-done.10 = f32[256,2048]{1,0:T(8,128)} collective-permute-done((f32[256,2048]{1,0:T(8,128)S(1)}, f32[256,2048]{1,0:T(8,128)}, u32[]{:S(2)}, u32[]{:S(2)}) %collective-permute-start.10) | collective-permute-done | bytes 2097184 | tf_op jit(solution)/shard_map/ppermute | solution.py:17
  194.6 22.5 %shard_map.311 = (bf16[1024,4096]{1,0:T(8,128)(2,1)}, bf16[1024,4096]{1,0:T(8,128)(2,1)}, f32[512,2048]{1,0:T(8,128)}, f32[1,4096]{1,0:T(1,128)}) custom-call(bf16[256,2048]{1,0:T(8,128)(2,1)} %get-tuple-element.474.normed_ref, bf16[1024,2048]{1,0:T(8,128)(2,1)} %dy_ref.7, bf16[2048,4096]{1,0:T(8,128)(2,1)} %up_ref.7, ...), custom_call_target="tpu_custom_call", output_to_operand_aliasing={{0}: (5, {}), {1}: (6, {})} | custom-call | tf_op jit(solution)/shard_map/pallas_call | solution.py:280
  217.1 16.1 %collective-permute-done.9 = f32[256,2048]{1,0:T(8,128)} collective-permute-done((f32[256,2048]{1,0:T(8,128)}, f32[256,2048]{1,0:T(8,128)}, u32[]{:S(2)}, u32[]{:S(2)}) %collective-permute-start.9) | collective-permute-done | bytes 2097184 | tf_op jit(solution)/shard_map/ppermute | solution.py:17
  240.1 22.3 %shard_map.313 = (bf16[1024,4096]{1,0:T(8,128)(2,1)}, bf16[1024,4096]{1,0:T(8,128)(2,1)}, f32[512,2048]{1,0:T(8,128)}, f32[1,4096]{1,0:T(1,128)}) custom-call(bf16[256,2048]{1,0:T(8,128)(2,1)} %get-tuple-element.470.normed_ref, bf16[1024,2048]{1,0:T(8,128)(2,1)} %dy_ref.7, ...), custom_call_target="tpu_custom_call", output_to_operand_aliasing={{0}: (5, {}), {1}: (6, {}), {2}: (7, {})} | custom-call | tf_op jit(solution)/shard_map/pallas_call | solution.py:280
  262.4 9.9 shard_map.318
  272.3 13.5 %while.80 = (s32[]{:T(128)}, f32[2048,1024]{1,0:T(8,128)}, s32[]{:T(128)}, f32[2048,1024]{1,0:T(8,128)}, s32[]{:T(128)}) while((s32[]{:T(128)}, f32[2048,1024]{1,0:T(8,128)}, s32[]{:T(128)}, f32[2048,1024]{1,0:T(8,128)}, s32[]{:T(128)}) %tuple.284), condition=%wide.region_11.12_spmd, body=%wide.region_10.0_spmd.sunk | while | flops 2 | bytes 33554532 | solution.py:362
  272.3 13.5 %collective-permute-done = f32[2048,1024]{1,0:T(8,128)} collective-permute-done((f32[2048,1024]{1,0:T(8,128)}, f32[2048,1024]{1,0:T(8,128)}, u32[]{:S(2)}, u32[]{:S(2)}) %collective-permute-start) | collective-permute-done | bytes 8388640 | tf_op jit(solution)/shard_map/while/body/ppermute | solution.py:17
  285.8 12.0 %shard_map.319 = f32[2048,1024]{1,0:T(8,128)} custom-call(s32[4]{0:T(128)} %get-tuple-element.500.starts_ref, bf16[1024,4096]{1,0:T(8,128)(2,1)} %get-tuple-element.311.left_ref, bf16[1024,2048]{1,0:T(8,128)(2,1)} %shard_map.310.right_ref, f32[2048,1024]{1,0:T(8,128)} %get-tuple-element.300.rest_0_), custom_call_target="tpu_custom_call" | custom-call | tf_op jit(solution)/shard_map/pallas_call | solution.py:89
  300.3 9.9 shard_map.320
  310.2 13.5 %while.81 = (s32[]{:T(128)}, f32[2048,1024]{1,0:T(8,128)}, s32[]{:T(128)}, f32[2048,1024]{1,0:T(8,128)}, s32[]{:T(128)}) while((s32[]{:T(128)}, f32[2048,1024]{1,0:T(8,128)}, s32[]{:T(128)}, f32[2048,1024]{1,0:T(8,128)}, s32[]{:T(128)}) %tuple.287), condition=%wide.region_13.14_spmd, body=%wide.region_12.13_spmd.sunk | while | flops 2 | bytes 33554532 | solution.py:362
  310.2 13.5 %collective-permute-done.1 = f32[2048,1024]{1,0:T(8,128)} collective-permute-done((f32[2048,1024]{1,0:T(8,128)}, f32[2048,1024]{1,0:T(8,128)}, u32[]{:S(2)}, u32[]{:S(2)}) %collective-permute-start.1) | collective-permute-done | bytes 8388640 | tf_op jit(solution)/shard_map/while/body/ppermute | solution.py:17
  323.7 8.1 shard_map.321
  333.4 6.8 convert_element_type.69
  343.1 10.3 %shard_map.314.left_ref = bf16[1024,2048]{1,0:T(8,128)(2,1)} custom-call(bf16[1024,2048]{1,0:T(8,128)(2,1)} %pad_maximum_fusion.1.field_ref), custom_call_target="tpu_custom_call" | custom-call | tf_op jit(solution)/shard_map/pallas_call | solution.py:347
  353.4 11.4 %shard_map.322 = f32[1024,2048]{1,0:T(8,128)} custom-call(s32[4]{0:T(128)} %get-tuple-element.502.starts_ref, bf16[1024,2048]{1,0:T(8,128)(2,1)} %shard_map.314.left_ref, bf16[1024,4096]{1,0:T(8,128)(2,1)} %get-tuple-element.343.right_ref), custom_call_target="tpu_custom_call" | custom-call | tf_op jit(solution)/shard_map/pallas_call | solution.py:89
  364.8 13.5 %while.82 = (s32[]{:T(128)}, f32[1024,2048]{1,0:T(8,128)}, s32[]{:T(128)}, f32[1024,2048]{1,0:T(8,128)}, s32[]{:T(128)}) while((s32[]{:T(128)}, f32[1024,2048]{1,0:T(8,128)}, s32[]{:T(128)}, f32[1024,2048]{1,0:T(8,128)}, s32[]{:T(128)}) %tuple.290), condition=%wide.region_15.16_spmd, body=%wide.region_14.15_spmd.sunk | while | flops 2 | bytes 33554532 | solution.py:362
  364.8 13.5 %collective-permute-done.2 = f32[1024,2048]{1,0:T(8,128)} collective-permute-done((f32[1024,2048]{1,0:T(8,128)}, f32[1024,2048]{1,0:T(8,128)}, u32[]{:S(2)}, u32[]{:S(2)}) %collective-permute-start.2) | collective-permute-done | bytes 8388640 | tf_op jit(solution)/shard_map/while/body/ppermute | solution.py:17
  378.3 7.7 shard_map.323
  390.9 6.4 multiply_reduce_fusion.5
  406.3 18.5 %collective-permute-done.13.rest_1_ = f32[2048,512]{1,0:T(8,128)} collective-permute-done((f32[2048,512]{1,0:T(8,128)}, f32[2048,512]{1,0:T(8,128)}, u32[]{:S(2)}, u32[]{:S(2)}) %collective-permute-start.13) | collective-permute-done | bytes 4194336 | tf_op jit(solution)/shard_map/ppermute | solution.py:17
  424.8 9.4 shard_map.324
  437.5 28.2 %shard_map.325 = f32[1024,2048]{1,0:T(8,128)} custom-call(bf16[1024,4096]{1,0:T(8,128)(2,1)} %get-tuple-element.311.left_ref, bf16[4096,2048]{1,0:T(8,128)(2,1)} %right_ref.1), custom_call_target="tpu_custom_call" | custom-call | tf_op jit(solution)/shard_map/pallas_call | solution.py:117
  465.8 11.4 %shard_map.327 = f32[1024,2048]{1,0:T(8,128)} custom-call(s32[4]{0:T(128)} %get-tuple-element.498.starts_ref, bf16[1024,2048]{1,0:T(8,128)(2,1)} %shard_map.314.left_ref, bf16[1024,4096]{1,0:T(8,128)(2,1)} %get-tuple-element.343.right_ref), custom_call_target="tpu_custom_call" | custom-call | tf_op jit(solution)/shard_map/pallas_call | solution.py:89
  477.2 49.4 %collective-permute-done.14 = f32[512,2048]{1,0:T(8,128)} collective-permute-done((f32[512,2048]{1,0:T(8,128)}, f32[512,2048]{1,0:T(8,128)}, u32[]{:S(2)}, u32[]{:S(2)}) %collective-permute-start.14) | collective-permute-done | bytes 4194336 | tf_op jit(solution)/shard_map/ppermute | solution.py:17
  540.4 13.6 %while.83 = (s32[]{:T(128)}, f32[1024,2048]{1,0:T(8,128)}, s32[]{:T(128)}, f32[1024,2048]{1,0:T(8,128)}, s32[]{:T(128)}) while((s32[]{:T(128)}, f32[1024,2048]{1,0:T(8,128)}, s32[]{:T(128)}, f32[1024,2048]{1,0:T(8,128)}, s32[]{:T(128)}) %tuple.293), condition=%wide.region_21.22_spmd, body=%wide.region_20.21_spmd.sunk | while | flops 2 | bytes 33554532 | solution.py:362
  540.4 13.5 %collective-permute-done.3 = f32[1024,2048]{1,0:T(8,128)} collective-permute-done((f32[1024,2048]{1,0:T(8,128)}, f32[1024,2048]{1,0:T(8,128)}, u32[]{:S(2)}, u32[]{:S(2)}) %collective-permute-start.3) | collective-permute-done | bytes 8388640 | tf_op jit(solution)/shard_map/while/body/ppermute | solution.py:17
  554.0 7.2 shard_map.329
  561.2 8.4 shard_map.330
  577.9 28.0 %shard_map.331 = (bf16[1024,1024]{1,0:T(8,128)(2,1)}, bf16[1024,1024]{1,0:T(8,128)(2,1)}, bf16[1024,1024]{1,0:T(8,128)(2,1)}, f32[8,1,128]{2,1,0:T(1,128)}, f32[8,1,128]{2,1,0:T(1,128)}) custom-call(s32[1]{0:T(128)S(6)} %copy.114.boundary_ref, bf16[1024,1024]{1,0:T(8,128)(2,1)} %add_convert_fusion.2.query_ref, ...), custom_call_target="tpu_custom_call" | custom-call | tf_op jit(solution)/shard_map/pallas_call | solution.py:237
  605.9 8.9 shard_map.333
  614.9 15.6 %shard_map.332 = f32[768,2048]{1,0:T(8,128)} custom-call(bf16[1024,1024]{1,0:T(8,128)(2,1)} %get-tuple-element.350.refs_0_.right_ref, bf16[1024,1024]{1,0:T(8,128)(2,1)} %get-tuple-element.354.refs_1_.right_ref, bf16[1024,1024]{1,0:T(8,128)(2,1)} %get-tuple-element.358.refs_2_.right_ref, bf16[2048,1024]{1,0:T(8,128)(2,1)} %refs_3_.3, ...), custom_call_target="tpu_custom_call" | custom-call | tf_op jit(solution)/shard_map/pallas_call | solution.py:141
  634.8 10.4 %shard_map.340.right_ref = bf16[1024,2048]{1,0:T(8,128)(2,1)} custom-call(bf16[1024,2048]{1,0:T(8,128)(2,1)} %pad_maximum_fusion.4.field_ref), custom_call_target="tpu_custom_call" | custom-call | tf_op jit(solution)/shard_map/pallas_call | solution.py:347
  645.2 6.5 shard_map.334
  651.7 6.5 shard_map.341
  658.2 6.5 shard_map.338
  664.7 7.5 while.84
  664.7 7.5 collective-permute-done.4
  672.2 6.5 shard_map.336
  678.7 7.5 while.85
  678.9 7.4 collective-permute-done.5
  686.2 7.8 while.86
  686.6 7.4 collective-permute-done.6
  694.0 7.5 while.87
  694.1 7.4 collective-permute-done.7
  711.6 8.4 shard_map.343
  730.0 40.2 %collective-permute-done.19.rest_1_ = f32[1024,512]{1,0:T(8,128)} collective-permute-done((f32[1024,512]{1,0:T(8,128)S(1)}, f32[1024,512]{1,0:T(8,128)}, u32[]{:S(2)}, u32[]{:S(2)}) %collective-permute-start.19) | collective-permute-done | bytes 2097184 | tf_op jit(solution)/shard_map/ppermute | solution.py:17
  783.4 31.7 %collective-permute-done.20.rest_1_ = f32[512,1024]{1,0:T(8,128)} collective-permute-done((f32[512,1024]{1,0:T(8,128)}, f32[512,1024]{1,0:T(8,128)}, u32[]{:S(2)}, u32[]{:S(2)}) %collective-permute-start.20) | collective-permute-done | bytes 2097184 | tf_op jit(solution)/shard_map/ppermute | solution.py:17
  815.1 6.5 shard_map.347
  827.5 29.5 %collective-permute-done.18 = f32[768,2048]{1,0:T(8,128)} collective-permute-done((f32[768,2048]{1,0:T(8,128)}, f32[768,2048]{1,0:T(8,128)}, u32[]{:S(2)}, u32[]{:S(2)}) %collective-permute-start.18) | collective-permute-done | bytes 6291488 | tf_op jit(solution)/shard_map/ppermute | solution.py:17
  857.0 7.9 multiply_reduce_fusion.1
  873.3 6.5 shard_map.349
  887.8 8.7 fusion.4
  897.0 30.2 %collective-permute-done.21 = f32[256,2048]{1,0:T(8,128)} collective-permute-done((f32[256,2048]{1,0:T(8,128)}, f32[256,2048]{1,0:T(8,128)}, u32[]{:S(2)}, u32[]{:S(2)}) %collective-permute-start.21) | collective-permute-done | bytes 2097184 | tf_op jit(solution)/shard_map/ppermute | solution.py:17
  935.8 7.9 collective-permute-done.24
  943.7 6.8 shard_map.350
  967.9 14.8 %collective-permute-done.28 = f32[2048,128]{1,0:T(8,128)} collective-permute-done((f32[2048,128]{1,0:T(8,128)S(1)}, f32[2048,128]{1,0:T(8,128)}, u32[]{:S(2)}, u32[]{:S(2)}) %collective-permute-start.28) | collective-permute-done | bytes 1048608 | tf_op jit(solution)/shard_map/ppermute | solution.py:17
  989.8 25.9 %reduce-scatter.13.cloned.1.call-done = f32[128,1024]{1,0:T(8,128)} async-done(((f32[512,1024]{1,0:T(8,128)}), f32[128,1024]{1,0:T(8,128)}) %reduce-scatter.13.cloned.1.call-update) | async-done | bytes 524304 | tf_op jit(solution)/shard_map/reduce_scatter | solution.py:398
  (307 shorter events, 217.8 us)
Async XLA Ops:
  7.2 951.2 %reduce-scatter.21.cloned.1.call-start = ((), (), s32[]{:S(2)}) async-start(), calls=%async_computation.14 | async-start | bytes 10485760 | tf_op jit(solution)/shard_map/reduce_scatter | solution.py:403
  16.9 11.4 %copy-start.13 = (bf16[1024,2048]{1,0:T(8,128)(2,1)}, bf16[1024,2048]{1,0:T(8,128)(2,1)S(1)}, u32[]{:S(2)}) copy-start(bf16[1024,2048]{1,0:T(8,128)(2,1)S(1)} %get-tuple-element.487.field_ref) | copy-start | bytes 12582916
  44.4 8.1 copy-start.30
  44.4 8.1 copy-start.51
  49.5 64.1 %collective-permute-start.8 = (f32[256,2048]{1,0:T(8,128)}, f32[256,2048]{1,0:T(8,128)}, u32[]{:S(2)}, u32[]{:S(2)}) collective-permute-start(f32[256,2048]{1,0:T(8,128)} %fusion.15), channel_id=1, source_target_pairs={{0,1},{1,0},{2,3},{3,2},{4,5},{5,4},{6,7},{7,6},{8,9},{9,8},{10,11... | collective-permute-start | bytes 6291464 | tf_op jit(solution)/shard_map/ppermute | solution.py:17
  55.1 89.1 %collective-permute-start.11 = (f32[256,2048]{1,0:T(8,128)}, f32[256,2048]{1,0:T(8,128)}, u32[]{:S(2)}, u32[]{:S(2)}) collective-permute-start(f32[256,2048]{1,0:T(8,128)} %fusion.9), channel_id=1, source_target_pairs={{0,1},{1,0},{2,3},{3,2},{4,5},{5,4},{6,7},{7,6},{8,9},{9,8},{10,11... | collective-permute-start | bytes 6291464 | tf_op jit(solution)/shard_map/ppermute | solution.py:17
  72.2 116.9 %collective-permute-start.10 = (f32[256,2048]{1,0:T(8,128)S(1)}, f32[256,2048]{1,0:T(8,128)}, u32[]{:S(2)}, u32[]{:S(2)}) collective-permute-start(f32[256,2048]{1,0:T(8,128)S(1)} %fusion.11), channel_id=1, source_target_pairs={{0,1},{1,0},{2,3},{3,2},{4,5},{5,4},{6,7},{7,6},{8,9},{9,8},{10,11... | collective-permute-start | bytes 6291464 | tf_op jit(solution)/shard_map/ppermute | solution.py:17
  76.9 156.3 %collective-permute-start.9 = (f32[256,2048]{1,0:T(8,128)}, f32[256,2048]{1,0:T(8,128)}, u32[]{:S(2)}, u32[]{:S(2)}) collective-permute-start(f32[256,2048]{1,0:T(8,128)} %fusion.13), channel_id=1, source_target_pairs={{0,1},{1,0},{2,3},{3,2},{4,5},{5,4},{6,7},{7,6},{8,9},{9,8},{10,11... | collective-permute-start | bytes 6291464 | tf_op jit(solution)/shard_map/ppermute | solution.py:17
  272.3 13.5 %collective-permute-start = (f32[2048,1024]{1,0:T(8,128)}, f32[2048,1024]{1,0:T(8,128)}, u32[]{:S(2)}, u32[]{:S(2)}) collective-permute-start(f32[2048,1024]{1,0:T(8,128)} %get-tuple-element.684), channel_id=1, source_target_pairs={{0,2},{2,0},{1,3},{3,1},{4,6},{6,4},{5,7},{7,5},{8,10},{10,8},{9,1... | collective-permute-start | bytes 25165832 | tf_op jit(solution)/shard_map/while/body/ppermute | solution.py:17
  297.8 686.2 %reduce-scatter.23.cloned.1.call-start = ((), (), s32[]{:S(2)}) async-start(), calls=%async_computation.15 | async-start | bytes 5242880 | tf_op jit(solution)/shard_map/reduce_scatter | solution.py:398
  297.9 93.0 %collective-permute-start.12 = (f32[512,2048]{1,0:T(8,128)}, f32[512,2048]{1,0:T(8,128)}, u32[]{:S(2)}, u32[]{:S(2)}) collective-permute-start(f32[512,2048]{1,0:T(8,128)} %get-tuple-element.296), channel_id=1, source_target_pairs={{0,1},{1,0},{2,3},{3,2},{4,5},{5,4},{6,7},{7,6},{8,9},{9,8},{10,11... | collective-permute-start | bytes 12582920 | tf_op jit(solution)/shard_map/ppermute | solution.py:17
  310.2 13.5 %collective-permute-start.1 = (f32[2048,1024]{1,0:T(8,128)}, f32[2048,1024]{1,0:T(8,128)}, u32[]{:S(2)}, u32[]{:S(2)}) collective-permute-start(f32[2048,1024]{1,0:T(8,128)} %get-tuple-element.688), channel_id=1, source_target_pairs={{0,2},{2,0},{1,3},{3,1},{4,6},{6,4},{5,7},{7,5},{8,10},{10,8},{9,1... | collective-permute-start | bytes 25165832 | tf_op jit(solution)/shard_map/while/body/ppermute | solution.py:17
  331.8 93.0 %collective-permute-start.13 = (f32[2048,512]{1,0:T(8,128)}, f32[2048,512]{1,0:T(8,128)}, u32[]{:S(2)}, u32[]{:S(2)}) collective-permute-start(f32[2048,512]{1,0:T(8,128)} %shard_map.321), channel_id=1, source_target_pairs={{0,4},{4,0},{1,5},{5,1},{2,6},{6,2},{3,7},{7,3},{8,12},{12,8},{9,1... | collective-permute-start | bytes 12582920 | tf_op jit(solution)/shard_map/ppermute | solution.py:17
  333.4 7.4 copy-start.19
  333.4 7.4 copy-start.20
  333.4 7.4 copy-start.21
  333.4 7.4 copy-start.22
  364.8 13.5 %collective-permute-start.2 = (f32[1024,2048]{1,0:T(8,128)}, f32[1024,2048]{1,0:T(8,128)}, u32[]{:S(2)}, u32[]{:S(2)}) collective-permute-start(f32[1024,2048]{1,0:T(8,128)} %get-tuple-element.692), channel_id=1, source_target_pairs={{0,2},{2,0},{1,3},{3,1},{4,6},{6,4},{5,7},{7,5},{8,10},{10,8},{9,1... | collective-permute-start | bytes 25165832 | tf_op jit(solution)/shard_map/while/body/ppermute | solution.py:17
  390.9 6.4 copy-start.10
  390.9 6.4 copy-start.12
  434.3 552.4 %reduce-scatter.17.cloned.1.call-start = ((), (), s32[]{:S(2)}) async-start(), calls=%async_computation.12 | async-start | bytes 5242880 | tf_op jit(solution)/shard_map/reduce_scatter | solution.py:398
  434.3 92.2 %collective-permute-start.14 = (f32[512,2048]{1,0:T(8,128)}, f32[512,2048]{1,0:T(8,128)}, u32[]{:S(2)}, u32[]{:S(2)}) collective-permute-start(f32[512,2048]{1,0:T(8,128)} %get-tuple-element.312), channel_id=1, source_target_pairs={{0,1},{1,0},{2,3},{3,2},{4,5},{5,4},{6,7},{7,6},{8,9},{9,8},{10,11... | collective-permute-start | bytes 12582920 | tf_op jit(solution)/shard_map/ppermute | solution.py:17
  434.6 126.7 %collective-permute-start.16 = (f32[512,2048]{1,0:T(8,128)}, f32[512,2048]{1,0:T(8,128)}, u32[]{:S(2)}, u32[]{:S(2)}) collective-permute-start(f32[512,2048]{1,0:T(8,128)} %shard_map.323), channel_id=1, source_target_pairs={{0,4},{4,0},{1,5},{5,1},{2,6},{6,2},{3,7},{7,3},{8,12},{12,8},{9,1... | collective-permute-start | bytes 12582920 | tf_op jit(solution)/shard_map/ppermute | solution.py:17
  526.5 181.2 %collective-permute-start.15 = (f32[1024,2048]{1,0:T(8,128)}, f32[1024,2048]{1,0:T(8,128)}, u32[]{:S(2)}, u32[]{:S(2)}) collective-permute-start(f32[1024,2048]{1,0:T(8,128)} %shard_map.325), channel_id=1, source_target_pairs={{0,1},{1,0},{2,3},{3,2},{4,5},{5,4},{6,7},{7,6},{8,9},{9,8},{10,11... | collective-permute-start | bytes 25165832 | tf_op jit(solution)/shard_map/ppermute | solution.py:17
  540.4 13.5 %collective-permute-start.3 = (f32[1024,2048]{1,0:T(8,128)}, f32[1024,2048]{1,0:T(8,128)}, u32[]{:S(2)}, u32[]{:S(2)}) collective-permute-start(f32[1024,2048]{1,0:T(8,128)} %get-tuple-element.696), channel_id=1, source_target_pairs={{0,2},{2,0},{1,3},{3,1},{4,6},{6,4},{5,7},{7,5},{8,10},{10,8},{9,1... | collective-permute-start | bytes 25165832 | tf_op jit(solution)/shard_map/while/body/ppermute | solution.py:17
  569.6 417.1 %reduce-scatter.19.cloned.1.call-start = ((), (), s32[]{:S(2)}) async-start(), calls=%async_computation.13 | async-start | bytes 5242880 | tf_op jit(solution)/shard_map/reduce_scatter | solution.py:398
  569.7 141.9 %collective-permute-start.17 = (f32[512,2048]{1,0:T(8,128)}, f32[512,2048]{1,0:T(8,128)}, u32[]{:S(2)}, u32[]{:S(2)}) collective-permute-start(f32[512,2048]{1,0:T(8,128)} %shard_map.329), channel_id=1, source_target_pairs={{0,4},{4,0},{1,5},{5,1},{2,6},{6,2},{3,7},{7,3},{8,12},{12,8},{9,1... | collective-permute-start | bytes 12582920 | tf_op jit(solution)/shard_map/ppermute | solution.py:17
  574.1 31.8 %copy-start.9 = (bf16[1024,1024]{1,0:T(8,128)(2,1)}, bf16[1024,1024]{1,0:T(8,128)(2,1)S(1)}, u32[]{:S(2)}) copy-start(bf16[1024,1024]{1,0:T(8,128)(2,1)S(1)} %constant_dynamic-update-slice_fusion.left_ref) | copy-start | bytes 6291460
  614.9 15.7 %copy-start.25 = (bf16[512,2048]{1,0:T(8,128)(2,1)S(1)}, bf16[512,2048]{1,0:T(8,128)(2,1)}, u32[]{:S(2)}) copy-start(bf16[512,2048]{1,0:T(8,128)(2,1)} %copy-done.24) | copy-start | bytes 6291460
  664.7 7.5 collective-permute-start.4
  678.7 7.5 collective-permute-start.5
  686.4 7.6 collective-permute-start.6
  694.0 7.5 collective-permute-start.7
  701.5 6.2 copy-start.7
  701.5 6.2 copy-start.42
  720.0 269.8 %reduce-scatter.15.cloned.1.call-start = ((), (), s32[]{:S(2)}) async-start(), calls=%async_computation.11 | async-start | bytes 2621440 | tf_op jit(solution)/shard_map/reduce_scatter | solution.py:398
  720.1 136.9 %collective-permute-start.18 = (f32[768,2048]{1,0:T(8,128)}, f32[768,2048]{1,0:T(8,128)}, u32[]{:S(2)}, u32[]{:S(2)}) collective-permute-start(f32[768,2048]{1,0:T(8,128)} %shard_map.332), channel_id=1, source_target_pairs={{0,1},{1,0},{2,3},{3,2},{4,5},{5,4},{6,7},{7,6},{8,9},{9,8},{10,11... | collective-permute-start | bytes 18874376 | tf_op jit(solution)/shard_map/ppermute | solution.py:17
  721.6 48.6 %collective-permute-start.19 = (f32[1024,512]{1,0:T(8,128)S(1)}, f32[1024,512]{1,0:T(8,128)}, u32[]{:S(2)}, u32[]{:S(2)}) collective-permute-start(f32[1024,512]{1,0:T(8,128)S(1)} %copy-done.27), channel_id=1, source_target_pairs={{0,4},{4,0},{1,5},{5,1},{2,6},{6,2},{3,7},{7,3},{8,12},{12,8},{9,1... | collective-permute-start | bytes 6291464 | tf_op jit(solution)/shard_map/ppermute | solution.py:17
  729.0 86.1 %collective-permute-start.20 = (f32[512,1024]{1,0:T(8,128)}, f32[512,1024]{1,0:T(8,128)}, u32[]{:S(2)}, u32[]{:S(2)}) collective-permute-start(f32[512,1024]{1,0:T(8,128)} %shard_map.344), channel_id=1, source_target_pairs={{0,4},{4,0},{1,5},{5,1},{2,6},{6,2},{3,7},{7,3},{8,12},{12,8},{9,1... | collective-permute-start | bytes 6291464 | tf_op jit(solution)/shard_map/ppermute | solution.py:17
  776.0 213.8 %reduce-scatter.11.cloned.1.call-start = ((), (), s32[]{:S(2)}) async-start(), calls=%async_computation.9 | async-start | bytes 2621440 | tf_op jit(solution)/shard_map/reduce_scatter | solution.py:398
  781.9 90.1 %collective-permute-start.22 = (f32[512,1024]{1,0:T(8,128)}, f32[512,1024]{1,0:T(8,128)S(1)}, u32[]{:S(2)}, u32[]{:S(2)}) collective-permute-start(f32[512,1024]{1,0:T(8,128)} %shard_map.346), channel_id=1, source_target_pairs={{0,4},{4,0},{1,5},{5,1},{2,6},{6,2},{3,7},{7,3},{8,12},{12,8},{9,1... | collective-permute-start | bytes 6291464 | tf_op jit(solution)/shard_map/ppermute | solution.py:17
  821.6 35.4 %copy-start.35 = (f32[2048]{0:T(1024)S(1)}, f32[2048]{0:T(1024)}, u32[]{:S(2)}) copy-start(f32[2048]{0:T(1024)} %param.36) | copy-start | bytes 24580
  857.0 7.9 slice-start
  857.0 8.9 slice-start.1
  857.0 10.1 copy-start.8
  857.0 11.3 %copy-start.17 = (f32[512,2048]{1,0:T(8,128)S(1)}, f32[512,2048]{1,0:T(8,128)}, u32[]{:S(2)}) copy-start(f32[512,2048]{1,0:T(8,128)} %get-tuple-element.465) | copy-start | bytes 12582916
  857.0 11.3 %copy-start.39 = (f32[1024]{0:T(1024)S(1)}, f32[1024]{0:T(1024)}, u32[]{:S(2)}) copy-start(f32[1024]{0:T(1024)} %copy-done.38) | copy-start | bytes 12292
  879.9 7.0 copy-start.49
  879.9 7.9 copy-start.41
  879.9 7.9 copy-start.40
  879.9 7.9 copy-start.43
  879.9 7.9 copy-start.3
  879.9 109.9 %reduce-scatter.9.cloned.1.call-start = ((), (), s32[]{:S(2)}) async-start(), calls=%async_computation.8 | async-start | bytes 2621440 | tf_op jit(solution)/shard_map/reduce_scatter | solution.py:398
  880.0 47.2 %collective-permute-start.21 = (f32[256,2048]{1,0:T(8,128)}, f32[256,2048]{1,0:T(8,128)}, u32[]{:S(2)}, u32[]{:S(2)}) collective-permute-start(f32[256,2048]{1,0:T(8,128)} %shard_map.333), channel_id=1, source_target_pairs={{0,1},{1,0},{2,3},{3,2},{4,5},{5,4},{6,7},{7,6},{8,9},{9,8},{10,11... | collective-permute-start | bytes 6291464 | tf_op jit(solution)/shard_map/ppermute | solution.py:17
  881.8 134.0 %reduce-scatter.13.cloned.1.call-start = ((), (), s32[]{:S(2)}) async-start(), calls=%async_computation.10 | async-start | bytes 2621440 | tf_op jit(solution)/shard_map/reduce_scatter | solution.py:398
  887.8 39.4 %copy-start.23 = (f32[256,2048]{1,0:T(8,128)S(1)}, f32[256,2048]{1,0:T(8,128)}, u32[]{:S(2)}) copy-start(f32[256,2048]{1,0:T(8,128)} %shard_map.333) | copy-start | bytes 6291460
  896.5 47.2 %collective-permute-start.27 = (f32[512,1024]{1,0:T(8,128)}, f32[512,1024]{1,0:T(8,128)}, u32[]{:S(2)}, u32[]{:S(2)}) collective-permute-start(f32[512,1024]{1,0:T(8,128)} %shard_map.348), channel_id=1, source_target_pairs={{0,4},{4,0},{1,5},{5,1},{2,6},{6,2},{3,7},{7,3},{8,12},{12,8},{9,1... | collective-permute-start | bytes 6291464 | tf_op jit(solution)/shard_map/ppermute | solution.py:17
  930.5 1.3 collective-permute-start.23
  931.9 11.8 %collective-permute-start.24 = (f32[4,1152]{1,0:T(4,128)S(1)}, f32[4,1152]{1,0:T(4,128)S(1)}, u32[]{:S(2)}, u32[]{:S(2)}) collective-permute-start(f32[4,1152]{1,0:T(4,128)S(1)} %bitcast.84), channel_id=1, source_target_pairs={{0,4},{4,0},{1,5},{5,1},{2,6},{6,2},{3,7},{7,3},{8,12},{12,8},{9,1... | collective-permute-start | bytes 55304 | tf_op jit(solution)/shard_map/ppermute | solution.py:17
  943.7 9.4 copy-start.18
  950.5 6.3 collective-permute-start.25
  956.8 8.3 collective-permute-start.26
  959.7 23.0 %copy-start.28 = (f32[2048,256]{1,0:T(8,128)S(1)}, f32[2048,256]{1,0:T(8,128)}, u32[]{:S(2)}) copy-start(f32[2048,256]{1,0:T(8,128)} %reduce-scatter.21.cloned.1.call-done) | copy-start | bytes 6291460
  959.7 23.0 %collective-permute-start.28 = (f32[2048,128]{1,0:T(8,128)S(1)}, f32[2048,128]{1,0:T(8,128)}, u32[]{:S(2)}, u32[]{:S(2)}) collective-permute-start(f32[2048,128]{1,0:T(8,128)S(1)} %constant_dynamic-slice_fusion), channel_id=1, source_target_pairs={{0,4},{4,0},{1,5},{5,1},{2,6},{6,2},{3,7},{7,3},{8,12},{12,8},{9,1... | collective-permute-start | bytes 3145736 | tf_op jit(solution)/shard_map/ppermute | solution.py:17
  (32 other events, 131.6 us)
Sparse Core Ops, SparseCore 0:
  298.0 146.0 reduce-scatter.20
  446.4 77.4 reduce-scatter.22
  569.7 78.2 reduce-scatter.16
  720.1 76.9 reduce-scatter.18
  799.8 44.1 reduce-scatter.14
  880.0 43.9 reduce-scatter.10
  926.9 43.1 reduce-scatter.8
  972.9 42.8 reduce-scatter.12
